TPU v7x, 32 devices: a whole 2x2x4 slice. The times are simulated.
32 devices in a mesh: fsdp: 8 (over z, core), seq: 4 (over y, x).
Axes of the slice: x: 2, y: 2, z: 4, core: 2. Of those that a mesh axis runs over, the one named last changes fastest.
Arguments:
- tokens: bfloat16 [16, 1024, 1024], P('fsdp', 'seq'), may hold values from -6 to 6
- segment_ids: int32 [16, 1024], P('fsdp', 'seq'), may hold values from 0 to 3, never falling along the last dimension, each value on 1 to 512 neighbouring positions
- w_qkv: bfloat16 [1024, 3072], P('fsdp'), may hold values from -0.1875 to 0.1875
- w_out: bfloat16 [1024, 1024], P(None, 'fsdp'), may hold values from -1.5 to 1.5
- w_in: bfloat16 [1024, 5248], P('fsdp'), may hold values from -0.1875 to 0.1875
- w_down: bfloat16 [2624, 1024], P(None, 'fsdp'), may hold values from -0.125 to 0.125
- gain_attn: bfloat16 [1024], P('fsdp'), may hold values from 0.5 to 1.5
- gain_mlp: bfloat16 [1024], P('fsdp'), may hold values from 0.5 to 1.5
- grad_output: bfloat16 [16, 1024, 1024], P('fsdp', 'seq'), may hold values from -6 to 6
Outputs:
- output: bfloat16 [16, 1024, 1024], P('fsdp', 'seq')
- grad_tokens: bfloat16 [16, 1024, 1024], P('fsdp', 'seq')
- grad_w_qkv: float32 [1024, 3072], P('fsdp')
- grad_w_out: float32 [1024, 1024], P(None, 'fsdp')
- grad_w_in: float32 [1024, 5248], P('fsdp')
- grad_w_down: float32 [2624, 1024], P(None, 'fsdp')
- grad_gain_attn: float32 [1024], P('fsdp')
- grad_gain_mlp: float32 [1024], P('fsdp')
Inputs may be any that keep to these rules, and one draw needn't show every extreme that they name: `segment_ids`: in each sequence the ids never fall; a document is a run of equal ids of 1 to 512 tokens, one of exactly 512.
All inputs are finite; a program needn't handle non-finite values.
Results may differ from a plain program's by a relative error of at most 0.02.
Values may be sent and summed in bfloat16 or wider, within the bound.
No kernel may reach another device: no remote copies, remote signals or barrier semaphores. Data moves between devices by JAX's collectives and lax.ppermute only.
A program may use at most 192 MiB of HBM per device.

v0:
```python
import math

import jax
import jax.numpy as jnp
from jax import lax
from jax.sharding import PartitionSpec as P

D = 1024
HEADS = 16
HD = 64
FF = 2624
SEQ_MB = 1
MICRO = 2


def normalize(rows_in, gain):
    center_of = jnp.mean(rows_in, axis=-1, keepdims=True)
    centered = rows_in - center_of
    spread = jnp.mean(centered * centered, axis=-1, keepdims=True)
    return centered * lax.rsqrt(spread + 1e-05) * gain


def doc_positions(seg_rows):
    places = jnp.arange(seg_rows.shape[1], dtype=jnp.int32)[None, :]
    before = jnp.concatenate([seg_rows[:, :1] - 1, seg_rows[:, :-1]], axis=1)
    begins = jnp.where(seg_rows != before, places, 0)
    return places - lax.cummax(begins, axis=1)


def rope_tables(positions, head_dim):
    half_dim = head_dim // 2
    inverse = jnp.exp(
        jnp.arange(half_dim, dtype=jnp.float32) * (-2.0 * math.log(160000.0) / head_dim)
    )
    angles = positions.astype(jnp.float32)[..., None] * inverse
    return (jnp.cos(angles), jnp.sin(angles))


def rotate(vector, cosine, sine):
    half_dim = vector.shape[-1] // 2
    first, second = (vector[..., :half_dim], vector[..., half_dim:])
    return jnp.concatenate(
        [first * cosine - second * sine, second * cosine + first * sine], axis=-1
    )


def gelu_mix(gate_part, up_part):
    return jax.nn.gelu(gate_part, approximate=False) * up_part


def contract_rows(left, right):
    return lax.dot_general(
        left, right, (((0,), (0,)), ((), ())), preferred_element_type=jnp.float32
    )


def contract_cols(left, right):
    return lax.dot_general(
        left, right, (((1,), (1,)), ((), ())), preferred_element_type=jnp.float32
    )


def fetch(w_qkv, w_out, w_in, w_down, gain_attn, gain_mlp):
    return (
        lax.all_gather(w_qkv, "fsdp", axis=0, tiled=True),
        lax.all_gather(w_out, "fsdp", axis=1, tiled=True),
        lax.all_gather(w_in, "fsdp", axis=0, tiled=True),
        lax.all_gather(w_down, "fsdp", axis=1, tiled=True),
        lax.all_gather(gain_attn, "fsdp", axis=0, tiled=True),
        lax.all_gather(gain_mlp, "fsdp", axis=0, tiled=True),
    )


def attend_forward(queries, key_rows, values, seg_rows, block_rows):
    row_count, length, head_count, head_dim = queries.shape
    scaling = 1.0 / math.sqrt(head_dim)

    def advance(number, carried):
        out_buffer, sums_buffer = carried
        offset = number * block_rows
        query_block = lax.dynamic_slice_in_dim(queries, offset, block_rows, 1)
        seg_block = lax.dynamic_slice_in_dim(seg_rows, offset, block_rows, 1)
        scores = (
            jnp.einsum("rqhd,rkhd->rhqk", query_block, key_rows, preferred_element_type=jnp.float32)
            * scaling
        )
        allowed = seg_block[:, None, :, None] == seg_rows[:, None, None, :]
        scores = jnp.where(allowed, scores, -1e30)
        highest = jnp.max(scores, axis=-1, keepdims=True)
        raised = jnp.exp(scores - highest)
        totals = jnp.sum(raised, axis=-1, keepdims=True)
        shares = (raised / totals).astype(jnp.bfloat16)
        out_block = jnp.einsum(
            "rhqk,rkhd->rqhd", shares, values, preferred_element_type=jnp.float32
        )
        log_block = (highest + jnp.log(totals))[..., 0]
        out_buffer = lax.dynamic_update_slice_in_dim(
            out_buffer, out_block.astype(jnp.bfloat16), offset, 1
        )
        sums_buffer = lax.dynamic_update_slice_in_dim(sums_buffer, log_block, offset, 2)
        return (out_buffer, sums_buffer)

    initial = (
        jnp.zeros(queries.shape, jnp.bfloat16),
        jnp.zeros((row_count, head_count, length), jnp.float32),
    )
    return lax.fori_loop(0, length // block_rows, advance, initial)


def attend_backward(queries, key_rows, values, seg_rows, log_sums, grad_context, block_rows):
    row_count, length, head_count, head_dim = queries.shape
    scaling = 1.0 / math.sqrt(head_dim)

    def advance(number, carried):
        grad_query, grad_key, grad_value = carried
        offset = number * block_rows
        query_block = lax.dynamic_slice_in_dim(queries, offset, block_rows, 1)
        seg_block = lax.dynamic_slice_in_dim(seg_rows, offset, block_rows, 1)
        grad_block = lax.dynamic_slice_in_dim(grad_context, offset, block_rows, 1)
        sums_block = lax.dynamic_slice_in_dim(log_sums, offset, block_rows, 2)
        scores = (
            jnp.einsum("rqhd,rkhd->rhqk", query_block, key_rows, preferred_element_type=jnp.float32)
            * scaling
        )
        allowed = seg_block[:, None, :, None] == seg_rows[:, None, None, :]
        shares = jnp.where(allowed, jnp.exp(scores - sums_block[..., None]), 0.0)
        grad_value = grad_value + jnp.einsum(
            "rhqk,rqhd->rkhd",
            shares.astype(jnp.bfloat16),
            grad_block,
            preferred_element_type=jnp.float32,
        )
        grad_shares = jnp.einsum(
            "rqhd,rkhd->rhqk", grad_block, values, preferred_element_type=jnp.float32
        )
        grad_scores = shares * (grad_shares - jnp.sum(shares * grad_shares, axis=-1, keepdims=True))
        rounded = grad_scores.astype(jnp.bfloat16)
        query_piece = (
            jnp.einsum("rhqk,rkhd->rqhd", rounded, key_rows, preferred_element_type=jnp.float32)
            * scaling
        )
        grad_key = (
            grad_key
            + jnp.einsum(
                "rhqk,rqhd->rkhd", rounded, query_block, preferred_element_type=jnp.float32
            )
            * scaling
        )
        grad_query = lax.dynamic_update_slice_in_dim(
            grad_query, query_piece.astype(jnp.bfloat16), offset, 1
        )
        return (grad_query, grad_key, grad_value)

    initial = (
        jnp.zeros(queries.shape, jnp.bfloat16),
        jnp.zeros(queries.shape, jnp.float32),
        jnp.zeros(queries.shape, jnp.float32),
    )
    grad_query, grad_key, grad_value = lax.fori_loop(0, length // block_rows, advance, initial)
    return (grad_query, grad_key.astype(jnp.bfloat16), grad_value.astype(jnp.bfloat16))


def zero_totals():
    return (
        jnp.zeros((D, 3 * HEADS * HD), jnp.float32),
        jnp.zeros((HEADS * HD, D), jnp.float32),
        jnp.zeros((D, 2 * FF), jnp.float32),
        jnp.zeros((FF, D), jnp.float32),
        jnp.zeros((D,), jnp.float32),
        jnp.zeros((D,), jnp.float32),
    )


def local(tokens, segment_ids, w_qkv, w_out, w_in, w_down, gain_attn, gain_mlp, grad_output):
    seq_devices = lax.axis_size("seq")
    piece_len = tokens.shape[1]
    local_heads = HEADS // seq_devices
    all_ids = lax.all_gather(segment_ids, "seq", axis=1, tiled=True)
    length = all_ids.shape[1]
    block_rows = min(512, length)
    all_positions = doc_positions(all_ids)
    own_positions = lax.dynamic_slice_in_dim(
        all_positions, lax.axis_index("seq") * piece_len, piece_len, 1
    )
    acc_qkv, acc_out, acc_in, acc_down, acc_gain_attn, acc_gain_mlp = zero_totals()
    outputs = []
    input_grads = []
    per_micro = SEQ_MB
    for micro_index in range(MICRO):
        lower = micro_index * per_micro
        upper = lower + per_micro
        gathered = fetch(w_qkv, w_out, w_in, w_down, gain_attn, gain_mlp)
        full_qkv, full_out, full_in, full_down, full_gain_attn, full_gain_mlp = gathered
        gain_one = full_gain_attn.astype(jnp.float32)
        gain_two = full_gain_mlp.astype(jnp.float32)
        rows_in = tokens[lower:upper].astype(jnp.float32).reshape(-1, D)
        low_one = normalize(rows_in, gain_one).astype(jnp.bfloat16)
        mixed = jnp.dot(low_one, full_qkv, preferred_element_type=jnp.float32).reshape(
            per_micro, piece_len, HEADS, 3, HD
        )
        cosine, sine = rope_tables(own_positions[lower:upper], HD)
        cosine = cosine[:, :, None, :]
        sine = sine[:, :, None, :]
        stacked = jnp.stack(
            [
                rotate(mixed[:, :, :, 0], cosine, sine),
                rotate(mixed[:, :, :, 1], cosine, sine),
                mixed[:, :, :, 2],
            ],
            axis=3,
        )
        stacked = stacked.astype(jnp.bfloat16).reshape(per_micro, piece_len, HEADS * 3 * HD)
        head_side = lax.all_to_all(stacked, "seq", split_axis=2, concat_axis=1, tiled=True).reshape(
            per_micro, length, local_heads, 3, HD
        )
        queries = head_side[:, :, :, 0]
        key_rows = head_side[:, :, :, 1]
        values = head_side[:, :, :, 2]
        ids_micro = all_ids[lower:upper]
        attended, log_sums = attend_forward(queries, key_rows, values, ids_micro, block_rows)
        token_side = lax.all_to_all(
            attended.reshape(per_micro, length, local_heads * HD),
            "seq",
            split_axis=1,
            concat_axis=2,
            tiled=True,
        )
        context = token_side.reshape(-1, HEADS * HD)
        hidden = rows_in + jnp.dot(context, full_out, preferred_element_type=jnp.float32)
        low_two = normalize(hidden, gain_two).astype(jnp.bfloat16)
        gate_up = jnp.dot(low_two, full_in, preferred_element_type=jnp.float32)
        gate_part = gate_up[:, :FF]
        up_part = gate_up[:, FF:]
        product = gelu_mix(gate_part, up_part).astype(jnp.bfloat16)
        result = hidden + jnp.dot(product, full_down, preferred_element_type=jnp.float32)
        outputs.append(result.astype(jnp.bfloat16).reshape(per_micro, piece_len, D))
        grad_rows = grad_output[lower:upper].reshape(-1, D)
        acc_down = acc_down + contract_rows(product, grad_rows)
        grad_product = contract_cols(grad_rows, full_down)
        unused_mix, pull_mix = jax.vjp(gelu_mix, gate_part, up_part)
        grad_gate, grad_up = pull_mix(grad_product)
        grad_gate_up = jnp.concatenate([grad_gate, grad_up], axis=1).astype(jnp.bfloat16)
        acc_in = acc_in + contract_rows(low_two, grad_gate_up)
        grad_normed_two = contract_cols(grad_gate_up, full_in)
        unused_two, pull_two = jax.vjp(normalize, hidden, gain_two)
        grad_hidden_part, grad_gain_two = pull_two(grad_normed_two)
        acc_gain_mlp = acc_gain_mlp + grad_gain_two
        grad_hidden = grad_rows.astype(jnp.float32) + grad_hidden_part
        grad_branch = grad_hidden.astype(jnp.bfloat16)
        acc_out = acc_out + contract_rows(context, grad_branch)
        grad_context = (
            contract_cols(grad_branch, full_out)
            .astype(jnp.bfloat16)
            .reshape(per_micro, piece_len, HEADS * HD)
        )
        grad_heads = lax.all_to_all(
            grad_context, "seq", split_axis=2, concat_axis=1, tiled=True
        ).reshape(per_micro, length, local_heads, HD)
        grad_query, grad_key, grad_value = attend_backward(
            queries, key_rows, values, ids_micro, log_sums, grad_heads, block_rows
        )
        grad_stack = jnp.stack([grad_query, grad_key, grad_value], axis=3).reshape(
            per_micro, length, local_heads * 3 * HD
        )
        grad_tok_side = (
            lax.all_to_all(grad_stack, "seq", split_axis=1, concat_axis=2, tiled=True)
            .reshape(per_micro, piece_len, HEADS, 3, HD)
            .astype(jnp.float32)
        )
        grad_mixed = jnp.stack(
            [
                rotate(grad_tok_side[:, :, :, 0], cosine, -sine),
                rotate(grad_tok_side[:, :, :, 1], cosine, -sine),
                grad_tok_side[:, :, :, 2],
            ],
            axis=3,
        )
        grad_mixed = grad_mixed.astype(jnp.bfloat16).reshape(-1, 3 * HEADS * HD)
        acc_qkv = acc_qkv + contract_rows(low_one, grad_mixed)
        grad_normed_one = contract_cols(grad_mixed, full_qkv)
        unused_one, pull_one = jax.vjp(normalize, rows_in, gain_one)
        grad_input_part, grad_gain_one = pull_one(grad_normed_one)
        acc_gain_attn = acc_gain_attn + grad_gain_one
        input_grads.append(
            (grad_hidden + grad_input_part).astype(jnp.bfloat16).reshape(per_micro, piece_len, D)
        )
    totals = (acc_qkv, acc_out, acc_in, acc_down, acc_gain_attn, acc_gain_mlp)
    shards = (
        lax.psum_scatter(
            totals[0].astype(jnp.bfloat16), "fsdp", scatter_dimension=0, tiled=True
        ).astype(jnp.float32),
        lax.psum_scatter(
            totals[1].astype(jnp.bfloat16), "fsdp", scatter_dimension=1, tiled=True
        ).astype(jnp.float32),
        lax.psum_scatter(
            totals[2].astype(jnp.bfloat16), "fsdp", scatter_dimension=0, tiled=True
        ).astype(jnp.float32),
        lax.psum_scatter(
            totals[3].astype(jnp.bfloat16), "fsdp", scatter_dimension=1, tiled=True
        ).astype(jnp.float32),
        lax.psum_scatter(
            totals[4].astype(jnp.bfloat16), "fsdp", scatter_dimension=0, tiled=True
        ).astype(jnp.float32),
        lax.psum_scatter(
            totals[5].astype(jnp.bfloat16), "fsdp", scatter_dimension=0, tiled=True
        ).astype(jnp.float32),
    )
    owned = (
        lax.psum(shards[0].astype(jnp.bfloat16), "seq").astype(jnp.float32),
        lax.psum(shards[1].astype(jnp.bfloat16), "seq").astype(jnp.float32),
        lax.psum(shards[2].astype(jnp.bfloat16), "seq").astype(jnp.float32),
        lax.psum(shards[3].astype(jnp.bfloat16), "seq").astype(jnp.float32),
        lax.psum(shards[4].astype(jnp.bfloat16), "seq").astype(jnp.float32),
        lax.psum(shards[5].astype(jnp.bfloat16), "seq").astype(jnp.float32),
    )
    return (
        jnp.concatenate(outputs, axis=0),
        jnp.concatenate(input_grads, axis=0),
        owned[0],
        owned[1],
        owned[2],
        owned[3],
        owned[4],
        owned[5],
    )


def solution(mesh):
    return jax.shard_map(
        local,
        mesh=mesh,
        in_specs=(
            P("fsdp", "seq", None),
            P("fsdp", "seq"),
            P("fsdp", None),
            P(None, "fsdp"),
            P("fsdp", None),
            P(None, "fsdp"),
            P("fsdp"),
            P("fsdp"),
            P("fsdp", "seq", None),
        ),
        out_specs=(
            P("fsdp", "seq", None),
            P("fsdp", "seq", None),
            P("fsdp", None),
            P(None, "fsdp"),
            P("fsdp", None),
            P(None, "fsdp"),
            P("fsdp"),
            P("fsdp"),
        ),
        check_vma=False,
    )
```

profile of v0, /device:TPU:0, one launch (start us, length us, event | category | flops | bytes accessed | tf_op | source)
XLA Modules:
  0.0 875.4 jit_solution(6142257647087376550)
XLA Ops:
  10.0 9.5 %all_gather.27 = s32[2,1024]{1,0:T(2,128)S(1)} all-gather(s32[2,256]{1,0:T(2,128)S(1)} %copy-done.105), channel_id=1, replica_groups=mesh['fsdp'=8,'seq'=4] {'seq'}, dimensions={1}, use_global_device_ids=true | all-gather | bytes 10240 | tf_op jit(solution)/shard_map/all_gather | solution.py:178
  20.8 12.1 %all-gather = bf16[8,1,128]{2,1,0:T(2,128)(2,1)S(1)} all-gather(bf16[1,1,128]{2,1,0:T(2,128)(2,1)S(1)} %bitcast.621), channel_id=1, replica_groups=mesh['fsdp'=8,'seq'=4] {'fsdp'}, dimensions={0}, use_global_device_ids=true | all-gather | bytes 2304 | tf_op jit(solution)/shard_map/all_gather | solution.py:69
  35.1 42.1 %all-gather.7.cloned.1.call-done = bf16[1024,3072]{1,0:T(8,128)(2,1)} async-done(((bf16[128,3072]{1,0:T(8,128)(2,1)}), bf16[1024,3072]{1,0:T(8,128)(2,1)}) %all-gather.7.cloned.1.call-update) | async-done | bytes 6291472 | tf_op jit(solution)/shard_map/all_gather | solution.py:65
  77.2 8.7 copy.179
  85.8 4.9 convolution_bitcast_fusion
  91.6 19.0 %copy.248 = bf16[1,256,3072]{1,0,2:T(2,128)(2,1)} copy(bf16[1,256,3072]{1,2,0:T(8,128)(2,1)S(1)} %bitcast.566) | data formatting | bytes 3145728 | tf_op jit(solution)/shard_map/convert_element_type | solution.py:212
  111.2 16.6 %reduce.28 = bf16[3072,256]{1,0:T(8,128)(2,1)S(1)} reduce(bf16[3072,1,256]{2,1,0:T(2,128)(2,1)} %bitcast.544, bf16[]{:T(256)} %broadcast.964), dimensions={1}, to_apply=%bitcast.451.reduce_sub_computation | reduce | bytes 3145730
  129.6 15.8 %all-to-all-start.2 = ((bf16[4,2,98304]{2,1,0:T(2,128)(2,1)}), bf16[4,2,98304]{2,1,0:T(2,128)(2,1)}, u32[]{:S(2)}, u32[]{:S(2)}) async-start(bf16[4,2,98304]{2,1,0:T(2,128)(2,1)} %reshape.1197), calls=%async_computation.2 | async-start | bytes 3145728 | tf_op jit(solution)/shard_map/all_to_all | solution.py:213
  145.4 5.0 convolution_bitcast_fusion.1
  151.3 17.5 %copy.249 = bf16[1,256,3072]{1,0,2:T(2,128)(2,1)S(1)} copy(bf16[1,256,3072]{1,2,0:T(8,128)(2,1)S(1)} %bitcast.567) | data formatting | bytes 3145728 | tf_op jit(solution)/shard_map/convert_element_type | solution.py:212
  168.9 16.7 %reduce.30 = bf16[3072,256]{1,0:T(8,128)(2,1)} reduce(bf16[3072,1,256]{2,1,0:T(2,128)(2,1)S(1)} %bitcast.546, bf16[]{:T(256)} %broadcast.964), dimensions={1}, to_apply=%bitcast.452.reduce_sub_computation | reduce | bytes 3145730
  185.6 3.7 reshape.1201
  189.3 4.4 all-to-all-start
  203.2 16.9 %while.67 = (s32[]{:T(128)}, bf16[1,1024,4,64]{1,3,2,0:T(8,128)(2,1)S(1)}, f32[1,4,1024]{2,1,0:T(4,128)S(1)}, s32[1,1024]{1,0:T(1,128)S(1)}, bf16[1,1024,4,64]{1...) while((s32[]{:T(128)}, ...), condition=%wide.region_15.16_spmd, body=%wide.region_12.15_spmd.sunk | while | flops 562690048 | bytes 28911796 | solution.py:107
  221.0 3.8 reduce.29
  225.8 4.6 all-to-all-start.3
  230.3 4.5 reshape.1202
  239.6 15.0 %while.66 = (s32[]{:T(128)}, bf16[1,1024,4,64]{1,3,2,0:T(8,128)(2,1)S(1)}, f32[1,4,1024]{2,1,0:T(4,128)S(1)}, s32[1,1024]{1,0:T(1,128)S(1)}, bf16[1,1024,4,64]{1...) while((s32[]{:T(128)}, ...), condition=%wide.region_7.8_spmd, body=%wide.region_4.0_spmd.sunk | while | flops 562690048 | bytes 28911796 | solution.py:107
  256.0 3.8 reduce.31
  260.7 4.2 all-to-all-start.1
  264.9 9.4 %all-gather.1 = bf16[8,1,128]{2,1,0:T(2,128)(2,1)S(1)} all-gather(bf16[1,1,128]{2,1,0:T(2,128)(2,1)S(1)} %bitcast.622), channel_id=1, replica_groups=mesh['fsdp'=8,'seq'=4] {'fsdp'}, dimensions={0}, use_global_device_ids=true | all-gather | bytes 2304 | tf_op jit(solution)/shard_map/all_gather | solution.py:70
  282.6 9.0 %fusion.181 = f32[256,5248]{1,0:T(8,128)} fusion(bf16[1024,5248]{1,0:T(8,128)(2,1)} %all-gather.11.cloned.1.call-done, f32[256,1024]{1,0:T(8,128)S(1)} %get-tuple-element.848, f32[256]{0:T(256)S(1)} %fusion.169, f32[256]{0:T(256)S(1)} %broadcast_multiply_fusion, f32[1024]{0:T(1024)S(1)} %bitcast.592), kind=kOutput, calls=%fused_computation.345 | convolution fusion | flops 2752512000 | bytes 17176576 | tf_op jit(solution)/shard_map/dot_general | solution.py:231
  291.7 12.3 %add_convert_fusion.4 = (bf16[256,2624]{1,0:T(8,128)(2,1)S(1)}, f32[256,2624]{1,0:T(8,128)S(1)}, f32[256,2624]{1,0:T(8,128)}) fusion(f32[256,5248]{1,0:T(8,128)} %fusion.181, bf16[2624,1024]{1,0:T(8,128)(2,1)} %all-gather.13.cloned.1.call-done, bf16[2,256,1024]{2,1,0:T(8,128)(2,1)S(1)} %copy-done.25), kind=kOutput, calls=%fused_computation.127 | convolution fusion | flops 1424769024 | bytes 17989632 | tf_op jit(solution)/shard_map/dot_general | solution.py:58
  304.0 4.3 multiply_convert_fusion.2
  313.0 12.0 %add_convert_fusion.5 = (bf16[256,2624]{1,0:T(8,128)(2,1)}, f32[256,2624]{1,0:T(8,128)S(1)}, f32[256,2624]{1,0:T(8,128)}) fusion(f32[256,5248]{1,0:T(8,128)S(1)} %fusion.180, bf16[2624,1024]{1,0:T(8,128)(2,1)} %all-gather.13.cloned.1.call-done, bf16[2,256,1024]{2,1,0:T(8,128)(2,1)S(1)} %copy-done.26), kind=kOutput, calls=%fused_computation.129 | convolution fusion | flops 1424769024 | bytes 18120704 | tf_op jit(solution)/shard_map/dot_general | solution.py:58
  325.0 4.1 multiply_convert_fusion.3
  329.1 4.0 fusion.110
  333.2 6.9 multiply_reduce_fusion.3
  354.2 4.7 reduce.32
  360.8 4.1 all-to-all-start.6
  368.4 3.7 copy.196
  372.0 5.6 reduce.34
  382.6 3.9 add_convert_fusion.2
  386.5 8.0 copy.222
  394.6 4.4 all-to-all-start.4
  399.0 3.6 reshape.1210
  406.4 43.1 %while.69 = (s32[]{:T(128)}, bf16[1,1024,4,64]{1,3,2,0:T(8,128)(2,1)}, f32[1,1024,4,64]{1,3,2,0:T(8,128)S(1)}, f32[1,1024,4,64]{1,3,2,0:T(8,128)}, s32[1,1024]{1...) while((s32[]{:T(128)}, ...), condition=%wide.region_29.30_spmd.clone, body=%wide.region_27.29_spmd.clone.sunk | while | flops 1375729664 | bytes 166529504 | solution.py:159
  424.1 3.4 fusion.290
  445.0 4.5 fusion.290
  451.2 6.1 copy.209
  457.2 11.2 %reduce.33 = bf16[1024,768]{1,0:T(8,128)(2,1)S(1)} reduce(bf16[1024,1,768]{2,1,0:T(2,128)(2,1)} %bitcast.549, bf16[]{:T(256)} %broadcast.964), dimensions={1}, to_apply=%bitcast.389.reduce_sub_computation | reduce | bytes 3145730
  470.3 4.5 all-to-all-start.7
  474.9 3.6 reshape.1206
  484.1 40.5 %while.68 = (s32[]{:T(128)}, bf16[1,1024,4,64]{1,3,2,0:T(8,128)(2,1)}, f32[1,1024,4,64]{1,3,2,0:T(8,128)S(1)}, f32[1,1024,4,64]{1,3,2,0:T(8,128)}, s32[1,1024]{1...) while((s32[]{:T(128)}, ...), condition=%wide.region_22.23_spmd.clone, body=%wide.region_20.22_spmd.clone.sunk | while | flops 1375729664 | bytes 164432320 | solution.py:159
  500.4 3.4 fusion.278
  520.1 4.5 fusion.278
  527.4 7.4 copy.198
  534.8 11.4 %reduce.35 = bf16[1024,768]{1,0:T(8,128)(2,1)} reduce(bf16[1024,1,768]{2,1,0:T(2,128)(2,1)S(1)} %bitcast.545, bf16[]{:T(256)} %broadcast.964), dimensions={1}, to_apply=%bitcast.385.reduce_sub_computation | reduce | bytes 3145730
  546.2 3.7 reshape.1207
  549.9 4.3 all-to-all-start.5
  554.3 3.5 reshape.1212
  565.6 8.9 %all-to-all-done.5 = bf16[4,2,98304]{2,1,0:T(2,128)(2,1)} async-done(((bf16[4,2,98304]{2,1,0:T(2,128)(2,1)}), bf16[4,2,98304]{2,1,0:T(2,128)(2,1)}, u32[]{:S(2)}, u32[]{:S(2)}) %all-to-all-start.5) | async-done | bytes 1572896 | tf_op jit(solution)/shard_map/all_to_all | solution.py:266
  587.3 4.7 add_convert_fusion.1
  593.2 11.1 %fusion.111 = f32[1024,5248]{1,0:T(8,128)} fusion(bf16[256,2624]{1,0:T(8,128)(2,1)} %get-tuple-element.784, bf16[256,2624]{1,0:T(8,128)(2,1)} %get-tuple-element.772, f32[256,1024]{1,0:T(8,128)S(1)} %copy-done.19, f32[1024]{0:T(1024)S(1)} %bitcast.596, f32[256]{0:T(256)S(1)} %copy-done.82, f32[256]{0:T(256)S(1)} %copy-done.80), kind=kOutput, calls=%fused_computation.167 | convolution fusion | flops 2757885952 | bytes 25237504 | tf_op jit(solution)/shard_map/dot_general | solution.py:52
  604.3 13.2 %add_convert_fusion = bf16[1024,5248]{1,0:T(8,128)(2,1)} fusion(f32[1024,5248]{1,0:T(8,128)} %fusion.111, bf16[256,2624]{1,0:T(8,128)(2,1)} %copy-done.46, bf16[256,2624]{1,0:T(8,128)(2,1)} %copy-done.60, f32[256,1024]{1,0:T(8,128)S(1)} %copy-done.17, f32[256]{0:T(256)S(1)} %copy-done.88, f32[256]{0:T(256)S(1)} %copy-done.84, f32[1024]{0:T(1024)S(1)} %bitcast.597), kind=kOutput, calls=%fused_computation.114 | convolution fusion | flops 2768633856 | bytes 35985408 | tf_op jit(solution)/shard_map/dot_general | solution.py:52
  619.4 4.8 fusion.127
  624.2 4.3 fusion.128
  633.8 26.0 %reduce-scatter.9.cloned.1.call-done = bf16[128,3072]{1,0:T(8,128)(2,1)} async-done(((bf16[1024,3072]{1,0:T(8,128)(2,1)}), bf16[128,3072]{1,0:T(8,128)(2,1)}) %reduce-scatter.9.cloned.1.call-update) | async-done | bytes 786448 | tf_op jit(solution)/shard_map/reduce_scatter | solution.py:289
  659.8 112.6 %reduce-scatter.11.cloned.1.call-done = bf16[128,5248]{1,0:T(8,128)(2,1)} async-done(((bf16[1024,5248]{1,0:T(8,128)(2,1)}), bf16[128,5248]{1,0:T(8,128)(2,1)}) %reduce-scatter.11.cloned.1.call-update) | async-done | bytes 1343504 | tf_op jit(solution)/shard_map/reduce_scatter | solution.py:295
  772.5 4.7 fusion.189
  777.2 5.5 fusion.134
  783.9 13.6 %all-reduce.2 = (bf16[1024]{0:T(1024)(128)(2,1)S(1)}, bf16[1024]{0:T(1024)(128)(2,1)S(1)}) all-reduce(bf16[1024]{0:T(1024)(128)(2,1)S(1)} %add_convert_fusion.13, bf16[1024]{0:T(1024)(128)(2,1)S(1)} %add_convert_fusion.12), channel_id=6, replica_groups=mesh['fsdp'=8,'seq'=4] {'fsdp'}, use_global_device_ids=true, to_apply=%region_42.43.clone | all-reduce | flops 2048 | bytes 8192
  797.6 10.0 %all-reduce.3 = (bf16[128]{0:T(256)(128)(2,1)S(1)}, bf16[128]{0:T(256)(128)(2,1)S(1)}) all-reduce(bf16[128]{0:T(256)(128)(2,1)S(1)} %dynamic-slice.1, bf16[128]{0:T(256)(128)(2,1)S(1)} %dynamic-slice.3), channel_id=1, replica_groups=mesh['fsdp'=8,'seq'=4] {'seq'}, use_global_device_ids=true, to_apply=%region_43.44 | all-reduce | flops 256 | bytes 1024 | tf_op jit(solution)/shard_map/psum | solution.py:313
  812.2 49.2 %all-reduce.7.cloned.1.call-done = (bf16[128,3072]{1,0:T(8,128)(2,1)}, bf16[1024,128]{1,0:T(8,128)(2,1)}, bf16[128,5248]{1,0:T(8,128)(2,1)}, bf16[2624,128]{1,0:T(8,128)(2,1)}) async-done(((bf16[128,3072]{1,0:T(8,128)(2,1)}, bf16[1024,128]{1,0:T(8,128)(2,1)}, bf16[128,5248]{1,0:T(8,128)(2,1)}, bf16[2624,128]{1,0:T(8,128)(2,1)}), (bf16[128,3072]{1,0:T(8,128)(2,1)}, bf16[1024,128]{1,0:T(8,128)(2,1)}, ...) | async-done | bytes 3063824 | tf_op jit(solution)/shard_map/psum | solution.py:309
  (477 shorter events, 221.1 us)
Async XLA Ops:
  7.2 12.4 %copy-start.13 = (bf16[2,256,1024]{2,1,0:T(8,128)(2,1)S(1)}, bf16[2,256,1024]{2,1,0:T(8,128)(2,1)}, u32[]{:S(2)}) copy-start(bf16[2,256,1024]{2,1,0:T(8,128)(2,1)} %param.17) | copy-start | bytes 3145732
  7.2 13.6 %copy-start.106 = (bf16[128]{0:T(256)(128)(2,1)S(1)}, bf16[128]{0:T(256)(128)(2,1)}, u32[]{:S(2)}) copy-start(bf16[128]{0:T(256)(128)(2,1)} %param.23) | copy-start | bytes 772
  7.2 70.0 %all-gather.7.cloned.1.call-start = ((), (), s32[]{:S(2)}) async-start(), calls=%async_computation.12 | async-start | bytes 7077888 | tf_op jit(solution)/shard_map/all_gather | solution.py:65
  7.9 270.6 %all-gather.9.cloned.1.call-start = ((), (), s32[]{:S(2)}) async-start(), calls=%async_computation.13 | async-start | bytes 2359296 | tf_op jit(solution)/shard_map/all_gather | solution.py:66
  8.7 273.9 %all-gather.11.cloned.1.call-start = ((), (), s32[]{:S(2)}) async-start(), calls=%async_computation.14 | async-start | bytes 12091392 | tf_op jit(solution)/shard_map/all_gather | solution.py:67
  9.4 282.3 %all-gather.13.cloned.1.call-start = ((), (), s32[]{:S(2)}) async-start(), calls=%async_computation.15 | async-start | bytes 6045696 | tf_op jit(solution)/shard_map/all_gather | solution.py:68
  19.8 66.0 %copy-start.91 = (f32[256]{0:T(256)}, f32[256]{0:T(256)S(1)}, u32[]{:S(2)}) copy-start(f32[256]{0:T(256)S(1)} %get-tuple-element.855) | copy-start | bytes 3076
  19.8 125.6 %copy-start.85 = (f32[256]{0:T(256)}, f32[256]{0:T(256)S(1)}, u32[]{:S(2)}) copy-start(f32[256]{0:T(256)S(1)} %get-tuple-element.856) | copy-start | bytes 3076
  20.2 13.9 %copy-start.97 = (f32[256]{0:T(256)}, f32[256]{0:T(256)S(1)}, u32[]{:S(2)}) copy-start(f32[256]{0:T(256)S(1)} %get-tuple-element.688) | copy-start | bytes 3076
  20.8 65.0 %copy-start.93 = (f32[256]{0:T(256)}, f32[256]{0:T(256)S(1)}, u32[]{:S(2)}) copy-start(f32[256]{0:T(256)S(1)} %fusion.168) | copy-start | bytes 3076
  32.9 112.5 %copy-start.71 = (f32[8,1,128]{2,1,0:T(1,128)}, f32[8,1,128]{2,1,0:T(1,128)S(1)}, u32[]{:S(2)}) copy-start(f32[8,1,128]{2,1,0:T(1,128)S(1)} %convert_element_type.414) | copy-start | bytes 12292
  34.1 111.3 %copy-start.89 = (f32[256]{0:T(256)}, f32[256]{0:T(256)S(1)}, u32[]{:S(2)}) copy-start(f32[256]{0:T(256)S(1)} %fusion.166) | copy-start | bytes 3076
  35.1 55.9 %copy-start.69 = (f32[256,32]{0,1:T(8,128)}, f32[256,32]{0,1:T(8,128)S(1)}, u32[]{:S(2)}) copy-start(f32[256,32]{0,1:T(8,128)S(1)} %get-tuple-element.839) | copy-start | bytes 98308
  35.1 115.6 %copy-start.67 = (f32[256,32]{0,1:T(8,128)}, f32[256,32]{0,1:T(8,128)S(1)}, u32[]{:S(2)}) copy-start(f32[256,32]{0,1:T(8,128)S(1)} %get-tuple-element.844) | copy-start | bytes 98308
  129.6 59.7 %all-to-all-start.2 = ((bf16[4,2,98304]{2,1,0:T(2,128)(2,1)}), bf16[4,2,98304]{2,1,0:T(2,128)(2,1)}, u32[]{:S(2)}, u32[]{:S(2)}) async-start(bf16[4,2,98304]{2,1,0:T(2,128)(2,1)} %reshape.1197), calls=%async_computation.2 | async-start | bytes 3145728 | tf_op jit(solution)/shard_map/all_to_all | solution.py:213
  189.3 36.5 %all-to-all-start = ((bf16[4,2,98304]{2,1,0:T(2,128)(2,1)}), bf16[4,2,98304]{2,1,0:T(2,128)(2,1)}, u32[]{:S(2)}, u32[]{:S(2)}) async-start(bf16[4,2,98304]{2,1,0:T(2,128)(2,1)} %reshape.1201), calls=%async_computation | async-start | bytes 3145728 | tf_op jit(solution)/shard_map/all_to_all | solution.py:213
  220.1 14.7 %copy-start.8 = (bf16[1,1024,4,64]{1,3,2,0:T(8,128)(2,1)}, bf16[1,1024,4,64]{1,3,2,0:T(8,128)(2,1)S(1)}, u32[]{:S(2)}) copy-start(bf16[1,1024,4,64]{1,3,2,0:T(8,128)(2,1)S(1)} %get-tuple-element.1248) | copy-start | bytes 1572868
  220.1 14.7 %copy-start.23 = (bf16[1,1024,4,64]{1,3,2,0:T(8,128)(2,1)}, bf16[1,1024,4,64]{1,3,2,0:T(8,128)(2,1)S(1)}, u32[]{:S(2)}) copy-start(bf16[1,1024,4,64]{1,3,2,0:T(8,128)(2,1)S(1)} %get-tuple-element.1258) | copy-start | bytes 1572868
  220.1 14.7 %copy-start.64 = (s32[1,1024]{1,0:T(1,128)}, s32[1,1024]{1,0:T(1,128)S(1)}, u32[]{:S(2)}) copy-start(s32[1,1024]{1,0:T(1,128)S(1)} %get-tuple-element.1273) | copy-start | bytes 12292
  220.1 14.7 %copy-start.75 = (f32[1,4,1024]{2,1,0:T(4,128)}, f32[1,4,1024]{2,1,0:T(4,128)S(1)}, u32[]{:S(2)}) copy-start(f32[1,4,1024]{2,1,0:T(4,128)S(1)} %get-tuple-element.1154) | copy-start | bytes 49156
  225.8 35.0 %all-to-all-start.3 = ((bf16[4,2,32768]{2,1,0:T(2,128)(2,1)}), bf16[4,2,32768]{2,1,0:T(2,128)(2,1)}, u32[]{:S(2)}, u32[]{:S(2)}) async-start(bf16[4,2,32768]{2,1,0:T(2,128)(2,1)} %reshape.1199), calls=%async_computation.3 | async-start | bytes 1048576 | tf_op jit(solution)/shard_map/all_to_all | solution.py:221
  254.5 6.2 copy-start.62
  254.6 22.0 %copy-start.6 = (bf16[1,1024,4,64]{1,3,2,0:T(8,128)(2,1)}, bf16[1,1024,4,64]{1,3,2,0:T(8,128)(2,1)S(1)}, u32[]{:S(2)}) copy-start(bf16[1,1024,4,64]{1,3,2,0:T(8,128)(2,1)S(1)} %get-tuple-element.1247) | copy-start | bytes 1572868
  254.6 22.0 %copy-start.11 = (bf16[1,1024,4,64]{1,3,2,0:T(8,128)(2,1)}, bf16[1,1024,4,64]{1,3,2,0:T(8,128)(2,1)S(1)}, u32[]{:S(2)}) copy-start(bf16[1,1024,4,64]{1,3,2,0:T(8,128)(2,1)S(1)} %get-tuple-element.1252) | copy-start | bytes 1572868
  254.6 22.0 %copy-start.21 = (bf16[1,1024,4,64]{1,3,2,0:T(8,128)(2,1)}, bf16[1,1024,4,64]{1,3,2,0:T(8,128)(2,1)S(1)}, u32[]{:S(2)}) copy-start(bf16[1,1024,4,64]{1,3,2,0:T(8,128)(2,1)S(1)} %get-tuple-element.1257) | copy-start | bytes 1572868
  254.6 10.4 %copy-start.107 = (bf16[128]{0:T(256)(128)(2,1)S(1)}, bf16[128]{0:T(256)(128)(2,1)}, u32[]{:S(2)}) copy-start(bf16[128]{0:T(256)(128)(2,1)} %param.24) | copy-start | bytes 772
  260.7 16.2 %all-to-all-start.1 = ((bf16[4,2,32768]{2,1,0:T(2,128)(2,1)}), bf16[4,2,32768]{2,1,0:T(2,128)(2,1)S(1)}, u32[]{:S(2)}, u32[]{:S(2)}) async-start(bf16[4,2,32768]{2,1,0:T(2,128)(2,1)} %reshape.1203), calls=%async_computation.1 | async-start | bytes 1048576 | tf_op jit(solution)/shard_map/all_to_all | solution.py:221
  264.9 364.7 %reduce-scatter.13.cloned.1.call-start = ((), (), s32[]{:S(2)}) async-start(), calls=%async_computation.18 | async-start | bytes 2359296
  274.3 65.7 %copy-start.58 = (f32[8,1,128]{2,1,0:T(1,128)}, f32[8,1,128]{2,1,0:T(1,128)S(1)}, u32[]{:S(2)}) copy-start(f32[8,1,128]{2,1,0:T(1,128)S(1)} %convert_element_type.415) | copy-start | bytes 12292
  281.1 58.9 %copy-start.16 = (f32[256,1024]{1,0:T(8,128)}, f32[256,1024]{1,0:T(8,128)S(1)}, u32[]{:S(2)}) copy-start(f32[256,1024]{1,0:T(8,128)S(1)} %get-tuple-element.848) | copy-start | bytes 3145732
  281.2 58.9 %copy-start.83 = (f32[256]{0:T(256)}, f32[256]{0:T(256)S(1)}, u32[]{:S(2)}) copy-start(f32[256]{0:T(256)S(1)} %broadcast_multiply_fusion) | copy-start | bytes 3076
  282.3 57.8 %copy-start.18 = (f32[256,1024]{1,0:T(8,128)}, f32[256,1024]{1,0:T(8,128)S(1)}, u32[]{:S(2)}) copy-start(f32[256,1024]{1,0:T(8,128)S(1)} %get-tuple-element.851) | copy-start | bytes 3145732
  282.3 57.8 %copy-start.79 = (f32[256]{0:T(256)}, f32[256]{0:T(256)S(1)}, u32[]{:S(2)}) copy-start(f32[256]{0:T(256)S(1)} %broadcast_multiply_fusion.2) | copy-start | bytes 3076
  282.6 57.5 %copy-start.87 = (f32[256]{0:T(256)}, f32[256]{0:T(256)S(1)}, u32[]{:S(2)}) copy-start(f32[256]{0:T(256)S(1)} %fusion.169) | copy-start | bytes 3076
  282.6 57.5 %copy-start.81 = (f32[256]{0:T(256)}, f32[256]{0:T(256)S(1)}, u32[]{:S(2)}) copy-start(f32[256]{0:T(256)S(1)} %fusion.167) | copy-start | bytes 3076
  282.6 9.1 %copy-start.25 = (bf16[2,256,1024]{2,1,0:T(8,128)(2,1)S(1)}, bf16[2,256,1024]{2,1,0:T(8,128)(2,1)}, u32[]{:S(2)}) copy-start(bf16[2,256,1024]{2,1,0:T(8,128)(2,1)} %param.25) | copy-start | bytes 3145732
  291.7 12.4 %copy-start.20 = (f32[256,5248]{1,0:T(8,128)S(1)}, f32[256,5248]{1,0:T(8,128)}, u32[]{:S(2)}) copy-start(f32[256,5248]{1,0:T(8,128)} %fusion.181) | copy-start | bytes 16121860
  304.0 25.1 %copy-start.60 = (bf16[256,2624]{1,0:T(8,128)(2,1)}, bf16[256,2624]{1,0:T(8,128)(2,1)S(1)}, u32[]{:S(2)}) copy-start(bf16[256,2624]{1,0:T(8,128)(2,1)S(1)} %get-tuple-element.774) | copy-start | bytes 4030468
  309.9 19.2 %copy-start.46 = (bf16[256,2624]{1,0:T(8,128)(2,1)}, bf16[256,2624]{1,0:T(8,128)(2,1)S(1)}, u32[]{:S(2)}) copy-start(bf16[256,2624]{1,0:T(8,128)(2,1)S(1)} %get-tuple-element.786) | copy-start | bytes 4030468
  360.8 33.7 %all-to-all-start.6 = ((bf16[4,2,32768]{2,1,0:T(2,128)(2,1)}), bf16[4,2,32768]{2,1,0:T(2,128)(2,1)}, u32[]{:S(2)}, u32[]{:S(2)}) async-start(bf16[4,2,32768]{2,1,0:T(2,128)(2,1)} %reshape.1209), calls=%async_computation.6 | async-start | bytes 1048576 | tf_op jit(solution)/shard_map/all_to_all | solution.py:256
  365.0 266.6 %reduce-scatter.15.cloned.1.call-start = ((), (), s32[]{:S(2)}) async-start(), calls=%async_computation.19 | async-start | bytes 6193152
  368.4 11.2 %copy-start.28 = (bf16[2,256,1024]{2,1,0:T(8,128)(2,1)S(1)}, bf16[2,256,1024]{2,1,0:T(8,128)(2,1)}, u32[]{:S(2)}) copy-start(bf16[2,256,1024]{2,1,0:T(8,128)(2,1)} %param.25) | copy-start | bytes 3145732
  394.6 75.8 %all-to-all-start.4 = ((bf16[4,2,32768]{2,1,0:T(2,128)(2,1)}), bf16[4,2,32768]{2,1,0:T(2,128)(2,1)}, u32[]{:S(2)}, u32[]{:S(2)}) async-start(bf16[4,2,32768]{2,1,0:T(2,128)(2,1)} %reshape.1205), calls=%async_computation.4 | async-start | bytes 1048576 | tf_op jit(solution)/shard_map/all_to_all | solution.py:256
  399.0 7.4 copy-start.9
  399.0 7.4 copy-start.65
  399.0 7.4 copy-start.76
  470.3 79.6 %all-to-all-start.7 = ((bf16[4,2,98304]{2,1,0:T(2,128)(2,1)}), bf16[4,2,98304]{2,1,0:T(2,128)(2,1)}, u32[]{:S(2)}, u32[]{:S(2)}) async-start(bf16[4,2,98304]{2,1,0:T(2,128)(2,1)} %reshape.1211), calls=%async_computation.7 | async-start | bytes 3145728 | tf_op jit(solution)/shard_map/all_to_all | solution.py:266
  474.9 9.2 %copy-start.7 = (bf16[1,1024,4,64]{1,3,2,0:T(8,128)(2,1)S(1)}, bf16[1,1024,4,64]{1,3,2,0:T(8,128)(2,1)}, u32[]{:S(2)}) copy-start(bf16[1,1024,4,64]{1,3,2,0:T(8,128)(2,1)} %copy-done.6) | copy-start | bytes 1572868
  474.9 9.2 %copy-start.12 = (bf16[1,1024,4,64]{1,3,2,0:T(8,128)(2,1)S(1)}, bf16[1,1024,4,64]{1,3,2,0:T(8,128)(2,1)}, u32[]{:S(2)}) copy-start(bf16[1,1024,4,64]{1,3,2,0:T(8,128)(2,1)} %copy-done.11) | copy-start | bytes 1572868
  474.9 9.2 %copy-start.22 = (bf16[1,1024,4,64]{1,3,2,0:T(8,128)(2,1)S(1)}, bf16[1,1024,4,64]{1,3,2,0:T(8,128)(2,1)}, u32[]{:S(2)}) copy-start(bf16[1,1024,4,64]{1,3,2,0:T(8,128)(2,1)} %copy-done.21) | copy-start | bytes 1572868
  474.9 9.2 %copy-start.63 = (s32[1,1024]{1,0:T(1,128)S(1)}, s32[1,1024]{1,0:T(1,128)}, u32[]{:S(2)}) copy-start(s32[1,1024]{1,0:T(1,128)} %copy-done.62) | copy-start | bytes 12292
  474.9 9.2 %copy-start.74 = (f32[1,4,1024]{2,1,0:T(4,128)S(1)}, f32[1,4,1024]{2,1,0:T(4,128)}, u32[]{:S(2)}) copy-start(f32[1,4,1024]{2,1,0:T(4,128)} %copy-done.73) | copy-start | bytes 49156
  549.9 24.6 %all-to-all-start.5 = ((bf16[4,2,98304]{2,1,0:T(2,128)(2,1)}), bf16[4,2,98304]{2,1,0:T(2,128)(2,1)}, u32[]{:S(2)}, u32[]{:S(2)}) async-start(bf16[4,2,98304]{2,1,0:T(2,128)(2,1)} %reshape.1207), calls=%async_computation.5 | async-start | bytes 3145728 | tf_op jit(solution)/shard_map/all_to_all | solution.py:266
  554.3 105.6 %reduce-scatter.9.cloned.1.call-start = ((), (), s32[]{:S(2)}) async-start(), calls=%async_computation.16 | async-start | bytes 7077888 | tf_op jit(solution)/shard_map/reduce_scatter | solution.py:289
  592.0 12.3 %copy-start.17 = (f32[256,1024]{1,0:T(8,128)S(1)}, f32[256,1024]{1,0:T(8,128)}, u32[]{:S(2)}) copy-start(f32[256,1024]{1,0:T(8,128)} %copy-done.16) | copy-start | bytes 3145732
  592.0 12.3 %copy-start.84 = (f32[256]{0:T(256)S(1)}, f32[256]{0:T(256)}, u32[]{:S(2)}) copy-start(f32[256]{0:T(256)} %copy-done.83) | copy-start | bytes 3076
  592.1 12.2 %copy-start.88 = (f32[256]{0:T(256)S(1)}, f32[256]{0:T(256)}, u32[]{:S(2)}) copy-start(f32[256]{0:T(256)} %copy-done.87) | copy-start | bytes 3076
  592.1 180.3 %reduce-scatter.11.cloned.1.call-start = ((), (), s32[]{:S(2)}) async-start(), calls=%async_computation.17 | async-start | bytes 12091392 | tf_op jit(solution)/shard_map/reduce_scatter | solution.py:295
  617.6 243.9 %all-reduce.7.cloned.1.call-start = ((), (), s32[]{:S(2)}) async-start(), calls=%async_computation.20 | async-start | bytes 6127616 | tf_op jit(solution)/shard_map/psum | solution.py:309
  629.6 142.8 %copy-start.42 = (bf16[1,256,16,3,64]{1,4,3,2,0:T(8,128)(2,1)S(1)}, bf16[1,256,16,3,64]{1,4,3,2,0:T(8,128)(2,1)}, u32[]{:S(2)}) copy-start(bf16[1,256,16,3,64]{1,4,3,2,0:T(8,128)(2,1)} %copy.215) | copy-start | bytes 4718596
  782.7 26.0 %copy-start.29 = (bf16[2,256,1024]{2,1,0:T(8,128)(2,1)S(1)}, bf16[2,256,1024]{2,1,0:T(8,128)(2,1)}, u32[]{:S(2)}) copy-start(bf16[2,256,1024]{2,1,0:T(8,128)(2,1)} %param.25) | copy-start | bytes 3145732
  782.7 26.0 %copy-start.31 = (f32[256,1024]{1,0:T(8,128)S(1)}, f32[256,1024]{1,0:T(8,128)}, u32[]{:S(2)}) copy-start(f32[256,1024]{1,0:T(8,128)} %copy-done.30) | copy-start | bytes 3145732
  782.7 26.0 %copy-start.100 = (f32[256]{0:T(256)S(1)}, f32[256]{0:T(256)}, u32[]{:S(2)}) copy-start(f32[256]{0:T(256)} %copy-done.99) | copy-start | bytes 3076
  782.8 26.0 %copy-start.102 = (f32[256]{0:T(256)S(1)}, f32[256]{0:T(256)}, u32[]{:S(2)}) copy-start(f32[256]{0:T(256)} %copy-done.101) | copy-start | bytes 3076
  (77 other events, 212.0 us)
Sparse Core Ops, SparseCore 0:
  9.7 67.4 all-gather.6
  78.7 29.5 all-gather.8
  109.9 100.6 all-gather.10
  212.1 55.9 all-gather.12
  348.4 35.1 reduce-scatter.12
  394.7 61.6 reduce-scatter.14
  592.2 67.6 reduce-scatter.8
  662.1 110.2 reduce-scatter.10
  776.5 84.8 all-reduce.6
where the time goes:
time: 882 us; the launch traced here: 875 us
  waiting for transfers between devices  242 us (27%)
  matrix products  202 us (23%)
  local copies, waits for them, and re-layouts  183 us (21%)
  other arithmetic  131 us (15%)
  blocking collectives  54.7 us (6%)
  starting transfers between devices  46.7 us (5%)
  between operations  16.5 us (2%)
    reduce_scatter x1, waiting for transfers between devices, local(): lax.psum_scatter(totals[2].astype(jnp.bfloat16), 'fsdp', scatter_dimensio...  113 us
    unnamed x14, other arithmetic  74 us
    unnamed x222, local copies, waits for them, and re-layouts  71.5 us
    dot_general x8, matrix products, contract_cols(): lax.dot_general(left, right, (((1,), (1,)), ((), ())), preferred_element_...  51.9 us
    psum x1, waiting for transfers between devices, local(): lax.psum(shards[0].astype(jnp.bfloat16), 'seq').astype(jnp.float32)  49.2 us
    all_gather x1, waiting for transfers between devices, fetch(): lax.all_gather(w_qkv, 'fsdp', axis=0, tiled=True)  42.1 us
    dot_general x8, matrix products, contract_rows(): lax.dot_general(left, right, (((0,), (0,)), ((), ())), preferred_element_...  39.4 us
    convert_element_type x2, local copies, waits for them, and re-layouts, local(): stacked.astype(jnp.bfloat16).reshape(per_micro, piece_len, HEADS * 3 * HD)  36.5 us
  transfers between devices with their start and end apart: 17, of which 5 were waited for; matrix products, arithmetic and copies ran while one was open for 49% of the time, Pallas kernels for 0%

commit v1 on v0

--- a/solution.py
+++ b/solution.py
@@ -1,8 +1,12 @@
+import functools
 import math
 
 import jax
 import jax.numpy as jnp
 from jax import lax
+from jax.experimental import pallas as pl
+from jax.experimental.pallas import tpu as pltpu
+from jax.sharding import Mesh
 from jax.sharding import PartitionSpec as P
 
 D = 1024
@@ -325,7 +329,7 @@
     )
 
 
-def solution(mesh):
+def spread(mesh):
     return jax.shard_map(
         local,
         mesh=mesh,
@@ -352,3 +356,530 @@
         ),
         check_vma=False,
     )
+
+
+F32 = jnp.float32
+BF16 = jnp.bfloat16
+NN = (((1,), (0,)), ((), ()))
+NT = (((1,), (1,)), ((), ()))
+TN = (((0,), (0,)), ((), ()))
+MIB = 1 << 20
+LANES = 128
+HALF = HD // 2
+PAIR = 2
+QKV = 3 * PAIR * HD
+OUT = PAIR * HD
+UNITS = FF // 8
+HIDDEN = -(-UNITS // 16) * 16
+EXTRA = 16
+TILE = 256
+BOTH = [(0, 1), (1, 0)]
+
+
+def mul(left, right, dims):
+    return lax.dot_general(left, right, dims, preferred_element_type=F32)
+
+
+def whole_in_vmem(count):
+    return [pl.BlockSpec(memory_space=pltpu.VMEM)] * count
+
+
+def lay_flat(flat_ref, blocks_ref, start, count, to=0):
+    for k in range(blocks_ref.shape[0]):
+        flat_ref[to : to + count, LANES * k : LANES * (k + 1)] = blocks_ref[k, start : start + count, :]
+
+
+def mlp_body(first, n_ref, dy_ref, w_ref, *rest):
+    if first:
+        y_ref, dn_ref, ga_ref, gb_ref, w_all, acc = rest
+    else:
+        y_in, dn_in, y_ref, dn_ref, ga_ref, gb_ref, w_all, acc = rest
+    step = pl.program_id(0)
+
+    @pl.when(step == 0)
+    def _():
+        lay_flat(w_all, w_ref, OUT, 3 * HIDDEN)
+
+    n_t = n_ref[...]
+    dy_t = dy_ref[...]
+    gate = mul(w_all[0:HIDDEN, :], n_t, NT)
+    up = mul(w_all[HIDDEN : 2 * HIDDEN, :], n_t, NT)
+    dm = mul(w_all[2 * HIDDEN :, :], dy_t, NT)
+    phi = 0.5 * (1.0 + lax.erf(gate * math.sqrt(0.5)))
+    gelu = gate * phi
+    slope = phi + gate * (jnp.exp(-0.5 * gate * gate) * (1.0 / math.sqrt(2.0 * math.pi)))
+    mix = (gelu * up).astype(BF16)
+    dgu = jnp.concatenate([dm * up * slope, dm * gelu], axis=0).astype(BF16)
+    y = mul(mix, w_all[2 * HIDDEN :, :], TN)
+    dn = mul(dgu, w_all[0 : 2 * HIDDEN, :], TN)
+    if first:
+        y_ref[...] = y
+        dn_ref[...] = dn
+    else:
+        y_ref[...] = y_in[...] + y
+        dn_ref[...] = dn_in[...] + dn
+    g_in = mul(dgu, n_t, NN)
+    g_down = mul(mix, dy_t, NN)
+
+    @pl.when(step == 0)
+    def _():
+        acc[0 : 2 * HIDDEN, :] = g_in
+        acc[2 * HIDDEN :, :] = g_down
+
+    @pl.when(step != 0)
+    def _():
+        acc[0 : 2 * HIDDEN, :] += g_in
+        acc[2 * HIDDEN :, :] += g_down
+
+    @pl.when(step == pl.num_programs(0) - 1)
+    def _():
+        half = ga_ref.shape[0]
+        for k in range(half):
+            ga_ref[k] = acc[:, LANES * k : LANES * (k + 1)].astype(BF16)
+            gb_ref[k] = acc[:, LANES * (k + half) : LANES * (k + half + 1)].astype(BF16)
+
+
+def mlp(n2, dy, weights, sums):
+    first = sums is None
+    tokens, width = n2.shape
+    blocks, rows, lanes = weights.shape
+    row_tile = pl.BlockSpec((TILE, width), lambda t: (t, 0))
+    half = pl.BlockSpec((blocks // 2, 3 * HIDDEN, lanes), lambda t: (0, 0, 0))
+    total = jax.ShapeDtypeStruct((tokens, width), F32)
+    grads = jax.ShapeDtypeStruct((blocks // 2, 3 * HIDDEN, lanes), BF16)
+    y, dn, ga, gb = pl.pallas_call(
+        functools.partial(mlp_body, first),
+        grid=(tokens // TILE,),
+        in_specs=[row_tile, row_tile, pl.BlockSpec(weights.shape, lambda t: (0, 0, 0))]
+        + ([] if first else [row_tile, row_tile]),
+        out_specs=[row_tile, row_tile, half, half],
+        out_shape=[total, total, grads, grads],
+        scratch_shapes=[pltpu.VMEM((3 * HIDDEN, width), BF16), pltpu.VMEM((3 * HIDDEN, width), F32)],
+        input_output_aliases={} if first else {3: 0, 4: 1},
+        compiler_params=pltpu.CompilerParams(vmem_limit_bytes=40 * MIB),
+        cost_estimate=pl.CostEstimate(
+            flops=18 * tokens * HIDDEN * width,
+            transcendentals=2 * tokens * HIDDEN,
+            bytes_accessed=20 * tokens * width + 12 * HIDDEN * width,
+        ),
+        name="mlp",
+    )(*([n2, dy, weights] + ([] if first else list(sums))))
+    return (y, dn), (ga, gb)
+
+
+def lane_group(shape, width):
+    return (lax.broadcasted_iota(jnp.int32, shape, 1) // width) % 2
+
+
+def forward_body(n_ref, w_ref, cos_ref, sin_ref, row_ref, col_ref, q_ref, k_ref, v_ref, o_ref, lse_ref, w_all):
+    tokens = n_ref.shape[0]
+    lay_flat(w_all, w_ref, 0, QKV)
+
+    def project(i, carry):
+        here = pl.ds(pl.multiple_of(i * TILE, TILE), TILE)
+        mixed = mul(n_ref[here, :], w_all[...], NT)
+        cosine, sine = cos_ref[here, :], sin_ref[here, :]
+        query, key = mixed[:, 0:OUT], mixed[:, OUT : 2 * OUT]
+        q_ref[here, :] = (query * cosine + pltpu.roll(query, HD, 1) * sine).astype(BF16)
+        k_ref[here, :] = (key * cosine + pltpu.roll(key, HD, 1) * sine).astype(BF16)
+        v_ref[here, :] = mixed[:, 2 * OUT :].astype(BF16)
+        return carry
+
+    lax.fori_loop(0, tokens // TILE, project, 0)
+
+    def attend(i, carry):
+        here = pl.ds(pl.multiple_of(i * TILE, TILE), TILE)
+        query = q_ref[here, :]
+        allowed = col_ref[here, 0:1] == row_ref[0:1, :]
+        pair = lane_group((TILE, OUT), HALF)
+        outs, sums = [], []
+        for head in range(PAIR):
+            masked = jnp.where(pair == head, query, jnp.zeros_like(query))
+            scores = mul(masked, k_ref[...], NT) * (1.0 / math.sqrt(HD))
+            scores = jnp.where(allowed, scores, -1e30)
+            top = jnp.max(scores, axis=1, keepdims=True)
+            raised = jnp.exp(scores - top)
+            total = jnp.sum(raised, axis=1, keepdims=True)
+            outs.append(mul(raised.astype(BF16), v_ref[...], NN) / total)
+            sums.append(top + jnp.log(total))
+        side = lane_group((TILE, OUT), HD)
+        o_ref[here, :] = jnp.where(side == 0, outs[0], outs[1]).astype(BF16)
+        lane = lax.broadcasted_iota(jnp.int32, (TILE, LANES), 1)
+        both = jnp.where(lane == 0, sums[0], sums[1])
+        lse_ref[:, here] = both.T[0:8, :]
+        return carry
+
+    lax.fori_loop(0, tokens // TILE, attend, 0)
+
+
+def attention(n1, weights, tables):
+    tokens, width = n1.shape
+    return pl.pallas_call(
+        forward_body,
+        in_specs=whole_in_vmem(6),
+        out_specs=whole_in_vmem(5),
+        out_shape=[jax.ShapeDtypeStruct((tokens, OUT), BF16)] * 4 + [jax.ShapeDtypeStruct((8, tokens), F32)],
+        scratch_shapes=[pltpu.VMEM((QKV, width), BF16)],
+        compiler_params=pltpu.CompilerParams(vmem_limit_bytes=32 * MIB),
+        cost_estimate=pl.CostEstimate(
+            flops=2 * tokens * QKV * width + 8 * tokens * tokens * OUT,
+            transcendentals=2 * tokens * tokens,
+            bytes_accessed=6 * MIB,
+        ),
+        name="attention",
+    )(n1, weights, *tables)
+
+
+def backward_body(
+    q_ref, k_ref, v_ref, o_ref, lse_ref, da_ref, n_ref, w_ref, cos_ref, sin_ref, row_ref, col_ref,
+    d_ref, ga_ref, gb_ref, w_all, do_ref, dq_ref, dk_ref, dv_ref,
+):
+    tokens = n_ref.shape[0]
+    scaling = 1.0 / math.sqrt(HD)
+    lay_flat(w_all, w_ref, 0, OUT)
+    do_ref[...] = mul(da_ref[...], w_all[...], NT).astype(BF16)
+    dk_ref[...] = jnp.zeros_like(dk_ref)
+    dv_ref[...] = jnp.zeros_like(dv_ref)
+
+    def step(i, carry):
+        here = pl.ds(pl.multiple_of(i * TILE, TILE), TILE)
+        query, grad = q_ref[here, :], do_ref[here, :]
+        allowed = col_ref[:, 0:1] == row_ref[0:1, here]
+        pair = lane_group((TILE, OUT), HALF)
+        side = lane_group((TILE, OUT), HD)
+        pair_all = lane_group((tokens, OUT), HALF)
+        dq = jnp.zeros((TILE, OUT), F32)
+        for head in range(PAIR):
+            q_m = jnp.where(pair == head, query, jnp.zeros_like(query))
+            g_m = jnp.where(side == head, grad, jnp.zeros_like(grad))
+            k_m = jnp.where(pair_all == head, k_ref[...], jnp.zeros_like(k_ref))
+            scores = mul(k_ref[...], q_m, NT) * scaling
+            share = jnp.exp(jnp.where(allowed, scores - lse_ref[head : head + 1, here], -1e30))
+            dshare = mul(v_ref[...], g_m, NT)
+            delta = jnp.sum(share * dshare, axis=0, keepdims=True)
+            ds = (share * (dshare - delta)).astype(BF16)
+            dv_ref[...] += mul(share.astype(BF16), g_m, NN)
+            dk_ref[...] += mul(ds, q_m, NN)
+            dq += mul(ds, k_m, TN)
+        dq_ref[here, :] = dq
+        return carry
+
+    lax.fori_loop(0, tokens // TILE, step, 0)
+    cosine, sine = cos_ref[...], sin_ref[...]
+    dq = (dq_ref[...] * scaling).astype(BF16).astype(F32)
+    dk = (dk_ref[...] * scaling).astype(BF16).astype(F32)
+    d_ref[:, 0:OUT] = (dq * cosine - pltpu.roll(dq, HD, 1) * sine).astype(BF16)
+    d_ref[:, OUT : 2 * OUT] = (dk * cosine - pltpu.roll(dk, HD, 1) * sine).astype(BF16)
+    d_ref[:, 2 * OUT :] = dv_ref[...].astype(BF16)
+    half = ga_ref.shape[0]
+    for k in range(half):
+        for ref, at in ((ga_ref, k), (gb_ref, k + half)):
+            lanes = slice(LANES * at, LANES * (at + 1))
+            ref[k, 0:QKV, :] = mul(d_ref[...], n_ref[:, lanes], TN).astype(BF16)
+            ref[k, QKV:, :] = mul(o_ref[...], da_ref[:, lanes], TN).astype(BF16)
+
+
+def attention_back(saved, dattn, n1, rest, tables):
+    tokens, width = n1.shape
+    blocks = rest.shape[0]
+    vmem = pl.BlockSpec(memory_space=pltpu.VMEM)
+    grads = jax.ShapeDtypeStruct((blocks // 2, QKV + OUT, LANES), BF16)
+    return pl.pallas_call(
+        backward_body,
+        grid=(1,),
+        in_specs=[vmem] * 7 + [pl.BlockSpec((blocks, OUT, LANES), lambda i: (0, 0, 0))] + [vmem] * 4,
+        out_specs=whole_in_vmem(3),
+        out_shape=[jax.ShapeDtypeStruct((tokens, QKV), BF16), grads, grads],
+        scratch_shapes=[pltpu.VMEM((OUT, width), BF16), pltpu.VMEM((tokens, OUT), BF16)]
+        + [pltpu.VMEM((tokens, OUT), F32)] * 3,
+        compiler_params=pltpu.CompilerParams(vmem_limit_bytes=40 * MIB),
+        cost_estimate=pl.CostEstimate(
+            flops=2 * tokens * width * (QKV + 2 * OUT) + 20 * tokens * tokens * OUT,
+            transcendentals=2 * tokens * tokens,
+            bytes_accessed=10 * MIB,
+        ),
+        name="attention_back",
+    )(*saved, dattn, n1, rest, *tables)
+
+
+def gather_body(count, *refs):
+    lefts, weights = refs[:count], refs[count : 2 * count]
+    own_ref, other_ref, w_all = refs[2 * count :]
+    inner = lefts[0].shape[1]
+    step = pl.program_id(0)
+    steps = pl.num_programs(0)
+
+    @pl.when(step == 0)
+    def _():
+        for r in range(count):
+            lay_flat(w_all, weights[r], 0, inner, r * inner)
+
+    rows = jnp.concatenate([left[...] for left in lefts], axis=1)
+    total = mul(rows, w_all[...], NN)
+
+    @pl.when(step < steps // 2)
+    def _():
+        own_ref[...] = total
+
+    @pl.when(step >= steps // 2)
+    def _():
+        other_ref[...] = total.astype(BF16)
+
+
+def partial_rows(lefts, weights):
+    count = len(lefts)
+    tokens, inner = lefts[0].shape
+    blocks = weights[0].shape[0]
+    width = blocks * LANES
+    steps = tokens // TILE
+    return pl.pallas_call(
+        functools.partial(gather_body, count),
+        grid=(steps,),
+        in_specs=[pl.BlockSpec((TILE, inner), lambda t: (t, 0))] * count
+        + [pl.BlockSpec((blocks, inner, LANES), lambda t: (0, 0, 0))] * count,
+        out_specs=[
+            pl.BlockSpec((TILE, width), lambda t: (jnp.minimum(t, steps // 2 - 1), 0)),
+            pl.BlockSpec((TILE, width), lambda t: (jnp.maximum(t - steps // 2, 0), 0)),
+        ],
+        out_shape=[
+            jax.ShapeDtypeStruct((tokens // 2, width), F32),
+            jax.ShapeDtypeStruct((tokens // 2, width), BF16),
+        ],
+        scratch_shapes=[pltpu.VMEM((count * inner, width), BF16)],
+        compiler_params=pltpu.CompilerParams(vmem_limit_bytes=40 * MIB),
+        cost_estimate=pl.CostEstimate(
+            flops=2 * tokens * count * inner * width, transcendentals=0, bytes_accessed=8 * MIB
+        ),
+        name="partial_rows",
+    )(*lefts, *weights)
+
+
+def swap(value, axis):
+    return lax.ppermute(value, axis, BOTH)
+
+
+def plane_pairs():
+    near, far = [], []
+    for c in range(2):
+        for y in range(2):
+            for x in range(2):
+                at = 4 * c + 2 * y + x
+                if c == y:
+                    near.append((at, 4 * c + 2 * y + 1 - x))
+                else:
+                    near.append((at, 4 * y + 2 * (1 - y) + x))
+                    far.append((at, 4 * y + 2 * (1 - y) + 1 - x))
+    return near, far
+
+
+def to_sequence(local_rows, straight, x):
+    near, far = plane_pairs()
+    first, second = local_rows[0], local_rows[1]
+    same = jnp.where(x == 0, first, second)
+    other = jnp.where(x == 0, second, first)
+    got_near = lax.ppermute(jnp.where(straight, other, same), ("c", "y", "x"), near)
+    got_far = lax.ppermute(other, ("c", "y", "x"), far)
+    return jnp.where(straight, same, got_near), jnp.where(straight, got_near, got_far)
+
+
+def from_sequence(rows, straight, x):
+    near, far = plane_pairs()
+    piece = rows.shape[0] // 2
+    first, second = rows[:piece], rows[piece:]
+    got_near = lax.ppermute(jnp.where(straight, second, first), ("c", "y", "x"), near)
+    got_far = lax.ppermute(second, ("c", "y", "x"), far)
+    same = jnp.where(straight, first, got_near)
+    other = jnp.where(straight, got_near, got_far)
+    return jnp.where(x == 0, jnp.stack([same, other]), jnp.stack([other, same]))
+
+
+def moments(rows):
+    center = jnp.mean(rows, axis=-1, keepdims=True)
+    shifted = rows - center
+    scale = lax.rsqrt(jnp.mean(shifted * shifted, axis=-1, keepdims=True) + 1e-05)
+    return shifted * scale, scale
+
+
+def norm_back(grad, gain, normed, scale):
+    scaled = grad * gain
+    pulled = scaled - jnp.mean(scaled, axis=-1, keepdims=True)
+    pulled = pulled - normed * jnp.mean(scaled * normed, axis=-1, keepdims=True)
+    return pulled * scale, jnp.sum(grad * normed, axis=0)
+
+
+def plane_gather(own):
+    half = own.shape[0] // 2
+    across = swap(own, "x")
+    along = swap(own, "y")
+    corner = jnp.concatenate([swap(along[:half], "x"), swap(across[half:], "y")], axis=0)
+    return [own, across, along, corner]
+
+
+def add_low(left, right):
+    return (left.astype(F32) + right.astype(F32)).astype(BF16)
+
+
+def plane_reduce(parts):
+    a = [part[0] for part in parts]
+    b = [part[1] for part in parts]
+    here_a = add_low(a[0], swap(a[1], "x"))
+    next_a = add_low(a[2], swap(a[3], "x"))
+    here_b = add_low(b[0], swap(b[2], "y"))
+    next_b = add_low(b[1], swap(b[3], "y"))
+    return add_low(here_a, swap(next_a, "y")), add_low(here_b, swap(next_b, "x"))
+
+
+def in_order(parts, x, y, c):
+    stacked = jnp.stack(parts)
+    stacked = jnp.where(x == 0, stacked, stacked[jnp.array([1, 0, 3, 2])])
+    stacked = jnp.where(y == 0, stacked, stacked[jnp.array([2, 3, 0, 1])])
+    return jnp.where(c == 0, stacked, stacked[:, ::-1])
+
+
+def owned_gradient(total, c):
+    mine = lax.psum_scatter(total, "z", scatter_dimension=0, tiled=True)
+    keep = lax.dynamic_index_in_dim(mine, c, 0, keepdims=False)
+    give = lax.dynamic_index_in_dim(mine, 1 - c, 0, keepdims=False)
+    own = jnp.stack([keep, swap(give, "c")])
+    corner = lax.ppermute(own, ("y", "x"), [(0, 3), (1, 2), (2, 1), (3, 0)])
+    return [own, swap(own, "x"), swap(own, "y"), corner]
+
+
+def spread_pieces(pieces, c):
+    keep = lax.dynamic_index_in_dim(pieces, c, 0, keepdims=False)
+    give = lax.dynamic_index_in_dim(pieces, 1 - c, 0, keepdims=False)
+    got = swap(give, "c")
+    both = jnp.where(c == 0, jnp.stack([keep, got]), jnp.stack([got, keep]))
+    return lax.all_gather(both, "z", axis=0, tiled=True)
+
+
+def chip_local(tokens, segment_ids, w_qkv, w_out, w_in, w_down, gain_attn, gain_mlp, grad_output):
+    c, y, x = lax.axis_index("c"), lax.axis_index("y"), lax.axis_index("x")
+    place = 2 * y + x
+    straight = c == y
+    piece = tokens.shape[1]
+
+    qkv = lax.dynamic_index_in_dim(w_qkv.reshape(LANES, 2, 4, QKV), place, 2, keepdims=False)
+    qkv = qkv.reshape(LANES, 2, PAIR, 3, 2, HALF)
+    qk = qkv[:, :, :, 0:2].transpose(1, 3, 4, 2, 5, 0).reshape(2, 2 * OUT, LANES)
+    val = qkv[:, :, :, 2].transpose(1, 2, 3, 4, 0).reshape(2, OUT, LANES)
+    gains = jnp.broadcast_to(jnp.stack([gain_attn, gain_mlp])[None], (2, 2, LANES))
+    gains = jnp.concatenate([gains, jnp.zeros((2, EXTRA - 2, LANES), BF16)], axis=1)
+    first_pieces = jnp.concatenate([qk, val, gains], axis=1)
+    out_rows = lax.dynamic_index_in_dim(w_out.reshape(2, 4, OUT, LANES), place, 1, keepdims=False)
+    down_rows = lax.dynamic_index_in_dim(w_down.reshape(2, 4, UNITS, LANES), place, 1, keepdims=False)
+    in_rows = lax.dynamic_index_in_dim(w_in.T.reshape(2, 2, 4, UNITS, LANES), place, 2, keepdims=False)
+    fill = ((0, 0), (0, HIDDEN - UNITS), (0, 0))
+    rest_pieces = jnp.concatenate(
+        [out_rows, jnp.pad(in_rows[0], fill), jnp.pad(in_rows[1], fill), jnp.pad(down_rows, fill)], axis=1
+    )
+    qkv_own = spread_pieces(first_pieces, c)
+    rest_own = spread_pieces(rest_pieces, c)
+    gain_one = qkv_own[:, QKV, :].reshape(1, D).astype(F32)
+    gain_two = qkv_own[:, QKV + 1, :].reshape(1, D).astype(F32)
+
+    ids_row = jnp.pad(segment_ids.astype(BF16)[:, None, :], ((0, 0), (0, 7), (0, D - piece)))
+    first, second = to_sequence(jnp.concatenate([tokens, ids_row], axis=1), straight, x)
+    rows_in = jnp.concatenate([first[:piece], second[:piece]], axis=0).astype(F32)
+    own_ids = jnp.concatenate([first[piece : piece + 1, :piece], second[piece : piece + 1, :piece]], axis=1)
+    ids = jnp.concatenate([own_ids, swap(own_ids, "c")], axis=1).astype(F32)
+    dy_first, dy_second = to_sequence(grad_output, straight, x)
+    dy_own = jnp.concatenate([dy_first, dy_second], axis=0)
+    dy = jnp.concatenate([dy_own, swap(dy_own, "c")], axis=0)
+
+    order = jnp.stack([2 * c + x, 2 * c + 1 - x, 2 * (1 - c) + x, 2 * (1 - c) + 1 - x])
+    places = (order[:, None] * piece + jnp.arange(piece)[None, :]).reshape(-1)
+    begins = jnp.sum((ids < ids.reshape(-1, 1)).astype(F32), axis=1)
+    cosine, sine = rope_tables(places.astype(F32) - begins, HD)
+    cosine = jnp.concatenate([cosine] * 4, axis=1)
+    sine = jnp.concatenate([-sine, -sine, sine, sine], axis=1)
+    length = ids.shape[1]
+    ids_col = jnp.broadcast_to(ids.reshape(-1, 1), (length, LANES))
+    tables = (cosine, sine, jnp.broadcast_to(ids, (8, length)), ids_col)
+
+    normed_one, scale_one = moments(rows_in)
+    low_own = (normed_one * gain_one).astype(BF16)
+    low_one = jnp.concatenate([low_own, swap(low_own, "c")], axis=0)
+    qkv_parts = plane_gather(qkv_own)
+    rest_parts = plane_gather(rest_own)
+    saved = [attention(low_one, part, tables) for part in qkv_parts]
+    own, other = partial_rows([item[3] for item in saved], rest_parts)
+    hidden = rows_in + own + swap(other, "c").astype(F32)
+    normed_two, scale_two = moments(hidden)
+    low_own = (normed_two * gain_two).astype(BF16)
+    low_two = jnp.concatenate([low_own, swap(low_own, "c")], axis=0)
+
+    sums = None
+    rest_grads = []
+    for part in rest_parts:
+        sums, grads = mlp(low_two, dy, part, sums)
+        rest_grads.append(grads)
+    half = 2 * piece
+    result = hidden + sums[0][:half] + swap(sums[0][half:].astype(BF16), "c").astype(F32)
+    output = from_sequence(result.astype(BF16), straight, x)
+    dn_two = sums[1][:half] + swap(sums[1][half:].astype(BF16), "c").astype(F32)
+    pulled, gain_grad_two = norm_back(dn_two, gain_two, normed_two, scale_two)
+    grad_hidden = dy_own.astype(F32) + pulled
+    branch_own = grad_hidden.astype(BF16)
+    branch = jnp.concatenate([branch_own, swap(branch_own, "c")], axis=0)
+    rest_total = plane_reduce(rest_grads)
+    rest_owned = owned_gradient(jnp.concatenate(rest_total, axis=0), c)
+
+    mixed_grads, qkv_grads = [None] * 4, [None] * 4
+    for r in (3, 1, 2, 0):
+        mixed_grads[r], low, high = attention_back(saved[r], branch, low_one, rest_parts[r], tables)
+        qkv_grads[r] = (low, high)
+    own, other = partial_rows(mixed_grads, qkv_parts)
+    dn_one = own + swap(other, "c").astype(F32)
+    pulled, gain_grad_one = norm_back(dn_one, gain_one, normed_one, scale_one)
+    input_grad = from_sequence((grad_hidden + pulled).astype(BF16), straight, x)
+    gain_rows = jnp.stack([gain_grad_one, gain_grad_two]).reshape(2, -1, LANES).transpose(1, 0, 2)
+    gain_rows = jnp.pad(gain_rows, ((0, 0), (0, 6), (0, 0))).astype(BF16)
+    qkv_total = jnp.concatenate(plane_reduce(qkv_grads), axis=0)
+    qkv_owned = owned_gradient(jnp.concatenate([qkv_total, gain_rows], axis=1), c)
+
+    rest_all = in_order(rest_owned, x, y, c).astype(F32)
+    blocks = rest_all.reshape(4, 2, 3, HIDDEN, LANES)[:, :, :, :UNITS].transpose(2, 1, 0, 3, 4)
+    grad_in = blocks[0:2].reshape(2 * FF, LANES).T
+    grad_down = blocks[2].reshape(FF, LANES)
+    qkv_all = in_order(qkv_owned, x, y, c).astype(F32)
+    qk = qkv_all[:, :, : 2 * OUT].reshape(4, 2, 2, 2, PAIR, HALF, LANES).transpose(6, 1, 0, 4, 2, 3, 5)
+    val = qkv_all[:, :, 2 * OUT : QKV].reshape(4, 2, PAIR, 2, HALF, LANES).transpose(5, 1, 0, 2, 3, 4)
+    grad_qkv = jnp.concatenate([qk, val[:, :, :, :, None]], axis=4).reshape(LANES, 3 * HEADS * HD)
+    grad_out = qkv_all[:, :, QKV : QKV + OUT].transpose(1, 0, 2, 3).reshape(HEADS * HD, LANES)
+    gain_sums = jnp.sum(qkv_all[:, :, QKV + OUT : QKV + OUT + 2], axis=(0, 1))
+    return output, input_grad, grad_qkv, grad_out, grad_in, grad_down, gain_sums[0], gain_sums[1]
+
+
+def solution(mesh):
+    columns, pieces = mesh.shape["fsdp"], mesh.shape["seq"]
+    if pieces != 4 or columns * LANES != D:
+        return spread(mesh)
+    chips = Mesh(mesh.devices.reshape(columns // 2, 2, 2, 2), ("z", "c", "y", "x"))
+    batch, width, seq = ("z", "c"), ("z", "c"), ("y", "x")
+    return jax.shard_map(
+        chip_local,
+        mesh=chips,
+        in_specs=(
+            P(batch, seq, None),
+            P(batch, seq),
+            P(width, None),
+            P(None, width),
+            P(width, None),
+            P(None, width),
+            P(width),
+            P(width),
+            P(batch, seq, None),
+        ),
+        out_specs=(
+            P(batch, seq, None),
+            P(batch, seq, None),
+            P(width, None),
+            P(None, width),
+            P(width, None),
+            P(None, width),
+            P(width),
+            P(width),
+        ),
+        check_vma=False,
+    )

time: 882 us -> 565 us (0.64)
  matrix products: 202 us -> 0 us
  Pallas kernels: 0 us -> 148 us
  local copies, waits for them, and re-layouts: 183 us -> 53.1 us
  other arithmetic: 131 us -> 52 us
  waiting for transfers between devices: 242 us -> 209 us
  blocking collectives: 54.7 us -> 31.4 us
    dot_general x52 -> x0, matrix products: 202 us -> none  [the longest x8 51.9 us: contract_cols(): lax.dot_general(left, right, (((1,), (1,)), ((), ())), preferred_element_...]
    ppermute x0 -> x47, waiting for transfers between devices: none -> 188 us  [the longest x37 164 us: swap(): return lax.ppermute(value, axis, BOTH)]
    pallas_call x0 -> x14, Pallas kernels: none -> 148 us  [the longest x4 55.5 us: mlp(): pl.pallas_call(functools.partial(mlp_body, first), grid=(tokens // TILE,)...]
    reduce_scatter x2, waiting for transfers between devices: 139 us -> 0.02 us  [owned_gradient(): mine = lax.psum_scatter(total, 'z', scatter_dimension=0, tiled=True)]
    unnamed x14 -> x1, other arithmetic: 74 us -> 0.07 us
    psum x1 -> x0, waiting for transfers between devices: 49.2 us -> none  [local(): lax.psum(shards[0].astype(jnp.bfloat16), 'seq').astype(jnp.float32)]
    ppermute x0 -> x47, starting transfers between devices: none -> 47.6 us  [the longest x37 34 us: swap(): return lax.ppermute(value, axis, BOTH)]
    all_to_all x8 -> x0, starting transfers between devices: 46.3 us -> none  [the longest x2 20.2 us: local(): lax.all_to_all(stacked, 'seq', split_axis=2, concat_axis=1, tiled=True)]
  transfers between devices with their start and end apart: 17 -> 50, of which waited for: 5 -> 24; matrix products, arithmetic and copies ran while one was open for 49% -> 10% of each run, Pallas kernels for 0% -> 14%
where the time goes in v1:
time: 565 us; the launch traced here: 557 us
  waiting for transfers between devices  209 us (37%)
  Pallas kernels  148 us (26%)
  local copies, waits for them, and re-layouts  53.1 us (9%)
  other arithmetic  52 us (9%)
  starting transfers between devices  48 us (8%)
  blocking collectives  31.4 us (6%)
  between operations  15.6 us (3%)
    ppermute x37, waiting for transfers between devices, swap(): return lax.ppermute(value, axis, BOTH)  164 us
    pallas_call x4, Pallas kernels, mlp(): pl.pallas_call(functools.partial(mlp_body, first), grid=(tokens // TILE,)...  55.5 us
    pallas_call x4, Pallas kernels, attention_back(): pl.pallas_call(backward_body, grid=(1,), in_specs=[vmem] * 7 + [pl.BlockS...  49.4 us
    ppermute x37, starting transfers between devices, swap(): return lax.ppermute(value, axis, BOTH)  34 us
    pallas_call x4, Pallas kernels, attention(): pl.pallas_call(forward_body, in_specs=whole_in_vmem(6), out_specs=whole_i...  32.8 us
    all_gather x1, blocking collectives, spread_pieces(): return lax.all_gather(both, 'z', axis=0, tiled=True)  31.4 us
    unnamed x151, local copies, waits for them, and re-layouts  30 us
    all_gather x1, waiting for transfers between devices, spread_pieces(): return lax.all_gather(both, 'z', axis=0, tiled=True)  21.3 us
  transfers between devices with their start and end apart: 50, of which 24 were waited for; matrix products, arithmetic and copies ran while one was open for 10% of the time, Pallas kernels for 14%

profile of v1, /device:TPU:0, one launch (start us, length us, event | category | flops | bytes accessed | tf_op | source)
XLA Modules:
  0.0 557.0 jit_solution(10683991175706770733)
XLA Ops:
  7.2 2.1 copy.112
  15.3 2.8 collective-permute-start
  20.3 1.8 collective-permute-start.2
  23.1 31.4 %all_gather.6.w_ref.refs_4_ = bf16[8,400,128]{2,1,0:T(8,128)(2,1)} all-gather(bf16[2,400,128]{2,1,0:T(8,128)(2,1)S(1)} %maximum_select_fusion.3), channel_id=1, replica_groups=mesh['z'=4,'c'=2,'y'=2,'x'=2] {'z'}, dimensions={0}, use_global_device_ids=true | all-gather | bytes 1024000 | tf_op jit(solution)/shard_map/all_gather | solution.py:753
  54.6 1.7 collective-permute-start.6
  57.6 21.3 %all-gather.2.cloned.1.call-done.refs_4_.w_ref = bf16[8,1136,128]{2,1,0:T(8,128)(2,1)} async-done(((bf16[2,1136,128]{2,1,0:T(8,128)(2,1)}), bf16[8,1136,128]{2,1,0:T(8,128)(2,1)}) %all-gather.2.cloned.1.call-update) | async-done | bytes 2326544 | tf_op jit(solution)/shard_map/all_gather | solution.py:753
  90.0 1.9 fusion.28
  92.4 40.2 %collective-permute-done.11.refs_6_.w_ref = bf16[8,1136,128]{2,1,0:T(8,128)(2,1)} collective-permute-done((bf16[8,1136,128]{2,1,0:T(8,128)(2,1)}, bf16[8,1136,128]{2,1,0:T(8,128)(2,1)}, u32[]{:S(2)}, u32[]{:S(2)}) %collective-permute-start.11) | collective-permute-done | bytes 2326560 | tf_op jit(solution)/shard_map/ppermute | solution.py:658
  135.9 6.9 %collective-permute-done.7 = bf16[4,400,128]{2,1,0:T(8,128)(2,1)S(1)} collective-permute-done((bf16[4,400,128]{2,1,0:T(8,128)(2,1)S(1)}, bf16[4,400,128]{2,1,0:T(8,128)(2,1)S(1)}, u32[]{:S(2)}, u32[]{:S(2)}) %collective-permute-start.7) | collective-permute-done | bytes 409632 | tf_op jit(solution)/shard_map/ppermute | solution.py:658
  143.6 2.0 pad_maximum_fusion.n_ref
  145.9 8.6 %attention.4 = (bf16[1024,128]{1,0:T(8,128)(2,1)S(1)}, bf16[1024,128]{1,0:T(8,128)(2,1)S(1)}, bf16[1024,128]{1,0:T(8,128)(2,1)S(1)}, bf16[1024,128]{1,0:T(8,128)(2,1)S(1)}, f32[8,1024]{1,0:T(8,128)S(1)}) custom-call(bf16[1024,1024]{1,0:T(8,128)(2,1)S(1)} %pad_maximum_fusion.n_ref, bf16[8,400,128]{2,1,0:T(8,128)(2,1)} %all_gather.6.w_ref.refs_4_, ...), custom_call_target="tpu_custom_call" | custom-call | flops 1879048192 | bytes 6291456 | tf_op jit(solution)/shard_map/attention/pallas_call | solution.py:517
  156.6 7.3 %attention.7 = (bf16[1024,128]{1,0:T(8,128)(2,1)S(1)}, bf16[1024,128]{1,0:T(8,128)(2,1)S(1)}, bf16[1024,128]{1,0:T(8,128)(2,1)S(1)}, bf16[1024,128]{1,0:T(8,128)(2,1)S(1)}, f32[8,1024]{1,0:T(8,128)S(1)}) custom-call(bf16[1024,1024]{1,0:T(8,128)(2,1)S(1)} %pad_maximum_fusion.n_ref, bf16[8,400,128]{2,1,0:T(8,128)(2,1)S(1)} %constant_dynamic-update-slice_fusion.w_ref.refs_7_, ...), custom_call_target="tpu_custom_call" | custom-call | flops 1879048192 | bytes 6291456 | tf_op jit(solution)/shard_map/attention/pallas_call | solution.py:517
  166.0 8.4 %attention.6 = (bf16[1024,128]{1,0:T(8,128)(2,1)S(1)}, bf16[1024,128]{1,0:T(8,128)(2,1)S(1)}, bf16[1024,128]{1,0:T(8,128)(2,1)S(1)}, bf16[1024,128]{1,0:T(8,128)(2,1)S(1)}, f32[8,1024]{1,0:T(8,128)S(1)}) custom-call(bf16[1024,1024]{1,0:T(8,128)(2,1)S(1)} %pad_maximum_fusion.n_ref, bf16[8,400,128]{2,1,0:T(8,128)(2,1)} %collective-permute-done.6.w_ref.refs_6_, ...), custom_call_target="tpu_custom_call" | custom-call | flops 1879048192 | bytes 6291456 | tf_op jit(solution)/shard_map/attention/pallas_call | solution.py:517
  176.6 8.4 %attention.5 = (bf16[1024,128]{1,0:T(8,128)(2,1)S(1)}, bf16[1024,128]{1,0:T(8,128)(2,1)S(1)}, bf16[1024,128]{1,0:T(8,128)(2,1)S(1)}, bf16[1024,128]{1,0:T(8,128)(2,1)S(1)}, f32[8,1024]{1,0:T(8,128)S(1)}) custom-call(bf16[1024,1024]{1,0:T(8,128)(2,1)S(1)} %pad_maximum_fusion.n_ref, bf16[8,400,128]{2,1,0:T(8,128)(2,1)} %collective-permute-done.5.w_ref.refs_5_, ...), custom_call_target="tpu_custom_call" | custom-call | flops 1879048192 | bytes 6291456 | tf_op jit(solution)/shard_map/attention/pallas_call | solution.py:517
  187.0 3.4 partial_rows.2
  192.9 9.5 %collective-permute-done.16 = bf16[256,1024]{1,0:T(8,128)(2,1)S(1)} collective-permute-done((bf16[256,1024]{1,0:T(8,128)(2,1)S(1)}, bf16[256,1024]{1,0:T(8,128)(2,1)S(1)}, u32[]{:S(2)}, u32[]{:S(2)}) %collective-permute-start.16) | collective-permute-done | bytes 524320 | tf_op jit(solution)/shard_map/ppermute | solution.py:680
  202.6 3.4 collective-permute-start.18
  208.4 1.9 collective-permute-done.15
  210.5 12.3 %mlp.4 = (f32[1024,1024]{1,0:T(8,128)S(1)}, f32[1024,1024]{1,0:T(8,128)}, bf16[4,1008,128]{2,1,0:T(8,128)(2,1)S(1)}, bf16[4,1008,128]{2,1,0:T(8,128)(2,1)S(1)}) custom-call(bf16[1024,1024]{1,0:T(8,128)(2,1)S(1)} %pad_maximum_fusion.1.n_ref, bf16[1024,1024]{1,0:T(8,128)(2,1)S(1)} %pad_maximum_fusion.2.dy_ref, bf16[8,1136,128]{2,1,0:T(8,128)(2,1)S(1)} %copy-done.2), custom_call_target="tpu_custom_call" | custom-call | flops 6341787648 | bytes 25100288 | tf_op jit(solution)/shard_map/mlp/pallas_call | solution.py:450
  224.8 1.6 copy-done.4
  226.4 14.0 %mlp.5 = (f32[1024,1024]{1,0:T(8,128)S(1)}, f32[1024,1024]{1,0:T(8,128)}, bf16[4,1008,128]{2,1,0:T(8,128)(2,1)}, bf16[4,1008,128]{2,1,0:T(8,128)(2,1)S(1)}) custom-call(bf16[1024,1024]{1,0:T(8,128)(2,1)S(1)} %pad_maximum_fusion.1.n_ref, bf16[1024,1024]{1,0:T(8,128)(2,1)S(1)} %copy-done.4, ...), custom_call_target="tpu_custom_call", output_to_operand_aliasing={{0}: (3, {}), {1}: (4, {})} | custom-call | flops 6341787648 | bytes 25100288 | tf_op jit(solution)/shard_map/mlp/pallas_call | solution.py:450
  244.5 14.4 %mlp.6 = (f32[1024,1024]{1,0:T(8,128)S(1)}, f32[1024,1024]{1,0:T(8,128)}, bf16[4,1008,128]{2,1,0:T(8,128)(2,1)S(1)}, bf16[4,1008,128]{2,1,0:T(8,128)(2,1)S(1)}) custom-call(bf16[1024,1024]{1,0:T(8,128)(2,1)S(1)} %copy-done.8, bf16[1024,1024]{1,0:T(8,128)(2,1)S(1)} %copy-done.5, ...), custom_call_target="tpu_custom_call", output_to_operand_aliasing={{0}: (3, {}), {1}: (4, {})} | custom-call | flops 6341787648 | bytes 25100288 | tf_op jit(solution)/shard_map/mlp/pallas_call | solution.py:450
  259.0 2.3 copy-done.6
  261.3 1.6 copy-done.9
  262.9 14.8 %mlp.7 = (f32[1024,1024]{1,0:T(8,128)S(1)}, f32[1024,1024]{1,0:T(8,128)}, bf16[4,1008,128]{2,1,0:T(8,128)(2,1)}, bf16[4,1008,128]{2,1,0:T(8,128)(2,1)}) custom-call(bf16[1024,1024]{1,0:T(8,128)(2,1)S(1)} %copy-done.9, bf16[1024,1024]{1,0:T(8,128)(2,1)S(1)} %copy-done.6, ...), custom_call_target="tpu_custom_call", output_to_operand_aliasing={{0}: (3, {}), {1}: (4, {})} | custom-call | flops 6341787648 | bytes 25100288 | tf_op jit(solution)/shard_map/mlp/pallas_call | solution.py:450
  277.8 1.9 slice.233
  280.5 1.9 collective-permute-done.22
  282.4 2.5 multiply_reduce_fusion
  284.9 2.9 fusion.31
  288.0 2.5 collective-permute-done.23
  290.8 12.2 %attention_back.7 = (bf16[1024,384]{1,0:T(8,128)(2,1)S(1)}, bf16[4,512,128]{2,1,0:T(8,128)(2,1)S(1)}, bf16[4,512,128]{2,1,0:T(8,128)(2,1)S(1)}) custom-call(bf16[1024,128]{1,0:T(8,128)(2,1)S(1)} %copy-done.38, bf16[1024,128]{1,0:T(8,128)(2,1)S(1)} %copy-done.40, bf16[1024,128]{1,0:T(8,128)(2,1)S(1)} %copy-done.42, ...), custom_call_target="tpu_custom_call" | custom-call | flops 4026531840 | bytes 10485760 | tf_op jit(solution)/shard_map/attention_back/pallas_call | solution.py:587
  304.5 13.1 %attention_back.6 = (bf16[1024,384]{1,0:T(8,128)(2,1)S(1)}, bf16[4,512,128]{2,1,0:T(8,128)(2,1)S(1)}, bf16[4,512,128]{2,1,0:T(8,128)(2,1)S(1)}) custom-call(bf16[1024,128]{1,0:T(8,128)(2,1)S(1)} %copy-done.32, bf16[1024,128]{1,0:T(8,128)(2,1)S(1)} %copy-done.34, bf16[1024,128]{1,0:T(8,128)(2,1)S(1)} %copy-done.36, ...), custom_call_target="tpu_custom_call" | custom-call | flops 4026531840 | bytes 10485760 | tf_op jit(solution)/shard_map/attention_back/pallas_call | solution.py:587
  317.7 12.2 %attention_back.5 = (bf16[1024,384]{1,0:T(8,128)(2,1)S(1)}, bf16[4,512,128]{2,1,0:T(8,128)(2,1)S(1)}, bf16[4,512,128]{2,1,0:T(8,128)(2,1)S(1)}) custom-call(bf16[1024,128]{1,0:T(8,128)(2,1)S(1)} %copy-done.26, bf16[1024,128]{1,0:T(8,128)(2,1)S(1)} %copy-done.28, bf16[1024,128]{1,0:T(8,128)(2,1)S(1)} %copy-done.30, ...), custom_call_target="tpu_custom_call" | custom-call | flops 4026531840 | bytes 10485760 | tf_op jit(solution)/shard_map/attention_back/pallas_call | solution.py:587
  329.9 12.0 %attention_back.4 = (bf16[1024,384]{1,0:T(8,128)(2,1)S(1)}, bf16[4,512,128]{2,1,0:T(8,128)(2,1)S(1)}, bf16[4,512,128]{2,1,0:T(8,128)(2,1)S(1)}) custom-call(bf16[1024,128]{1,0:T(8,128)(2,1)S(1)} %copy-done.20, bf16[1024,128]{1,0:T(8,128)(2,1)S(1)} %copy-done.22, bf16[1024,128]{1,0:T(8,128)(2,1)S(1)} %copy-done.24, ...), custom_call_target="tpu_custom_call" | custom-call | flops 4026531840 | bytes 10485760 | tf_op jit(solution)/shard_map/attention_back/pallas_call | solution.py:587
  341.9 6.7 %partial_rows.3 = (f32[512,1024]{1,0:T(8,128)S(1)}, bf16[512,1024]{1,0:T(8,128)(2,1)S(1)}) custom-call(bf16[1024,384]{1,0:T(8,128)(2,1)S(1)} %get-tuple-element.78.refs_0_, bf16[1024,384]{1,0:T(8,128)(2,1)S(1)} %get-tuple-element.83.refs_1_, bf16[1024,384]{1,0:T(8,128)(2,1)S(1)} %get-tuple-element.88.refs_2_, ...), custom_call_target="tpu_custom_call" | custom-call | flops 3221225472 | bytes 8388608 | tf_op jit(solution)/shard_map/partial_rows/pallas_call | solution.py:635
  353.0 10.5 %collective-permute-done.31 = bf16[4,512,128]{2,1,0:T(8,128)(2,1)S(1)} collective-permute-done((bf16[4,512,128]{2,1,0:T(8,128)(2,1)S(1)}, bf16[4,512,128]{2,1,0:T(8,128)(2,1)S(1)}, u32[]{:S(2)}, u32[]{:S(2)}) %collective-permute-start.31) | collective-permute-done | bytes 524320 | tf_op jit(solution)/shard_map/ppermute | solution.py:658
  366.7 20.6 %collective-permute-done.27 = bf16[4,512,128]{2,1,0:T(8,128)(2,1)S(1)} collective-permute-done((bf16[4,512,128]{2,1,0:T(8,128)(2,1)S(1)}, bf16[4,512,128]{2,1,0:T(8,128)(2,1)S(1)}, u32[]{:S(2)}, u32[]{:S(2)}) %collective-permute-start.27) | collective-permute-done | bytes 524320 | tf_op jit(solution)/shard_map/ppermute | solution.py:658
  388.8 9.7 %collective-permute-done.32 = bf16[4,512,128]{2,1,0:T(8,128)(2,1)S(1)} collective-permute-done((bf16[4,512,128]{2,1,0:T(8,128)(2,1)S(1)}, bf16[4,512,128]{2,1,0:T(8,128)(2,1)S(1)}, u32[]{:S(2)}, u32[]{:S(2)}) %collective-permute-start.32) | collective-permute-done | bytes 524320 | tf_op jit(solution)/shard_map/ppermute | solution.py:658
  400.1 1.8 add_convert_fusion.5
  404.0 9.3 %collective-permute-done.41 = bf16[4,1008,128]{2,1,0:T(8,128)(2,1)} collective-permute-done((bf16[4,1008,128]{2,1,0:T(8,128)(2,1)}, bf16[4,1008,128]{2,1,0:T(8,128)(2,1)}, u32[]{:S(2)}, u32[]{:S(2)}) %collective-permute-start.41) | collective-permute-done | bytes 1032224 | tf_op jit(solution)/shard_map/ppermute | solution.py:658
  413.3 1.8 add_convert_fusion.2
  415.8 4.9 collective-permute-done.37
  420.7 14.6 %collective-permute-done.39 = bf16[4,1008,128]{2,1,0:T(8,128)(2,1)S(1)} collective-permute-done((bf16[4,1008,128]{2,1,0:T(8,128)(2,1)S(1)}, bf16[4,1008,128]{2,1,0:T(8,128)(2,1)S(1)}, u32[]{:S(2)}, u32[]{:S(2)}) %collective-permute-start.39) | collective-permute-done | bytes 1032224 | tf_op jit(solution)/shard_map/ppermute | solution.py:658
  435.3 1.7 add_convert_fusion.4
  437.0 18.0 %collective-permute-done.40 = bf16[4,1008,128]{2,1,0:T(8,128)(2,1)S(1)} collective-permute-done((bf16[4,1008,128]{2,1,0:T(8,128)(2,1)}, bf16[4,1008,128]{2,1,0:T(8,128)(2,1)S(1)}, u32[]{:S(2)}, u32[]{:S(2)}) %collective-permute-start.40) | collective-permute-done | bytes 1032224 | tf_op jit(solution)/shard_map/ppermute | solution.py:658
  459.0 2.7 fusion.13
  463.1 4.5 collective-permute-done.20
  469.2 4.4 collective-permute-done.25
  473.6 2.1 select_bitcast_fusion.2
  478.2 2.1 collective-permute-start.33
  481.7 1.9 collective-permute-start.35
  486.2 4.6 collective-permute-done.34
  492.4 5.0 collective-permute-done.36
  499.5 2.0 gather_fusion.1
  503.8 1.8 fusion.23
  512.4 3.0 copy.121
  515.4 1.9 copy.119
  517.8 3.5 collective-permute-done.44
  521.3 11.1 %collective-permute-done.45 = bf16[2,1008,128]{2,1,0:T(8,128)(2,1)} collective-permute-done((bf16[2,1008,128]{2,1,0:T(8,128)(2,1)}, bf16[2,1008,128]{2,1,0:T(8,128)(2,1)}, u32[]{:S(2)}, u32[]{:S(2)}) %collective-permute-start.45) | collective-permute-done | bytes 516128 | tf_op jit(solution)/shard_map/ppermute | solution.py:658
  532.4 2.8 pad_maximum_fusion.5
  535.2 2.5 gather_fusion.2
  537.7 2.8 broadcast_select_fusion
  540.5 3.7 gather_fusion.3
  547.8 2.2 copy.122
  (329 shorter events, 92.2 us)
Async XLA Ops:
  7.2 71.7 %all-gather.2.cloned.1.call-start = ((), (), s32[]{:S(2)}) async-start(), calls=%async_computation.2 | async-start | bytes 2908160 | tf_op jit(solution)/shard_map/all_gather | solution.py:753
  10.5 1.7 collective-permute-start.9
  13.2 464.0 %reduce-scatter.3.cloned.1.call-start = ((), (), s32[]{:S(2)}) async-start(), calls=%async_computation.3 | async-start | bytes 1331200 | tf_op jit(solution)/shard_map/reduce_scatter | solution.py:740
  15.3 65.1 %collective-permute-start = (bf16[264,1024]{1,0:T(8,128)(2,1)S(1)}, bf16[264,1024]{1,0:T(8,128)(2,1)S(1)}, u32[]{:S(2)}, u32[]{:S(2)}) collective-permute-start(bf16[264,1024]{1,0:T(8,128)(2,1)S(1)} %get-tuple-element.172), channel_id=1, source_target_pairs={{0,1},{1,0},{2,4},{3,5},{4,2},{5,3},{6,7},{7,6},{8,9},{9,8},{10,12... | collective-permute-start | bytes 1622024 | tf_op jit(solution)/shard_map/ppermute | solution.py:680
  18.1 63.7 %collective-permute-start.1 = (bf16[264,1024]{1,0:T(8,128)(2,1)}, bf16[264,1024]{1,0:T(8,128)(2,1)}, u32[]{:S(2)}, u32[]{:S(2)}) collective-permute-start(bf16[264,1024]{1,0:T(8,128)(2,1)} %get-tuple-element.173), channel_id=1, source_target_pairs={{2,5},{3,4},{4,3},{5,2},{10,13},{11,12},{12,11},{13,10},{18,21},{1... | collective-permute-start | bytes 1622024 | tf_op jit(solution)/shard_map/ppermute | solution.py:681
  20.3 2.8 collective-permute-start.2
  54.6 32.0 %collective-permute-start.6 = (bf16[8,400,128]{2,1,0:T(8,128)(2,1)}, bf16[8,400,128]{2,1,0:T(8,128)(2,1)}, u32[]{:S(2)}, u32[]{:S(2)}) collective-permute-start(bf16[8,400,128]{2,1,0:T(8,128)(2,1)} %all_gather.6.w_ref.refs_4_), channel_id=1, source_target_pairs={{0,2},{2,0},{1,3},{3,1},{4,6},{6,4},{5,7},{7,5},{8,10},{10,8},{9,1... | collective-permute-start | bytes 2457608 | tf_op jit(solution)/shard_map/ppermute | solution.py:658
  56.2 32.0 %collective-permute-start.5 = (bf16[8,400,128]{2,1,0:T(8,128)(2,1)}, bf16[8,400,128]{2,1,0:T(8,128)(2,1)}, u32[]{:S(2)}, u32[]{:S(2)}) collective-permute-start(bf16[8,400,128]{2,1,0:T(8,128)(2,1)} %all_gather.6.w_ref.refs_4_), channel_id=1, source_target_pairs={{0,1},{1,0},{2,3},{3,2},{4,5},{5,4},{6,7},{7,6},{8,9},{9,8},{10,11... | collective-permute-start | bytes 2457608 | tf_op jit(solution)/shard_map/ppermute | solution.py:658
  78.9 53.8 %collective-permute-start.11 = (bf16[8,1136,128]{2,1,0:T(8,128)(2,1)}, bf16[8,1136,128]{2,1,0:T(8,128)(2,1)}, u32[]{:S(2)}, u32[]{:S(2)}) collective-permute-start(bf16[8,1136,128]{2,1,0:T(8,128)(2,1)} %all-gather.2.cloned.1.call-done.refs_4_.w_ref), channel_id=1, source_target_pairs={{0,2},{2,0},{1,3},{3,1},{4,6},{6,4},{5,7},{7,5},{8,10},{10,8},{9,1... | collective-permute-start | bytes 6979592 | tf_op jit(solution)/shard_map/ppermute | solution.py:658
  80.3 62.5 %collective-permute-start.10 = (bf16[8,1136,128]{2,1,0:T(8,128)(2,1)}, bf16[8,1136,128]{2,1,0:T(8,128)(2,1)S(1)}, u32[]{:S(2)}, u32[]{:S(2)}) collective-permute-start(bf16[8,1136,128]{2,1,0:T(8,128)(2,1)} %all-gather.2.cloned.1.call-done.refs_4_.w_ref), channel_id=1, source_target_pairs={{0,1},{1,0},{2,3},{3,2},{4,5},{5,4},{6,7},{7,6},{8,9},{9,8},{10,11... | collective-permute-start | bytes 6979592 | tf_op jit(solution)/shard_map/ppermute | solution.py:658
  83.3 2.1 collective-permute-start.4
  85.4 58.2 %collective-permute-start.3 = (bf16[512,1024]{1,0:T(8,128)(2,1)}, bf16[512,1024]{1,0:T(8,128)(2,1)}, u32[]{:S(2)}, u32[]{:S(2)}) collective-permute-start(bf16[512,1024]{1,0:T(8,128)(2,1)} %fusion.8), channel_id=1, source_target_pairs={{0,4},{4,0},{1,5},{5,1},{2,6},{6,2},{3,7},{7,3},{8,12},{12,8},{9,1... | collective-permute-start | bytes 3145736 | tf_op jit(solution)/shard_map/ppermute | solution.py:658
  87.6 55.2 %collective-permute-start.7 = (bf16[4,400,128]{2,1,0:T(8,128)(2,1)S(1)}, bf16[4,400,128]{2,1,0:T(8,128)(2,1)S(1)}, u32[]{:S(2)}, u32[]{:S(2)}) collective-permute-start(bf16[4,400,128]{2,1,0:T(8,128)(2,1)S(1)} %slice.162), channel_id=1, source_target_pairs={{0,1},{1,0},{2,3},{3,2},{4,5},{5,4},{6,7},{7,6},{8,9},{9,8},{10,11... | collective-permute-start | bytes 1228808 | tf_op jit(solution)/shard_map/ppermute | solution.py:658
  89.3 54.3 %collective-permute-start.8 = (bf16[4,400,128]{2,1,0:T(8,128)(2,1)S(1)}, bf16[4,400,128]{2,1,0:T(8,128)(2,1)S(1)}, u32[]{:S(2)}, u32[]{:S(2)}) collective-permute-start(bf16[4,400,128]{2,1,0:T(8,128)(2,1)S(1)} %slice.163), channel_id=1, source_target_pairs={{0,2},{2,0},{1,3},{3,1},{4,6},{6,4},{5,7},{7,5},{8,10},{10,8},{9,1... | collective-permute-start | bytes 1228808 | tf_op jit(solution)/shard_map/ppermute | solution.py:658
  134.0 51.1 %collective-permute-start.12 = (bf16[4,1136,128]{2,1,0:T(8,128)(2,1)S(1)}, bf16[4,1136,128]{2,1,0:T(8,128)(2,1)S(1)}, u32[]{:S(2)}, u32[]{:S(2)}) collective-permute-start(bf16[4,1136,128]{2,1,0:T(8,128)(2,1)S(1)} %slice.165), channel_id=1, source_target_pairs={{0,1},{1,0},{2,3},{3,2},{4,5},{5,4},{6,7},{7,6},{8,9},{9,8},{10,11... | collective-permute-start | bytes 3489800 | tf_op jit(solution)/shard_map/ppermute | solution.py:658
  142.9 42.3 %collective-permute-start.13 = (bf16[4,1136,128]{2,1,0:T(8,128)(2,1)S(1)}, bf16[4,1136,128]{2,1,0:T(8,128)(2,1)S(1)}, u32[]{:S(2)}, u32[]{:S(2)}) collective-permute-start(bf16[4,1136,128]{2,1,0:T(8,128)(2,1)S(1)} %slice.166), channel_id=1, source_target_pairs={{0,2},{2,0},{1,3},{3,1},{4,6},{6,4},{5,7},{7,5},{8,10},{10,8},{9,1... | collective-permute-start | bytes 3489800 | tf_op jit(solution)/shard_map/ppermute | solution.py:658
  190.4 15.6 %collective-permute-start.14 = (bf16[512,1024]{1,0:T(8,128)(2,1)S(1)}, bf16[512,1024]{1,0:T(8,128)(2,1)S(1)}, u32[]{:S(2)}, u32[]{:S(2)}) collective-permute-start(bf16[512,1024]{1,0:T(8,128)(2,1)S(1)} %get-tuple-element.65), channel_id=1, source_target_pairs={{0,4},{4,0},{1,5},{5,1},{2,6},{6,2},{3,7},{7,3},{8,12},{12,8},{9,1... | collective-permute-start | bytes 3145736 | tf_op jit(solution)/shard_map/ppermute | solution.py:658
  190.6 11.8 %collective-permute-start.16 = (bf16[256,1024]{1,0:T(8,128)(2,1)S(1)}, bf16[256,1024]{1,0:T(8,128)(2,1)S(1)}, u32[]{:S(2)}, u32[]{:S(2)}) collective-permute-start(bf16[256,1024]{1,0:T(8,128)(2,1)S(1)} %get-tuple-element.168), channel_id=1, source_target_pairs={{0,1},{1,0},{2,4},{3,5},{4,2},{5,3},{6,7},{7,6},{8,9},{9,8},{10,12... | collective-permute-start | bytes 1572872 | tf_op jit(solution)/shard_map/ppermute | solution.py:680
  192.1 13.9 %copy-start.46 = (bf16[256,1024]{1,0:T(8,128)(2,1)S(1)}, bf16[256,1024]{1,0:T(8,128)(2,1)}, u32[]{:S(2)}) copy-start(bf16[256,1024]{1,0:T(8,128)(2,1)} %copy-done.45) | copy-start | bytes 1572868
  192.1 13.9 %copy-start.49 = (bf16[256,1024]{1,0:T(8,128)(2,1)S(1)}, bf16[256,1024]{1,0:T(8,128)(2,1)}, u32[]{:S(2)}) copy-start(bf16[256,1024]{1,0:T(8,128)(2,1)} %copy-done.48) | copy-start | bytes 1572868
  192.1 10.3 %collective-permute-start.17 = (bf16[256,1024]{1,0:T(8,128)(2,1)S(1)}, bf16[256,1024]{1,0:T(8,128)(2,1)S(1)}, u32[]{:S(2)}, u32[]{:S(2)}) collective-permute-start(bf16[256,1024]{1,0:T(8,128)(2,1)S(1)} %get-tuple-element.169), channel_id=1, source_target_pairs={{2,5},{3,4},{4,3},{5,2},{10,13},{11,12},{12,11},{13,10},{18,21},{1... | collective-permute-start | bytes 1572872 | tf_op jit(solution)/shard_map/ppermute | solution.py:681
  202.6 5.6 %collective-permute-start.18 = (bf16[512,1024]{1,0:T(8,128)(2,1)S(1)}, bf16[512,1024]{1,0:T(8,128)(2,1)S(1)}, u32[]{:S(2)}, u32[]{:S(2)}) collective-permute-start(bf16[512,1024]{1,0:T(8,128)(2,1)S(1)} %pad_maximum_fusion.9), channel_id=1, source_target_pairs={{0,4},{4,0},{1,5},{5,1},{2,6},{6,2},{3,7},{7,3},{8,12},{12,8},{9,1... | collective-permute-start | bytes 3145736 | tf_op jit(solution)/shard_map/ppermute | solution.py:658
  207.7 2.7 collective-permute-start.15
  208.4 14.4 %copy-start.3 = (bf16[1024,1024]{1,0:T(8,128)(2,1)}, bf16[1024,1024]{1,0:T(8,128)(2,1)S(1)}, u32[]{:S(2)}) copy-start(bf16[1024,1024]{1,0:T(8,128)(2,1)S(1)} %pad_maximum_fusion.2.dy_ref) | copy-start | bytes 6291460
  210.5 14.3 %copy-start.7 = (bf16[1024,1024]{1,0:T(8,128)(2,1)}, bf16[1024,1024]{1,0:T(8,128)(2,1)S(1)}, u32[]{:S(2)}) copy-start(bf16[1024,1024]{1,0:T(8,128)(2,1)S(1)} %pad_maximum_fusion.1.n_ref) | copy-start | bytes 6291460
  259.0 18.8 %copy-start.11 = (bf16[4,1008,128]{2,1,0:T(8,128)(2,1)}, bf16[4,1008,128]{2,1,0:T(8,128)(2,1)S(1)}, u32[]{:S(2)}) copy-start(bf16[4,1008,128]{2,1,0:T(8,128)(2,1)S(1)} %get-tuple-element.106) | copy-start | bytes 3096580
  259.0 18.8 %copy-start.18 = (bf16[4,1008,128]{2,1,0:T(8,128)(2,1)}, bf16[4,1008,128]{2,1,0:T(8,128)(2,1)S(1)}, u32[]{:S(2)}) copy-start(bf16[4,1008,128]{2,1,0:T(8,128)(2,1)S(1)} %get-tuple-element.109) | copy-start | bytes 3096580
  279.7 2.7 collective-permute-start.22
  280.1 4.8 collective-permute-start.19
  287.8 2.7 collective-permute-start.23
  290.8 13.7 %copy-start.32 = (bf16[1024,128]{1,0:T(8,128)(2,1)S(1)}, bf16[1024,128]{1,0:T(8,128)(2,1)}, u32[]{:S(2)}) copy-start(bf16[1024,128]{1,0:T(8,128)(2,1)} %copy-done.31) | copy-start | bytes 786436
  290.8 13.7 %copy-start.34 = (bf16[1024,128]{1,0:T(8,128)(2,1)S(1)}, bf16[1024,128]{1,0:T(8,128)(2,1)}, u32[]{:S(2)}) copy-start(bf16[1024,128]{1,0:T(8,128)(2,1)} %copy-done.33) | copy-start | bytes 786436
  290.8 13.7 %copy-start.36 = (bf16[1024,128]{1,0:T(8,128)(2,1)S(1)}, bf16[1024,128]{1,0:T(8,128)(2,1)}, u32[]{:S(2)}) copy-start(bf16[1024,128]{1,0:T(8,128)(2,1)} %copy-done.35) | copy-start | bytes 786436
  303.0 49.2 %collective-permute-start.28 = (bf16[4,512,128]{2,1,0:T(8,128)(2,1)S(1)}, bf16[4,512,128]{2,1,0:T(8,128)(2,1)S(1)}, u32[]{:S(2)}, u32[]{:S(2)}) collective-permute-start(bf16[4,512,128]{2,1,0:T(8,128)(2,1)S(1)} %get-tuple-element.99), channel_id=1, source_target_pairs={{0,1},{1,0},{2,3},{3,2},{4,5},{5,4},{6,7},{7,6},{8,9},{9,8},{10,11... | collective-permute-start | bytes 1572872 | tf_op jit(solution)/shard_map/ppermute | solution.py:658
  304.5 13.1 %copy-start.28 = (bf16[1024,128]{1,0:T(8,128)(2,1)S(1)}, bf16[1024,128]{1,0:T(8,128)(2,1)}, u32[]{:S(2)}) copy-start(bf16[1024,128]{1,0:T(8,128)(2,1)} %copy-done.27) | copy-start | bytes 786436
  348.6 17.1 %copy-start.47 = (bf16[256,1024]{1,0:T(8,128)(2,1)S(1)}, bf16[256,1024]{1,0:T(8,128)(2,1)}, u32[]{:S(2)}) copy-start(bf16[256,1024]{1,0:T(8,128)(2,1)} %copy-done.45) | copy-start | bytes 1572868
  348.7 17.0 %copy-start.50 = (bf16[256,1024]{1,0:T(8,128)(2,1)S(1)}, bf16[256,1024]{1,0:T(8,128)(2,1)}, u32[]{:S(2)}) copy-start(bf16[256,1024]{1,0:T(8,128)(2,1)} %copy-done.48) | copy-start | bytes 1572868
  348.7 16.3 %collective-permute-start.24 = (bf16[512,1024]{1,0:T(8,128)(2,1)S(1)}, bf16[512,1024]{1,0:T(8,128)(2,1)S(1)}, u32[]{:S(2)}, u32[]{:S(2)}) collective-permute-start(bf16[512,1024]{1,0:T(8,128)(2,1)S(1)} %get-tuple-element.95), channel_id=1, source_target_pairs={{0,4},{4,0},{1,5},{5,1},{2,6},{6,2},{3,7},{7,3},{8,12},{12,8},{9,1... | collective-permute-start | bytes 3145736 | tf_op jit(solution)/shard_map/ppermute | solution.py:658
  348.7 14.8 %collective-permute-start.31 = (bf16[4,512,128]{2,1,0:T(8,128)(2,1)S(1)}, bf16[4,512,128]{2,1,0:T(8,128)(2,1)S(1)}, u32[]{:S(2)}, u32[]{:S(2)}) collective-permute-start(bf16[4,512,128]{2,1,0:T(8,128)(2,1)S(1)} %get-tuple-element.103), channel_id=1, source_target_pairs={{0,2},{2,0},{1,3},{3,1},{4,6},{6,4},{5,7},{7,5},{8,10},{10,8},{9,1... | collective-permute-start | bytes 1572872 | tf_op jit(solution)/shard_map/ppermute | solution.py:658
  350.1 49.9 %collective-permute-start.38 = (bf16[4,1008,128]{2,1,0:T(8,128)(2,1)}, bf16[4,1008,128]{2,1,0:T(8,128)(2,1)}, u32[]{:S(2)}, u32[]{:S(2)}) collective-permute-start(bf16[4,1008,128]{2,1,0:T(8,128)(2,1)} %get-tuple-element.107), channel_id=1, source_target_pairs={{0,1},{1,0},{2,3},{3,2},{4,5},{5,4},{6,7},{7,6},{8,9},{9,8},{10,11... | collective-permute-start | bytes 3096584 | tf_op jit(solution)/shard_map/ppermute | solution.py:658
  350.7 36.5 %collective-permute-start.27 = (bf16[4,512,128]{2,1,0:T(8,128)(2,1)S(1)}, bf16[4,512,128]{2,1,0:T(8,128)(2,1)S(1)}, u32[]{:S(2)}, u32[]{:S(2)}) collective-permute-start(bf16[4,512,128]{2,1,0:T(8,128)(2,1)S(1)} %get-tuple-element.97), channel_id=1, source_target_pairs={{0,1},{1,0},{2,3},{3,2},{4,5},{5,4},{6,7},{7,6},{8,9},{9,8},{10,11... | collective-permute-start | bytes 1572872 | tf_op jit(solution)/shard_map/ppermute | solution.py:658
  352.2 36.6 %collective-permute-start.30 = (bf16[4,512,128]{2,1,0:T(8,128)(2,1)S(1)}, bf16[4,512,128]{2,1,0:T(8,128)(2,1)S(1)}, u32[]{:S(2)}, u32[]{:S(2)}) collective-permute-start(bf16[4,512,128]{2,1,0:T(8,128)(2,1)S(1)} %get-tuple-element.101), channel_id=1, source_target_pairs={{0,2},{2,0},{1,3},{3,1},{4,6},{6,4},{5,7},{7,5},{8,10},{10,8},{9,1... | collective-permute-start | bytes 1572872 | tf_op jit(solution)/shard_map/ppermute | solution.py:658
  363.5 24.4 %collective-permute-start.29 = (bf16[4,512,128]{2,1,0:T(8,128)(2,1)S(1)}, bf16[4,512,128]{2,1,0:T(8,128)(2,1)S(1)}, u32[]{:S(2)}, u32[]{:S(2)}) collective-permute-start(bf16[4,512,128]{2,1,0:T(8,128)(2,1)S(1)} %add_convert_fusion.11), channel_id=1, source_target_pairs={{0,2},{2,0},{1,3},{3,1},{4,6},{6,4},{5,7},{7,5},{8,10},{10,8},{9,1... | collective-permute-start | bytes 1572872 | tf_op jit(solution)/shard_map/ppermute | solution.py:658
  365.0 33.4 %collective-permute-start.32 = (bf16[4,512,128]{2,1,0:T(8,128)(2,1)S(1)}, bf16[4,512,128]{2,1,0:T(8,128)(2,1)S(1)}, u32[]{:S(2)}, u32[]{:S(2)}) collective-permute-start(bf16[4,512,128]{2,1,0:T(8,128)(2,1)S(1)} %add_convert_fusion.8), channel_id=1, source_target_pairs={{0,1},{1,0},{2,3},{3,2},{4,5},{5,4},{6,7},{7,6},{8,9},{9,8},{10,11... | collective-permute-start | bytes 1572872 | tf_op jit(solution)/shard_map/ppermute | solution.py:658
  387.2 26.1 %collective-permute-start.41 = (bf16[4,1008,128]{2,1,0:T(8,128)(2,1)}, bf16[4,1008,128]{2,1,0:T(8,128)(2,1)}, u32[]{:S(2)}, u32[]{:S(2)}) collective-permute-start(bf16[4,1008,128]{2,1,0:T(8,128)(2,1)} %get-tuple-element.111), channel_id=1, source_target_pairs={{0,2},{2,0},{1,3},{3,1},{4,6},{6,4},{5,7},{7,5},{8,10},{10,8},{9,1... | collective-permute-start | bytes 3096584 | tf_op jit(solution)/shard_map/ppermute | solution.py:658
  388.0 32.7 %collective-permute-start.37 = (bf16[4,1008,128]{2,1,0:T(8,128)(2,1)}, bf16[4,1008,128]{2,1,0:T(8,128)(2,1)}, u32[]{:S(2)}, u32[]{:S(2)}) collective-permute-start(bf16[4,1008,128]{2,1,0:T(8,128)(2,1)} %get-tuple-element.105), channel_id=1, source_target_pairs={{0,1},{1,0},{2,3},{3,2},{4,5},{5,4},{6,7},{7,6},{8,9},{9,8},{10,11... | collective-permute-start | bytes 3096584 | tf_op jit(solution)/shard_map/ppermute | solution.py:658
  399.8 102.9 %reduce-scatter.5.cloned.1.call-start = ((), (), s32[]{:S(2)}) async-start(), calls=%async_computation.4 | async-start | bytes 2580480 | tf_op jit(solution)/shard_map/reduce_scatter | solution.py:740
  401.9 33.4 %copy-start.15 = (bf16[4,1008,128]{2,1,0:T(8,128)(2,1)S(1)}, bf16[4,1008,128]{2,1,0:T(8,128)(2,1)}, u32[]{:S(2)}) copy-start(bf16[4,1008,128]{2,1,0:T(8,128)(2,1)} %copy-done.14) | copy-start | bytes 3096580
  401.9 33.4 %collective-permute-start.39 = (bf16[4,1008,128]{2,1,0:T(8,128)(2,1)S(1)}, bf16[4,1008,128]{2,1,0:T(8,128)(2,1)S(1)}, u32[]{:S(2)}, u32[]{:S(2)}) collective-permute-start(bf16[4,1008,128]{2,1,0:T(8,128)(2,1)S(1)} %add_convert_fusion.5), channel_id=1, source_target_pairs={{0,2},{2,0},{1,3},{3,1},{4,6},{6,4},{5,7},{7,5},{8,10},{10,8},{9,1... | collective-permute-start | bytes 3096584 | tf_op jit(solution)/shard_map/ppermute | solution.py:658
  402.6 52.3 %collective-permute-start.40 = (bf16[4,1008,128]{2,1,0:T(8,128)(2,1)}, bf16[4,1008,128]{2,1,0:T(8,128)(2,1)S(1)}, u32[]{:S(2)}, u32[]{:S(2)}) collective-permute-start(bf16[4,1008,128]{2,1,0:T(8,128)(2,1)} %copy-done.18), channel_id=1, source_target_pairs={{0,2},{2,0},{1,3},{3,1},{4,6},{6,4},{5,7},{7,5},{8,10},{10,8},{9,1... | collective-permute-start | bytes 3096584 | tf_op jit(solution)/shard_map/ppermute | solution.py:658
  415.1 39.9 %copy-start.13 = (bf16[4,1008,128]{2,1,0:T(8,128)(2,1)S(1)}, bf16[4,1008,128]{2,1,0:T(8,128)(2,1)}, u32[]{:S(2)}) copy-start(bf16[4,1008,128]{2,1,0:T(8,128)(2,1)} %copy-done.12) | copy-start | bytes 3096580
  415.1 39.9 %collective-permute-start.42 = (bf16[4,1008,128]{2,1,0:T(8,128)(2,1)S(1)}, bf16[4,1008,128]{2,1,0:T(8,128)(2,1)S(1)}, u32[]{:S(2)}, u32[]{:S(2)}) collective-permute-start(bf16[4,1008,128]{2,1,0:T(8,128)(2,1)S(1)} %add_convert_fusion.2), channel_id=1, source_target_pairs={{0,1},{1,0},{2,3},{3,2},{4,5},{5,4},{6,7},{7,6},{8,9},{9,8},{10,11... | collective-permute-start | bytes 3096584 | tf_op jit(solution)/shard_map/ppermute | solution.py:658
  458.4 9.2 %collective-permute-start.20 = (bf16[256,1024]{1,0:T(8,128)(2,1)S(1)}, bf16[256,1024]{1,0:T(8,128)(2,1)S(1)}, u32[]{:S(2)}, u32[]{:S(2)}) collective-permute-start(bf16[256,1024]{1,0:T(8,128)(2,1)S(1)} %broadcast_select_fusion.8), channel_id=1, source_target_pairs={{0,1},{1,0},{2,4},{3,5},{4,2},{5,3},{6,7},{7,6},{8,9},{9,8},{10,12... | collective-permute-start | bytes 1572872 | tf_op jit(solution)/shard_map/ppermute | solution.py:689
  461.8 11.7 %collective-permute-start.25 = (bf16[256,1024]{1,0:T(8,128)(2,1)S(1)}, bf16[256,1024]{1,0:T(8,128)(2,1)S(1)}, u32[]{:S(2)}, u32[]{:S(2)}) collective-permute-start(bf16[256,1024]{1,0:T(8,128)(2,1)S(1)} %broadcast_select_fusion.7), channel_id=1, source_target_pairs={{0,1},{1,0},{2,4},{3,5},{4,2},{5,3},{6,7},{7,6},{8,9},{9,8},{10,12... | collective-permute-start | bytes 1572872 | tf_op jit(solution)/shard_map/ppermute | solution.py:689
  468.4 8.7 %collective-permute-start.21 = (bf16[256,1024]{1,0:T(8,128)(2,1)S(1)}, bf16[256,1024]{1,0:T(8,128)(2,1)S(1)}, u32[]{:S(2)}, u32[]{:S(2)}) collective-permute-start(bf16[256,1024]{1,0:T(8,128)(2,1)S(1)} %get-tuple-element.180), channel_id=1, source_target_pairs={{2,5},{3,4},{4,3},{5,2},{10,13},{11,12},{12,11},{13,10},{18,21},{1... | collective-permute-start | bytes 1572872 | tf_op jit(solution)/shard_map/ppermute | solution.py:690
  475.7 9.3 %collective-permute-start.26 = (bf16[256,1024]{1,0:T(8,128)(2,1)}, bf16[256,1024]{1,0:T(8,128)(2,1)}, u32[]{:S(2)}, u32[]{:S(2)}) collective-permute-start(bf16[256,1024]{1,0:T(8,128)(2,1)} %get-tuple-element.178), channel_id=1, source_target_pairs={{2,5},{3,4},{4,3},{5,2},{10,13},{11,12},{12,11},{13,10},{18,21},{1... | collective-permute-start | bytes 1572872 | tf_op jit(solution)/shard_map/ppermute | solution.py:690
  478.2 3.2 collective-permute-start.33
  481.4 9.4 %collective-permute-start.34 = (bf16[2,520,128]{2,1,0:T(8,128)(2,1)S(1)}, bf16[2,520,128]{2,1,0:T(8,128)(2,1)S(1)}, u32[]{:S(2)}, u32[]{:S(2)}) collective-permute-start(bf16[2,520,128]{2,1,0:T(8,128)(2,1)S(1)} %get-tuple-element.198), channel_id=1, source_target_pairs={{0,1},{1,0},{2,3},{3,2},{4,5},{5,4},{6,7},{7,6},{8,9},{9,8},{10,11... | collective-permute-start | bytes 798728 | tf_op jit(solution)/shard_map/ppermute | solution.py:658
  481.7 10.7 %collective-permute-start.35 = (bf16[2,520,128]{2,1,0:T(8,128)(2,1)S(1)}, bf16[2,520,128]{2,1,0:T(8,128)(2,1)S(1)}, u32[]{:S(2)}, u32[]{:S(2)}) collective-permute-start(bf16[2,520,128]{2,1,0:T(8,128)(2,1)S(1)} %get-tuple-element.198), channel_id=1, source_target_pairs={{0,2},{2,0},{1,3},{3,1},{4,6},{6,4},{5,7},{7,5},{8,10},{10,8},{9,1... | collective-permute-start | bytes 798728 | tf_op jit(solution)/shard_map/ppermute | solution.py:658
  483.5 13.9 %collective-permute-start.36 = (bf16[2,520,128]{2,1,0:T(8,128)(2,1)S(1)}, bf16[2,520,128]{2,1,0:T(8,128)(2,1)S(1)}, u32[]{:S(2)}, u32[]{:S(2)}) collective-permute-start(bf16[2,520,128]{2,1,0:T(8,128)(2,1)S(1)} %get-tuple-element.198), channel_id=1, source_target_pairs={{0,3},{1,2},{2,1},{3,0},{4,7},{5,6},{6,5},{7,4},{8,11},{9,10},{10,... | collective-permute-start | bytes 798728 | tf_op jit(solution)/shard_map/ppermute | solution.py:744
  503.8 1.8 collective-permute-start.43
  506.5 14.8 %collective-permute-start.44 = (bf16[2,1008,128]{2,1,0:T(8,128)(2,1)}, bf16[2,1008,128]{2,1,0:T(8,128)(2,1)S(1)}, u32[]{:S(2)}, u32[]{:S(2)}) collective-permute-start(bf16[2,1008,128]{2,1,0:T(8,128)(2,1)} %get-tuple-element.194), channel_id=1, source_target_pairs={{0,1},{1,0},{2,3},{3,2},{4,5},{5,4},{6,7},{7,6},{8,9},{9,8},{10,11... | collective-permute-start | bytes 1548296 | tf_op jit(solution)/shard_map/ppermute | solution.py:658
  507.2 25.2 %collective-permute-start.45 = (bf16[2,1008,128]{2,1,0:T(8,128)(2,1)}, bf16[2,1008,128]{2,1,0:T(8,128)(2,1)}, u32[]{:S(2)}, u32[]{:S(2)}) collective-permute-start(bf16[2,1008,128]{2,1,0:T(8,128)(2,1)} %get-tuple-element.194), channel_id=1, source_target_pairs={{0,2},{2,0},{1,3},{3,1},{4,6},{6,4},{5,7},{7,5},{8,10},{10,8},{9,1... | collective-permute-start | bytes 1548296 | tf_op jit(solution)/shard_map/ppermute | solution.py:658
  508.5 23.9 %collective-permute-start.46 = (bf16[2,1008,128]{2,1,0:T(8,128)(2,1)}, bf16[2,1008,128]{2,1,0:T(8,128)(2,1)}, u32[]{:S(2)}, u32[]{:S(2)}) collective-permute-start(bf16[2,1008,128]{2,1,0:T(8,128)(2,1)} %get-tuple-element.194), channel_id=1, source_target_pairs={{0,3},{1,2},{2,1},{3,0},{4,7},{5,6},{6,5},{7,4},{8,11},{9,10},{10,... | collective-permute-start | bytes 1548296 | tf_op jit(solution)/shard_map/ppermute | solution.py:744
  (58 other events, 228.8 us)
Sparse Core Ops, SparseCore 0:
  13.3 65.4 all-gather.1
  399.9 24.7 reduce-scatter.2
  457.1 40.2 reduce-scatter.4

commit v2 on v1

--- a/solution.py
+++ b/solution.py
@@ -372,6 +372,7 @@
 UNITS = FF // 8
 HIDDEN = -(-UNITS // 16) * 16
 EXTRA = 16
+SPLIT = (160, HIDDEN - 160)
 TILE = 256
 BOTH = [(0, 1), (1, 0)]
 
@@ -382,6 +383,10 @@
 
 def whole_in_vmem(count):
     return [pl.BlockSpec(memory_space=pltpu.VMEM)] * count
+
+
+def after(value, *others):
+    return lax.optimization_barrier((value, others))[0]
 
 
 def lay_flat(flat_ref, blocks_ref, start, count, to=0):
@@ -389,7 +394,7 @@
         flat_ref[to : to + count, LANES * k : LANES * (k + 1)] = blocks_ref[k, start : start + count, :]
 
 
-def mlp_body(first, n_ref, dy_ref, w_ref, *rest):
+def mlp_body(first, n_ref, dy_ref, wa_ref, wb_ref, *rest):
     if first:
         y_ref, dn_ref, ga_ref, gb_ref, w_all, acc = rest
     else:
@@ -398,7 +403,9 @@
 
     @pl.when(step == 0)
     def _():
-        lay_flat(w_all, w_ref, OUT, 3 * HIDDEN)
+        for i in range(3):
+            lay_flat(w_all, wa_ref, i * SPLIT[0], SPLIT[0], i * HIDDEN)
+            lay_flat(w_all, wb_ref, i * SPLIT[1], SPLIT[1], i * HIDDEN + SPLIT[0])
 
     n_t = n_ref[...]
     dy_t = dy_ref[...]
@@ -442,7 +449,7 @@
 def mlp(n2, dy, weights, sums):
     first = sums is None
     tokens, width = n2.shape
-    blocks, rows, lanes = weights.shape
+    blocks, _, lanes = weights[0].shape
     row_tile = pl.BlockSpec((TILE, width), lambda t: (t, 0))
     half = pl.BlockSpec((blocks // 2, 3 * HIDDEN, lanes), lambda t: (0, 0, 0))
     total = jax.ShapeDtypeStruct((tokens, width), F32)
@@ -450,12 +457,13 @@
     y, dn, ga, gb = pl.pallas_call(
         functools.partial(mlp_body, first),
         grid=(tokens // TILE,),
-        in_specs=[row_tile, row_tile, pl.BlockSpec(weights.shape, lambda t: (0, 0, 0))]
+        in_specs=[row_tile, row_tile]
+        + [pl.BlockSpec(item.shape, lambda t: (0, 0, 0)) for item in weights]
         + ([] if first else [row_tile, row_tile]),
         out_specs=[row_tile, row_tile, half, half],
         out_shape=[total, total, grads, grads],
         scratch_shapes=[pltpu.VMEM((3 * HIDDEN, width), BF16), pltpu.VMEM((3 * HIDDEN, width), F32)],
-        input_output_aliases={} if first else {3: 0, 4: 1},
+        input_output_aliases={} if first else {4: 0, 5: 1},
         compiler_params=pltpu.CompilerParams(vmem_limit_bytes=40 * MIB),
         cost_estimate=pl.CostEstimate(
             flops=18 * tokens * HIDDEN * width,
@@ -463,7 +471,7 @@
             bytes_accessed=20 * tokens * width + 12 * HIDDEN * width,
         ),
         name="mlp",
-    )(*([n2, dy, weights] + ([] if first else list(sums))))
+    )(*([n2, dy, *weights] + ([] if first else list(sums))))
     return (y, dn), (ga, gb)
 
 
@@ -704,53 +712,107 @@
     scaled = grad * gain
     pulled = scaled - jnp.mean(scaled, axis=-1, keepdims=True)
     pulled = pulled - normed * jnp.mean(scaled * normed, axis=-1, keepdims=True)
-    return pulled * scale, jnp.sum(grad * normed, axis=0)
-
-
-def plane_gather(own):
-    half = own.shape[0] // 2
-    across = swap(own, "x")
-    along = swap(own, "y")
-    corner = jnp.concatenate([swap(along[:half], "x"), swap(across[half:], "y")], axis=0)
-    return [own, across, along, corner]
+    return pulled * scale
+
+
+def corner_half(value, part, axis):
+    half = value.shape[0] // 2
+    return swap(value[part * half : (part + 1) * half], axis)
+
+
+def swap_corner(value):
+    return lax.ppermute(value, ("y", "x"), [(0, 3), (1, 2), (2, 1), (3, 0)])
 
 
 def add_low(left, right):
     return (left.astype(F32) + right.astype(F32)).astype(BF16)
 
 
-def plane_reduce(parts):
-    a = [part[0] for part in parts]
-    b = [part[1] for part in parts]
-    here_a = add_low(a[0], swap(a[1], "x"))
-    next_a = add_low(a[2], swap(a[3], "x"))
-    here_b = add_low(b[0], swap(b[2], "y"))
-    next_b = add_low(b[1], swap(b[3], "y"))
-    return add_low(here_a, swap(next_a, "y")), add_low(here_b, swap(next_b, "x"))
-
-
-def in_order(parts, x, y, c):
-    stacked = jnp.stack(parts)
-    stacked = jnp.where(x == 0, stacked, stacked[jnp.array([1, 0, 3, 2])])
-    stacked = jnp.where(y == 0, stacked, stacked[jnp.array([2, 3, 0, 1])])
-    return jnp.where(c == 0, stacked, stacked[:, ::-1])
-
-
-def owned_gradient(total, c):
-    mine = lax.psum_scatter(total, "z", scatter_dimension=0, tiled=True)
+def where_from(places_ref, r, h):
+    core = places_ref[0] if h == 0 else 1 - places_ref[0]
+    row = places_ref[1] if r < 2 else 1 - places_ref[1]
+    column = places_ref[2] if r % 2 == 0 else 1 - places_ref[2]
+    return core, 2 * row + column
+
+
+def gain_gradient(pairs, gain_ref, out_ref):
+    total = jnp.zeros((LANES, LANES), F32)
+    for weight, grad in pairs:
+        total += weight.astype(F32) * grad
+    out_ref[...] = jnp.sum(total.T, axis=0, keepdims=True) / gain_ref[...]
+
+
+def rest_order_body(places_ref, *refs):
+    parts, (w_ref, gain_ref, in_ref, down_ref, gain_grad_ref, rows) = refs[:4], refs[4:]
+    for r in range(4):
+        for h in range(2):
+            core, place = where_from(places_ref, r, h)
+            at = pl.multiple_of((core * 4 + place) * UNITS, 8)
+            for i in range(2):
+                rows[pl.ds(i * FF + at, UNITS), :] = parts[r][h, i * HIDDEN : (i + 1) * HIDDEN].astype(F32)[:UNITS]
+            down_ref[pl.ds(at, UNITS), :] = parts[r][h, 2 * HIDDEN :].astype(F32)[:UNITS]
+    turned_pairs(rows, in_ref, w_ref, gain_ref, gain_grad_ref)
+
+
+def turned_pairs(rows, grad_ref, w_ref, gain_ref, gain_grad_ref):
+    pairs = []
+    for j in range(grad_ref.shape[1] // LANES):
+        lanes = slice(LANES * j, LANES * (j + 1))
+        grad = rows[lanes, :].T
+        grad_ref[:, lanes] = grad
+        pairs.append((w_ref[:, lanes], grad))
+    gain_gradient(pairs, gain_ref, gain_grad_ref)
+
+
+def qkv_order_body(places_ref, *refs):
+    parts, (w_ref, gain_ref, qkv_ref, out_ref, gain_grad_ref, rows) = refs[:4], refs[4:]
+    for r in range(4):
+        for h in range(2):
+            core, place = where_from(places_ref, r, h)
+            part = parts[r][h].astype(F32)
+            at = (core * 4 + place) * QKV
+            for head in range(PAIR):
+                for t in range(2):
+                    for side in range(2):
+                        to = pl.multiple_of(at + head * 3 * HD + t * HD + side * HALF, 8)
+                        source = t * OUT + side * HD + head * HALF
+                        rows[pl.ds(to, HALF), :] = part[source : source + HALF]
+                to = pl.multiple_of(at + head * 3 * HD + 2 * HD, 8)
+                rows[pl.ds(to, HD), :] = part[2 * OUT + head * HD : 2 * OUT + (head + 1) * HD]
+            to = pl.multiple_of((core * 4 + place) * OUT, 8)
+            out_ref[pl.ds(to, OUT), :] = part[QKV : QKV + OUT]
+    turned_pairs(rows, qkv_ref, w_ref, gain_ref, gain_grad_ref)
+
+
+def in_weight_order(body, places, parts, weight, gain, shapes, rows, name):
+    return pl.pallas_call(
+        body,
+        in_specs=[pl.BlockSpec(memory_space=pltpu.SMEM)] + whole_in_vmem(6),
+        out_specs=whole_in_vmem(len(shapes)),
+        out_shape=[jax.ShapeDtypeStruct(shape, F32) for shape in shapes],
+        scratch_shapes=[pltpu.VMEM((rows, LANES), F32)],
+        compiler_params=pltpu.CompilerParams(vmem_limit_bytes=24 * MIB),
+        cost_estimate=pl.CostEstimate(flops=0, transcendentals=0, bytes_accessed=16 * rows * LANES),
+        name=name,
+    )(places, *parts, weight, gain.astype(F32).reshape(1, LANES))
+
+
+def owned_gradient(mine, c):
     keep = lax.dynamic_index_in_dim(mine, c, 0, keepdims=False)
     give = lax.dynamic_index_in_dim(mine, 1 - c, 0, keepdims=False)
     own = jnp.stack([keep, swap(give, "c")])
-    corner = lax.ppermute(own, ("y", "x"), [(0, 3), (1, 2), (2, 1), (3, 0)])
-    return [own, swap(own, "x"), swap(own, "y"), corner]
-
-
-def spread_pieces(pieces, c):
+    return [own, swap(own, "x"), swap(own, "y"), swap_corner(own)]
+
+
+def core_pieces(pieces, c):
     keep = lax.dynamic_index_in_dim(pieces, c, 0, keepdims=False)
     give = lax.dynamic_index_in_dim(pieces, 1 - c, 0, keepdims=False)
     got = swap(give, "c")
-    both = jnp.where(c == 0, jnp.stack([keep, got]), jnp.stack([got, keep]))
-    return lax.all_gather(both, "z", axis=0, tiled=True)
+    return jnp.where(c == 0, jnp.stack([keep, got]), jnp.stack([got, keep]))
+
+
+def gather_columns(pieces):
+    return lax.all_gather(pieces, "z", axis=0, tiled=True)
 
 
 def chip_local(tokens, segment_ids, w_qkv, w_out, w_in, w_down, gain_attn, gain_mlp, grad_output):
@@ -769,12 +831,13 @@
     out_rows = lax.dynamic_index_in_dim(w_out.reshape(2, 4, OUT, LANES), place, 1, keepdims=False)
     down_rows = lax.dynamic_index_in_dim(w_down.reshape(2, 4, UNITS, LANES), place, 1, keepdims=False)
     in_rows = lax.dynamic_index_in_dim(w_in.T.reshape(2, 2, 4, UNITS, LANES), place, 2, keepdims=False)
+    units = [in_rows[0], in_rows[1], down_rows]
     fill = ((0, 0), (0, HIDDEN - UNITS), (0, 0))
-    rest_pieces = jnp.concatenate(
-        [out_rows, jnp.pad(in_rows[0], fill), jnp.pad(in_rows[1], fill), jnp.pad(down_rows, fill)], axis=1
-    )
-    qkv_own = spread_pieces(first_pieces, c)
-    rest_own = spread_pieces(rest_pieces, c)
+    early = jnp.concatenate([out_rows] + [item[:, : SPLIT[0]] for item in units], axis=1)
+    late = jnp.concatenate([jnp.pad(item[:, SPLIT[0] :], fill) for item in units], axis=1)
+    qkv_own = gather_columns(core_pieces(first_pieces, c))
+    others = core_pieces(jnp.concatenate([early, late], axis=1), c)
+    early_own = gather_columns(after(others[:, : early.shape[1]], qkv_own))
     gain_one = qkv_own[:, QKV, :].reshape(1, D).astype(F32)
     gain_two = qkv_own[:, QKV + 1, :].reshape(1, D).astype(F32)
 
@@ -800,55 +863,115 @@
     normed_one, scale_one = moments(rows_in)
     low_own = (normed_one * gain_one).astype(BF16)
     low_one = jnp.concatenate([low_own, swap(low_own, "c")], axis=0)
-    qkv_parts = plane_gather(qkv_own)
-    rest_parts = plane_gather(rest_own)
-    saved = [attention(low_one, part, tables) for part in qkv_parts]
-    own, other = partial_rows([item[3] for item in saved], rest_parts)
+    qkv_parts = [qkv_own, swap(qkv_own, "x"), swap(qkv_own, "y")]
+    saved = [attention(low_one, qkv_own, tables)]
+    across, along = after(tuple(qkv_parts[1:]), saved[0][3])
+    corner = [corner_half(along, 0, "x"), corner_half(across, 1, "y")]
+    late_own = gather_columns(after(others[:, early.shape[1] :], saved[0][3]))
+    saved.append(attention(after(low_one, saved[0][3], across, along, dy), across, tables))
+    early_own = after(early_own, saved[1][3])
+    out_own, early_own = early_own[:, :OUT], early_own[:, OUT:]
+    out_parts = [out_own, swap(out_own, "x"), swap(out_own, "y"), swap_corner(out_own)]
+    early_parts = [early_own, swap(early_own, "x"), swap(early_own, "y")]
+    saved.append(attention(after(low_one, saved[1][3], early_own), along, tables))
+    qkv_parts.append(jnp.concatenate(corner, axis=0))
+    saved.append(attention(after(low_one, saved[2][3]), qkv_parts[3], tables))
+    late_own = after(late_own, saved[3][3])
+    late_parts = [late_own, swap(late_own, "x"), swap(late_own, "y")]
+    own, other = partial_rows([item[3] for item in saved], out_parts)
     hidden = rows_in + own + swap(other, "c").astype(F32)
     normed_two, scale_two = moments(hidden)
     low_own = (normed_two * gain_two).astype(BF16)
     low_two = jnp.concatenate([low_own, swap(low_own, "c")], axis=0)
 
-    sums = None
-    rest_grads = []
-    for part in rest_parts:
-        sums, grads = mlp(low_two, dy, part, sums)
-        rest_grads.append(grads)
+    grads, got = [None] * 4, {}
+    across, along = after(tuple(early_parts[1:]), low_own)
+    early_corner = [corner_half(along, 0, "x"), corner_half(across, 1, "y")]
+    sums, grads[0] = mlp(after(low_two, across, along), dy, (early_own, late_own), None)
+    across, along = after(tuple(late_parts[1:]), sums)
+    late_corner = [corner_half(along, 0, "x"), corner_half(across, 1, "y")]
+    sums, grads[1] = mlp(after(low_two, across, along), dy, (early_parts[1], across), sums)
+    got[1, 0] = swap(grads[1][0], "x")
+    sums, grads[2] = mlp(low_two, dy, (early_parts[2], along), sums)
+    got[2, 1] = swap(grads[2][1], "y")
+    early_corner, late_corner = after((tuple(early_corner), tuple(late_corner)), sums)
+    corner = (jnp.concatenate(early_corner, axis=0), jnp.concatenate(late_corner, axis=0))
+    sums, grads[3] = mlp(after(low_two, got[1, 0]), dy, corner, sums)
+    got[3, 0], got[3, 1] = swap(grads[3][0], "x"), swap(grads[3][1], "y")
     half = 2 * piece
+    dn_two = sums[1][:half] + swap(after(sums[1][half:].astype(BF16), got[2, 1]), "c").astype(F32)
     result = hidden + sums[0][:half] + swap(sums[0][half:].astype(BF16), "c").astype(F32)
-    output = from_sequence(result.astype(BF16), straight, x)
-    dn_two = sums[1][:half] + swap(sums[1][half:].astype(BF16), "c").astype(F32)
-    pulled, gain_grad_two = norm_back(dn_two, gain_two, normed_two, scale_two)
+    pulled = norm_back(dn_two, gain_two, normed_two, scale_two)
     grad_hidden = dy_own.astype(F32) + pulled
     branch_own = grad_hidden.astype(BF16)
     branch = jnp.concatenate([branch_own, swap(branch_own, "c")], axis=0)
-    rest_total = plane_reduce(rest_grads)
-    rest_owned = owned_gradient(jnp.concatenate(rest_total, axis=0), c)
-
-    mixed_grads, qkv_grads = [None] * 4, [None] * 4
-    for r in (3, 1, 2, 0):
-        mixed_grads[r], low, high = attention_back(saved[r], branch, low_one, rest_parts[r], tables)
+
+    mixed_grads, qkv_grads, q_got = [None] * 4, [None] * 4, {}
+
+    def back(r, *others):
+        mixed_grads[r], low, high = attention_back(saved[r], after(branch, *others), low_one, out_parts[r], tables)
         qkv_grads[r] = (low, high)
-    own, other = partial_rows(mixed_grads, qkv_parts)
+
+    def summed(r, h, piece, done):
+        return add_low(grads[r][h], after(piece, done))
+
+    back(3)
+    done = mixed_grads[3]
+    here_a, next_a = summed(0, 0, got[1, 0], done), summed(2, 0, got[3, 0], done)
+    here_b, next_b = summed(0, 1, got[2, 1], done), summed(1, 1, got[3, 1], done)
+    got_a, got_b = swap(next_a, "y"), swap(next_b, "x")
+    back(1, here_a, next_a, here_b, next_b)
+    done = mixed_grads[1]
+    low, high = after(qkv_grads[3], done)
+    q_got[3, 0], q_got[3, 1] = swap(low, "x"), swap(high, "y")
+    q_got[1, 0] = swap(qkv_grads[1][0], "x")
+    back(2, done)
+    done = mixed_grads[2]
+    q_got[2, 1] = swap(qkv_grads[2][1], "y")
+    got_a, got_b = after((got_a, got_b), done)
+    rest_total = jnp.concatenate([add_low(here_a, got_a), add_low(here_b, got_b)], axis=0)
+    rest_sum = lax.psum_scatter(rest_total, "z", scatter_dimension=0, tiled=True)
+    next_a = add_low(qkv_grads[2][0], after(q_got[3, 0], done))
+    next_b = add_low(qkv_grads[1][1], after(q_got[3, 1], done))
+    got_a, got_b = swap(next_a, "y"), swap(next_b, "x")
+    back(0, rest_total, q_got[1, 0], next_a, next_b)
+    done = mixed_grads[0]
+    here_a = add_low(qkv_grads[0][0], q_got[1, 0])
+    here_b = add_low(qkv_grads[0][1], after(q_got[2, 1], done))
+    got_a, got_b = after((got_a, got_b), done)
+    qkv_total = jnp.concatenate([add_low(here_a, got_a), add_low(here_b, got_b)], axis=0)
+    qkv_sum = lax.psum_scatter(after(qkv_total, rest_sum), "z", scatter_dimension=0, tiled=True)
+    rest_owned = owned_gradient(rest_sum, c)
+    own, other = partial_rows(after(tuple(mixed_grads), qkv_total), qkv_parts)
     dn_one = own + swap(other, "c").astype(F32)
-    pulled, gain_grad_one = norm_back(dn_one, gain_one, normed_one, scale_one)
-    input_grad = from_sequence((grad_hidden + pulled).astype(BF16), straight, x)
-    gain_rows = jnp.stack([gain_grad_one, gain_grad_two]).reshape(2, -1, LANES).transpose(1, 0, 2)
-    gain_rows = jnp.pad(gain_rows, ((0, 0), (0, 6), (0, 0))).astype(BF16)
-    qkv_total = jnp.concatenate(plane_reduce(qkv_grads), axis=0)
-    qkv_owned = owned_gradient(jnp.concatenate([qkv_total, gain_rows], axis=1), c)
-
-    rest_all = in_order(rest_owned, x, y, c).astype(F32)
-    blocks = rest_all.reshape(4, 2, 3, HIDDEN, LANES)[:, :, :, :UNITS].transpose(2, 1, 0, 3, 4)
-    grad_in = blocks[0:2].reshape(2 * FF, LANES).T
-    grad_down = blocks[2].reshape(FF, LANES)
-    qkv_all = in_order(qkv_owned, x, y, c).astype(F32)
-    qk = qkv_all[:, :, : 2 * OUT].reshape(4, 2, 2, 2, PAIR, HALF, LANES).transpose(6, 1, 0, 4, 2, 3, 5)
-    val = qkv_all[:, :, 2 * OUT : QKV].reshape(4, 2, PAIR, 2, HALF, LANES).transpose(5, 1, 0, 2, 3, 4)
-    grad_qkv = jnp.concatenate([qk, val[:, :, :, :, None]], axis=4).reshape(LANES, 3 * HEADS * HD)
-    grad_out = qkv_all[:, :, QKV : QKV + OUT].transpose(1, 0, 2, 3).reshape(HEADS * HD, LANES)
-    gain_sums = jnp.sum(qkv_all[:, :, QKV + OUT : QKV + OUT + 2], axis=(0, 1))
-    return output, input_grad, grad_qkv, grad_out, grad_in, grad_down, gain_sums[0], gain_sums[1]
+    input_grad = (grad_hidden + norm_back(dn_one, gain_one, normed_one, scale_one)).astype(BF16)
+    output = from_sequence(after(result.astype(BF16), own), straight, x)
+    input_grad = from_sequence(input_grad, straight, x)
+    qkv_owned = owned_gradient(qkv_sum, c)
+
+    own_place = jnp.stack([c, y, x]).astype(jnp.int32)
+    grad_in, grad_down, grad_gain_mlp = in_weight_order(
+        rest_order_body,
+        own_place,
+        rest_owned,
+        w_in,
+        gain_mlp,
+        [(LANES, 2 * FF), (FF, LANES), (1, LANES)],
+        2 * FF,
+        "rest_order",
+    )
+    grad_qkv, grad_out, grad_gain_attn = in_weight_order(
+        qkv_order_body,
+        own_place,
+        qkv_owned,
+        w_qkv,
+        gain_attn,
+        [(LANES, 3 * HEADS * HD), (HEADS * HD, LANES), (1, LANES)],
+        3 * HEADS * HD,
+        "qkv_order",
+    )
+    gain_grads = grad_gain_attn.reshape(-1), grad_gain_mlp.reshape(-1)
+    return output, input_grad, grad_qkv, grad_out, grad_in, grad_down, *gain_grads
 
 
 def solution(mesh):

time: 565 us -> 444 us (0.79)
  waiting for transfers between devices: 209 us -> 89.2 us
  blocking collectives: 31.4 us -> 21.2 us
  starting transfers between devices: 48 us -> 57.3 us
  Pallas kernels: 148 us -> 154 us
    ppermute x37 -> x43, waiting for transfers between devices: 164 us -> 50.1 us  [swap(): return lax.ppermute(value, axis, BOTH)]
    all_gather x1, blocking collectives: 31.4 us -> 21.2 us  [gather_columns(): return lax.all_gather(pieces, 'z', axis=0, tiled=True)]
    ppermute x2, waiting for transfers between devices: 9.48 us -> 0.01 us  [to_sequence(): lax.ppermute(jnp.where(straight, other, same), ('c', 'y', 'x'), near)]
    gather x4 -> x0, local copies, waits for them, and re-layouts: 8.96 us -> none  [the longest x2 5.68 us: in_order(): stacked = jnp.where(y == 0, stacked, stacked[jnp.array([2, 3, 0, 1])])]
    ppermute x37 -> x43, starting transfers between devices: 34 us -> 42.7 us  [swap(): return lax.ppermute(value, axis, BOTH)]
    select_n x7 -> x2, other arithmetic: 8.04 us -> 1.08 us  [core_pieces(): return jnp.where(c == 0, jnp.stack([keep, got]), jnp.stack([got, keep]))]
    pallas_call x0 -> x2, Pallas kernels: none -> 5.95 us  [in_weight_order(): pl.pallas_call(body, in_specs=[pl.BlockSpec(memory_space=pltpu.SMEM)] + w...]
    reduce_scatter x2, waiting for transfers between devices: 0.02 us -> 5.76 us  [the longest x1 5.76 us: chip_local(): lax.psum_scatter(after(qkv_total, rest_sum), 'z', scatter_dimension=0, ti...]
  transfers between devices with their start and end apart: 50 -> 58, of which waited for: 24 -> 19; matrix products, arithmetic and copies ran while one was open for 10% -> 15% of each run, Pallas kernels for 14% -> 34%
where the time goes in v2:
time: 444 us; the launch traced here: 436 us
  Pallas kernels  154 us (35%)
  waiting for transfers between devices  89.2 us (20%)
  starting transfers between devices  57.3 us (13%)
  other arithmetic  50.9 us (11%)
  local copies, waits for them, and re-layouts  48.6 us (11%)
  blocking collectives  21.2 us (5%)
  between operations  15.7 us (4%)
    pallas_call x4, Pallas kernels, mlp(): pl.pallas_call(functools.partial(mlp_body, first), grid=(tokens // TILE,)...  55.4 us
    ppermute x43, waiting for transfers between devices, swap(): return lax.ppermute(value, axis, BOTH)  50.1 us
    pallas_call x4, Pallas kernels, attention_back(): pl.pallas_call(backward_body, grid=(1,), in_specs=[vmem] * 7 + [pl.BlockS...  49.1 us
    ppermute x43, starting transfers between devices, swap(): return lax.ppermute(value, axis, BOTH)  42.7 us
    pallas_call x4, Pallas kernels, attention(): pl.pallas_call(forward_body, in_specs=whole_in_vmem(6), out_specs=whole_i...  33.2 us
    unnamed x248, local copies, waits for them, and re-layouts  31.8 us
    all_gather x1, blocking collectives, gather_columns(): return lax.all_gather(pieces, 'z', axis=0, tiled=True)  21.2 us
    all_gather x2, waiting for transfers between devices, gather_columns(): return lax.all_gather(pieces, 'z', axis=0, tiled=True)  19.6 us
  transfers between devices with their start and end apart: 58, of which 19 were waited for; matrix products, arithmetic and copies ran while one was open for 15% of the time, Pallas kernels for 34%

profile of v2, /device:TPU:0, one launch (start us, length us, event | category | flops | bytes accessed | tf_op | source)
XLA Modules:
  0.0 436.4 jit_solution(1590450317592587299)
XLA Ops:
  7.3 1.6 copy.60
  11.4 2.5 collective-permute-start.7
  20.5 1.6 copy.64
  25.2 3.8 collective-permute-start.10
  30.0 21.2 %all_gather.9.w_ref.refs_4_ = bf16[8,400,128]{2,1,0:T(8,128)(2,1)} all-gather(bf16[2,400,128]{2,1,0:T(8,128)(2,1)S(1)} %maximum_select_fusion.3), channel_id=1, replica_groups=mesh['z'=4,'c'=2,'y'=2,'x'=2] {'z'}, dimensions={0}, use_global_device_ids=true | all-gather | bytes 1024000 | tf_op jit(solution)/shard_map/all_gather | solution.py:815
  54.7 1.6 collective-permute-start.5
  57.8 1.5 bitcast_select_fusion
  63.5 1.9 fusion.17
  69.0 8.9 %attention.4 = (bf16[1024,128]{1,0:T(8,128)(2,1)S(1)}, bf16[1024,128]{1,0:T(8,128)(2,1)S(1)}, bf16[1024,128]{1,0:T(8,128)(2,1)S(1)}, bf16[1024,128]{1,0:T(8,128)(2,1)S(1)}, f32[8,1024]{1,0:T(8,128)S(1)}) custom-call(bf16[1024,1024]{1,0:T(8,128)(2,1)S(1)} %pad_maximum_fusion.n_ref, bf16[8,400,128]{2,1,0:T(8,128)(2,1)} %all_gather.9.w_ref.refs_4_, ...), custom_call_target="tpu_custom_call" | custom-call | flops 1879048192 | bytes 6291456 | tf_op jit(solution)/shard_map/attention/pallas_call | solution.py:525
  81.6 1.5 collective-permute-start.12
  83.1 2.7 pad_maximum_fusion.1.dy_ref
  85.9 8.4 %attention.5 = (bf16[1024,128]{1,0:T(8,128)(2,1)S(1)}, bf16[1024,128]{1,0:T(8,128)(2,1)S(1)}, bf16[1024,128]{1,0:T(8,128)(2,1)S(1)}, bf16[1024,128]{1,0:T(8,128)(2,1)S(1)}, f32[8,1024]{1,0:T(8,128)S(1)}) custom-call(bf16[1024,1024]{1,0:T(8,128)(2,1)S(1)} %pad_maximum_fusion.n_ref, bf16[8,400,128]{2,1,0:T(8,128)(2,1)} %collective-permute-done.5.w_ref.refs_5_, ...), custom_call_target="tpu_custom_call" | custom-call | flops 1879048192 | bytes 6291456 | tf_op jit(solution)/shard_map/attention/pallas_call | solution.py:525
  98.0 2.3 slice.138.wa_ref
  100.3 1.6 collective-permute-start.15
  103.8 8.4 %attention.6 = (bf16[1024,128]{1,0:T(8,128)(2,1)S(1)}, bf16[1024,128]{1,0:T(8,128)(2,1)S(1)}, bf16[1024,128]{1,0:T(8,128)(2,1)S(1)}, bf16[1024,128]{1,0:T(8,128)(2,1)S(1)}, f32[8,1024]{1,0:T(8,128)S(1)}) custom-call(bf16[1024,1024]{1,0:T(8,128)(2,1)S(1)} %pad_maximum_fusion.n_ref, bf16[8,400,128]{2,1,0:T(8,128)(2,1)} %collective-permute-done.6.w_ref.refs_6_, ...), custom_call_target="tpu_custom_call" | custom-call | flops 1879048192 | bytes 6291456 | tf_op jit(solution)/shard_map/attention/pallas_call | solution.py:525
  114.4 7.3 %attention.7 = (bf16[1024,128]{1,0:T(8,128)(2,1)S(1)}, bf16[1024,128]{1,0:T(8,128)(2,1)S(1)}, bf16[1024,128]{1,0:T(8,128)(2,1)S(1)}, bf16[1024,128]{1,0:T(8,128)(2,1)S(1)}, f32[8,1024]{1,0:T(8,128)S(1)}) custom-call(bf16[1024,1024]{1,0:T(8,128)(2,1)S(1)} %pad_maximum_fusion.n_ref, bf16[8,400,128]{2,1,0:T(8,128)(2,1)S(1)} %copy-done.25, ...), custom_call_target="tpu_custom_call" | custom-call | flops 1879048192 | bytes 6291456 | tf_op jit(solution)/shard_map/attention/pallas_call | solution.py:525
  124.5 3.1 partial_rows.2
  128.9 1.7 slice.174
  131.9 2.6 fusion.19
  137.0 1.5 collective-permute-start.20
  138.5 19.6 %all-gather.5.cloned.1.call-done.wb_ref = bf16[8,528,128]{2,1,0:T(8,128)(2,1)} async-done(((bf16[2,528,128]{2,1,0:T(8,128)(2,1)}), bf16[8,528,128]{2,1,0:T(8,128)(2,1)}) %all-gather.5.cloned.1.call-update) | async-done | bytes 1081360 | tf_op jit(solution)/shard_map/all_gather | solution.py:815
  158.1 1.5 collective-permute-start.19
  159.5 1.5 collective-permute-start.18
  163.2 1.6 collective-permute-start.23
  166.2 1.7 pad_maximum_fusion.2.n_ref
  167.9 13.8 %mlp.4 = (f32[1024,1024]{1,0:T(8,128)S(1)}, f32[1024,1024]{1,0:T(8,128)}, bf16[4,1008,128]{2,1,0:T(8,128)(2,1)S(1)}, bf16[4,1008,128]{2,1,0:T(8,128)(2,1)S(1)}) custom-call(bf16[1024,1024]{1,0:T(8,128)(2,1)S(1)} %pad_maximum_fusion.2.n_ref, bf16[1024,1024]{1,0:T(8,128)(2,1)S(1)} %copy-done.4, bf16[8,480,128]{2,1,0:T(8,128)(2,1)} %slice.138.wa_ref, ...), custom_call_target="tpu_custom_call" | custom-call | flops 6341787648 | bytes 25100288 | tf_op jit(solution)/shard_map/mlp/pallas_call | solution.py:457
  181.7 3.3 collective-permute-done.19.wb_ref
  185.0 1.5 collective-permute-done.18.wb_ref
  186.6 1.5 collective-permute-start.25
  188.2 13.9 %mlp.5 = (f32[1024,1024]{1,0:T(8,128)S(1)}, f32[1024,1024]{1,0:T(8,128)}, bf16[4,1008,128]{2,1,0:T(8,128)(2,1)S(1)}, bf16[4,1008,128]{2,1,0:T(8,128)(2,1)S(1)}) custom-call(bf16[1024,1024]{1,0:T(8,128)(2,1)S(1)} %pad_maximum_fusion.2.n_ref, bf16[1024,1024]{1,0:T(8,128)(2,1)S(1)} %copy-done.4, ...), custom_call_target="tpu_custom_call", output_to_operand_aliasing={{0}: (4, {}), {1}: (5, {})} | custom-call | flops 6341787648 | bytes 25100288 | tf_op jit(solution)/shard_map/mlp/pallas_call | solution.py:457
  203.2 13.9 %mlp.6 = (f32[1024,1024]{1,0:T(8,128)S(1)}, f32[1024,1024]{1,0:T(8,128)}, bf16[4,1008,128]{2,1,0:T(8,128)(2,1)S(1)}, bf16[4,1008,128]{2,1,0:T(8,128)(2,1)S(1)}) custom-call(bf16[1024,1024]{1,0:T(8,128)(2,1)S(1)} %pad_maximum_fusion.2.n_ref, bf16[1024,1024]{1,0:T(8,128)(2,1)S(1)} %copy-done.4, ...), custom_call_target="tpu_custom_call", output_to_operand_aliasing={{0}: (4, {}), {1}: (5, {})} | custom-call | flops 6341787648 | bytes 25100288 | tf_op jit(solution)/shard_map/mlp/pallas_call | solution.py:457
  219.8 9.4 %collective-permute-done.22 = bf16[4,1008,128]{2,1,0:T(8,128)(2,1)} collective-permute-done((bf16[4,1008,128]{2,1,0:T(8,128)(2,1)S(1)}, bf16[4,1008,128]{2,1,0:T(8,128)(2,1)}, u32[]{:S(2)}, u32[]{:S(2)}) %collective-permute-start.22) | collective-permute-done | bytes 1032224 | tf_op jit(solution)/shard_map/ppermute | solution.py:666
  229.2 13.8 %mlp.7 = (f32[1024,1024]{1,0:T(8,128)S(1)}, f32[1024,1024]{1,0:T(8,128)}, bf16[4,1008,128]{2,1,0:T(8,128)(2,1)S(1)}, bf16[4,1008,128]{2,1,0:T(8,128)(2,1)S(1)}) custom-call(bf16[1024,1024]{1,0:T(8,128)(2,1)S(1)} %pad_maximum_fusion.2.n_ref, bf16[1024,1024]{1,0:T(8,128)(2,1)S(1)} %copy-done.4, ...), custom_call_target="tpu_custom_call", output_to_operand_aliasing={{0}: (4, {}), {1}: (5, {})} | custom-call | flops 6341787648 | bytes 25100288 | tf_op jit(solution)/shard_map/mlp/pallas_call | solution.py:457
  243.0 1.9 slice.228
  246.2 1.5 collective-permute-done.29
  247.7 2.3 fusion.16
  250.1 2.9 fusion.18
  253.8 1.6 collective-permute-start.31
  255.9 12.8 %attention_back.4 = (bf16[1024,384]{1,0:T(8,128)(2,1)S(1)}, bf16[4,512,128]{2,1,0:T(8,128)(2,1)}, bf16[4,512,128]{2,1,0:T(8,128)(2,1)S(1)}) custom-call(bf16[1024,128]{1,0:T(8,128)(2,1)S(1)} %copy-done.66, bf16[1024,128]{1,0:T(8,128)(2,1)S(1)} %copy-done.68, bf16[1024,128]{1,0:T(8,128)(2,1)S(1)} %copy-done.70, bf16[1024,128]{1,0:T(8,128)(2,1)S(1)} %copy-done.46, ...), custom_call_target="tpu_custom_call" | custom-call | flops 4026531840 | bytes 10485760 | tf_op jit(solution)/shard_map/attention_back/pallas_call | solution.py:595
  268.7 9.5 %collective-permute-done.33 = bf16[4,1008,128]{2,1,0:T(8,128)(2,1)S(1)} collective-permute-done((bf16[4,1008,128]{2,1,0:T(8,128)(2,1)S(1)}, bf16[4,1008,128]{2,1,0:T(8,128)(2,1)S(1)}, u32[]{:S(2)}, u32[]{:S(2)}) %collective-permute-start.33) | collective-permute-done | bytes 1032224 | tf_op jit(solution)/shard_map/ppermute | solution.py:666
  280.7 1.5 collective-permute-start.34
  282.5 1.6 add_convert_fusion.6
  284.2 12.0 %attention_back.5 = (bf16[1024,384]{1,0:T(8,128)(2,1)S(1)}, bf16[4,512,128]{2,1,0:T(8,128)(2,1)S(1)}, bf16[4,512,128]{2,1,0:T(8,128)(2,1)S(1)}) custom-call(bf16[1024,128]{1,0:T(8,128)(2,1)S(1)} %copy-done.54, bf16[1024,128]{1,0:T(8,128)(2,1)S(1)} %copy-done.56, bf16[1024,128]{1,0:T(8,128)(2,1)S(1)} %copy-done.58, bf16[1024,128]{1,0:T(8,128)(2,1)S(1)} %copy-done.42, ...), custom_call_target="tpu_custom_call" | custom-call | flops 4026531840 | bytes 10485760 | tf_op jit(solution)/shard_map/attention_back/pallas_call | solution.py:595
  298.5 12.4 %attention_back.6 = (bf16[1024,384]{1,0:T(8,128)(2,1)S(1)}, bf16[4,512,128]{2,1,0:T(8,128)(2,1)S(1)}, bf16[4,512,128]{2,1,0:T(8,128)(2,1)S(1)}) custom-call(bf16[1024,128]{1,0:T(8,128)(2,1)S(1)} %copy-done.60, bf16[1024,128]{1,0:T(8,128)(2,1)S(1)} %copy-done.62, bf16[1024,128]{1,0:T(8,128)(2,1)S(1)} %copy-done.64, bf16[1024,128]{1,0:T(8,128)(2,1)S(1)} %copy-done.44, ...), custom_call_target="tpu_custom_call" | custom-call | flops 4026531840 | bytes 10485760 | tf_op jit(solution)/shard_map/attention_back/pallas_call | solution.py:595
  312.3 1.5 pad_maximum_fusion.4
  319.5 9.5 %collective-permute-done.37 = bf16[4,512,128]{2,1,0:T(8,128)(2,1)S(1)} collective-permute-done((bf16[4,512,128]{2,1,0:T(8,128)(2,1)}, bf16[4,512,128]{2,1,0:T(8,128)(2,1)S(1)}, u32[]{:S(2)}, u32[]{:S(2)}) %collective-permute-start.37) | collective-permute-done | bytes 524320 | tf_op jit(solution)/shard_map/ppermute | solution.py:666
  330.2 1.5 collective-permute-start.39
  337.6 12.0 %attention_back.7 = (bf16[1024,384]{1,0:T(8,128)(2,1)S(1)}, bf16[4,512,128]{2,1,0:T(8,128)(2,1)S(1)}, bf16[4,512,128]{2,1,0:T(8,128)(2,1)S(1)}) custom-call(bf16[1024,128]{1,0:T(8,128)(2,1)S(1)} %copy-done.48, bf16[1024,128]{1,0:T(8,128)(2,1)S(1)} %copy-done.50, bf16[1024,128]{1,0:T(8,128)(2,1)S(1)} %copy-done.52, bf16[1024,128]{1,0:T(8,128)(2,1)S(1)} %copy-done.39, ...), custom_call_target="tpu_custom_call" | custom-call | flops 4026531840 | bytes 10485760 | tf_op jit(solution)/shard_map/attention_back/pallas_call | solution.py:595
  357.2 6.9 %partial_rows.3 = (f32[512,1024]{1,0:T(8,128)S(1)}, bf16[512,1024]{1,0:T(8,128)(2,1)S(1)}) custom-call(bf16[1024,384]{1,0:T(8,128)(2,1)S(1)} %copy-done.78, bf16[1024,384]{1,0:T(8,128)(2,1)S(1)} %copy-done.74, bf16[1024,384]{1,0:T(8,128)(2,1)S(1)} %copy-done.76, bf16[1024,384]{1,0:T(8,128)(2,1)S(1)} %copy-done.72, ...), custom_call_target="tpu_custom_call" | custom-call | flops 3221225472 | bytes 8388608 | tf_op jit(solution)/shard_map/partial_rows/pallas_call | solution.py:643
  367.8 3.0 fusion.11
  371.6 2.9 collective-permute-done.41
  376.2 2.5 collective-permute-start.50
  381.3 1.6 collective-permute-start.45
  383.0 3.2 collective-permute-start.53
  387.3 5.8 %reduce-scatter.5.cloned.1.call-done = bf16[2,512,128]{2,1,0:T(8,128)(2,1)} async-done(((bf16[8,512,128]{2,1,0:T(8,128)(2,1)}), bf16[2,512,128]{2,1,0:T(8,128)(2,1)}) %reduce-scatter.5.cloned.1.call-update) | async-done | bytes 262160 | tf_op jit(solution)/shard_map/reduce_scatter | solution.py:943
  394.2 2.4 maximum_select_fusion
  396.6 1.5 collective-permute-start.52
  400.2 1.5 collective-permute-start.48
  401.7 7.2 %collective-permute-done.53.refs_3_ = bf16[2,1008,128]{2,1,0:T(8,128)(2,1)S(1)} collective-permute-done((bf16[2,1008,128]{2,1,0:T(8,128)(2,1)S(1)}, bf16[2,1008,128]{2,1,0:T(8,128)(2,1)S(1)}, u32[]{:S(2)}, u32[]{:S(2)}) %collective-permute-start.53) | collective-permute-done | bytes 516128 | tf_op jit(solution)/shard_map/ppermute | solution.py:724
  410.1 8.7 %collective-permute-done.52.refs_2_ = bf16[2,1008,128]{2,1,0:T(8,128)(2,1)S(1)} collective-permute-done((bf16[2,1008,128]{2,1,0:T(8,128)(2,1)S(1)}, bf16[2,1008,128]{2,1,0:T(8,128)(2,1)S(1)}, u32[]{:S(2)}, u32[]{:S(2)}) %collective-permute-start.52) | collective-permute-done | bytes 516128 | tf_op jit(solution)/shard_map/ppermute | solution.py:666
  418.8 3.5 rest_order.1
  422.3 2.2 collective-permute-done.49.refs_3_
  424.5 2.7 collective-permute-done.48.refs_2_
  427.2 2.5 qkv_order.1
  (432 shorter events, 95.5 us)
Async XLA Ops:
  7.2 89.7 %all-gather.3.cloned.1.call-start = ((), (), s32[]{:S(2)}) async-start(), calls=%async_computation.2 | async-start | bytes 1556480 | tf_op jit(solution)/shard_map/all_gather | solution.py:815
  9.9 15.2 %collective-permute-start.2 = (bf16[400,128]{1,0:T(8,128)(2,1)}, bf16[400,128]{1,0:T(8,128)(2,1)}, u32[]{:S(2)}, u32[]{:S(2)}) collective-permute-start(bf16[400,128]{1,0:T(8,128)(2,1)} %get-tuple-element.244), channel_id=1, source_target_pairs={{0,4},{4,0},{1,5},{5,1},{2,6},{6,2},{3,7},{7,3},{8,12},{12,8},{9,1... | collective-permute-start | bytes 307208 | tf_op jit(solution)/shard_map/ppermute | solution.py:666
  11.4 43.3 %collective-permute-start.7 = (bf16[256,1024]{1,0:T(8,128)(2,1)}, bf16[256,1024]{1,0:T(8,128)(2,1)}, u32[]{:S(2)}, u32[]{:S(2)}) collective-permute-start(bf16[256,1024]{1,0:T(8,128)(2,1)} %get-tuple-element.218), channel_id=1, source_target_pairs={{0,1},{1,0},{2,4},{3,5},{4,2},{5,3},{6,7},{7,6},{8,9},{9,8},{10,12... | collective-permute-start | bytes 1572872 | tf_op jit(solution)/shard_map/ppermute | solution.py:688
  13.9 42.4 %collective-permute-start.8 = (bf16[256,1024]{1,0:T(8,128)(2,1)}, bf16[256,1024]{1,0:T(8,128)(2,1)}, u32[]{:S(2)}, u32[]{:S(2)}) collective-permute-start(bf16[256,1024]{1,0:T(8,128)(2,1)} %get-tuple-element.219), channel_id=1, source_target_pairs={{2,5},{3,4},{4,3},{5,2},{10,13},{11,12},{12,11},{13,10},{18,21},{1... | collective-permute-start | bytes 1572872 | tf_op jit(solution)/shard_map/ppermute | solution.py:689
  17.9 39.9 %collective-permute-start = (bf16[264,1024]{1,0:T(8,128)(2,1)}, bf16[264,1024]{1,0:T(8,128)(2,1)}, u32[]{:S(2)}, u32[]{:S(2)}) collective-permute-start(bf16[264,1024]{1,0:T(8,128)(2,1)} %get-tuple-element.220), channel_id=1, source_target_pairs={{0,1},{1,0},{2,4},{3,5},{4,2},{5,3},{6,7},{7,6},{8,9},{9,8},{10,12... | collective-permute-start | bytes 1622024 | tf_op jit(solution)/shard_map/ppermute | solution.py:688
  17.9 39.9 %collective-permute-start.1 = (bf16[264,1024]{1,0:T(8,128)(2,1)}, bf16[264,1024]{1,0:T(8,128)(2,1)}, u32[]{:S(2)}, u32[]{:S(2)}) collective-permute-start(bf16[264,1024]{1,0:T(8,128)(2,1)} %get-tuple-element.221), channel_id=1, source_target_pairs={{2,5},{3,4},{4,3},{5,2},{10,13},{11,12},{12,11},{13,10},{18,21},{1... | collective-permute-start | bytes 1622024 | tf_op jit(solution)/shard_map/ppermute | solution.py:689
  25.2 26.9 %collective-permute-start.10 = (bf16[1136,128]{1,0:T(8,128)(2,1)S(1)}, bf16[1136,128]{1,0:T(8,128)(2,1)S(1)}, u32[]{:S(2)}, u32[]{:S(2)}) collective-permute-start(bf16[1136,128]{1,0:T(8,128)(2,1)S(1)} %get-tuple-element.230), channel_id=1, source_target_pairs={{0,4},{4,0},{1,5},{5,1},{2,6},{6,2},{3,7},{7,3},{8,12},{12,8},{9,1... | collective-permute-start | bytes 872456 | tf_op jit(solution)/shard_map/ppermute | solution.py:666
  52.0 26.6 %collective-permute-start.6 = (bf16[8,400,128]{2,1,0:T(8,128)(2,1)}, bf16[8,400,128]{2,1,0:T(8,128)(2,1)}, u32[]{:S(2)}, u32[]{:S(2)}) collective-permute-start(bf16[8,400,128]{2,1,0:T(8,128)(2,1)} %all_gather.9.w_ref.refs_4_), channel_id=1, source_target_pairs={{0,2},{2,0},{1,3},{3,1},{4,6},{6,4},{5,7},{7,5},{8,10},{10,8},{9,1... | collective-permute-start | bytes 2457608 | tf_op jit(solution)/shard_map/ppermute | solution.py:666
  54.7 103.4 %all-gather.5.cloned.1.call-start = ((), (), s32[]{:S(2)}) async-start(), calls=%async_computation.3 | async-start | bytes 1351680 | tf_op jit(solution)/shard_map/all_gather | solution.py:815
  54.7 23.9 %collective-permute-start.5 = (bf16[8,400,128]{2,1,0:T(8,128)(2,1)}, bf16[8,400,128]{2,1,0:T(8,128)(2,1)}, u32[]{:S(2)}, u32[]{:S(2)}) collective-permute-start(bf16[8,400,128]{2,1,0:T(8,128)(2,1)} %all_gather.9.w_ref.refs_4_), channel_id=1, source_target_pairs={{0,1},{1,0},{2,3},{3,2},{4,5},{5,4},{6,7},{7,6},{8,9},{9,8},{10,11... | collective-permute-start | bytes 2457608 | tf_op jit(solution)/shard_map/ppermute | solution.py:666
  60.5 5.9 %collective-permute-start.3 = (bf16[512,1024]{1,0:T(8,128)(2,1)S(1)}, bf16[512,1024]{1,0:T(8,128)(2,1)}, u32[]{:S(2)}, u32[]{:S(2)}) collective-permute-start(bf16[512,1024]{1,0:T(8,128)(2,1)S(1)} %fusion.6), channel_id=1, source_target_pairs={{0,4},{4,0},{1,5},{5,1},{2,6},{6,2},{3,7},{7,3},{8,12},{12,8},{9,1... | collective-permute-start | bytes 3145736 | tf_op jit(solution)/shard_map/ppermute | solution.py:666
  60.6 2.3 collective-permute-start.4
  62.2 20.9 %collective-permute-start.9 = (bf16[512,1024]{1,0:T(8,128)(2,1)}, bf16[512,1024]{1,0:T(8,128)(2,1)}, u32[]{:S(2)}, u32[]{:S(2)}) collective-permute-start(bf16[512,1024]{1,0:T(8,128)(2,1)} %pad_maximum_fusion.7), channel_id=1, source_target_pairs={{0,4},{4,0},{1,5},{5,1},{2,6},{6,2},{3,7},{7,3},{8,12},{12,8},{9,1... | collective-permute-start | bytes 3145736 | tf_op jit(solution)/shard_map/ppermute | solution.py:666
  65.9 19.9 %copy-start.14 = (f32[1024,128]{1,0:T(8,128)}, f32[1024,128]{1,0:T(8,128)S(1)}, u32[]{:S(2)}) copy-start(f32[1024,128]{1,0:T(8,128)S(1)} %pad_maximum_fusion.10.cos_ref) | copy-start | bytes 1572868
  66.4 19.4 %copy-start.8 = (f32[1024,128]{1,0:T(8,128)}, f32[1024,128]{1,0:T(8,128)S(1)}, u32[]{:S(2)}) copy-start(f32[1024,128]{1,0:T(8,128)S(1)} %pad_maximum_fusion.11.sin_ref) | copy-start | bytes 1572868
  80.0 15.1 %collective-permute-start.11 = (bf16[4,400,128]{2,1,0:T(8,128)(2,1)S(1)}, bf16[4,400,128]{2,1,0:T(8,128)(2,1)S(1)}, u32[]{:S(2)}, u32[]{:S(2)}) collective-permute-start(bf16[4,400,128]{2,1,0:T(8,128)(2,1)S(1)} %slice.139), channel_id=1, source_target_pairs={{0,1},{1,0},{2,3},{3,2},{4,5},{5,4},{6,7},{7,6},{8,9},{9,8},{10,11... | collective-permute-start | bytes 1228808 | tf_op jit(solution)/shard_map/ppermute | solution.py:666
  81.6 14.1 %collective-permute-start.12 = (bf16[4,400,128]{2,1,0:T(8,128)(2,1)S(1)}, bf16[4,400,128]{2,1,0:T(8,128)(2,1)S(1)}, u32[]{:S(2)}, u32[]{:S(2)}) collective-permute-start(bf16[4,400,128]{2,1,0:T(8,128)(2,1)S(1)} %slice.140), channel_id=1, source_target_pairs={{0,2},{2,0},{1,3},{3,1},{4,6},{6,4},{5,7},{7,5},{8,10},{10,8},{9,1... | collective-permute-start | bytes 1228808 | tf_op jit(solution)/shard_map/ppermute | solution.py:666
  98.0 26.5 %copy-start.22 = (bf16[8,128,128]{2,1,0:T(8,128)(2,1)}, bf16[8,128,128]{2,1,0:T(8,128)(2,1)S(1)}, u32[]{:S(2)}) copy-start(bf16[8,128,128]{2,1,0:T(8,128)(2,1)S(1)} %slice.141.refs_4_.w_ref) | copy-start | bytes 786436
  100.3 24.1 %collective-permute-start.15 = (bf16[8,128,128]{2,1,0:T(8,128)(2,1)S(1)}, bf16[8,128,128]{2,1,0:T(8,128)(2,1)S(1)}, u32[]{:S(2)}, u32[]{:S(2)}) collective-permute-start(bf16[8,128,128]{2,1,0:T(8,128)(2,1)S(1)} %slice.141.refs_4_.w_ref), channel_id=1, source_target_pairs={{0,3},{1,2},{2,1},{3,0},{4,7},{5,6},{6,5},{7,4},{8,11},{9,10},{10,... | collective-permute-start | bytes 786440 | tf_op jit(solution)/shard_map/ppermute | solution.py:724
  101.8 22.6 %collective-permute-start.14 = (bf16[8,128,128]{2,1,0:T(8,128)(2,1)S(1)}, bf16[8,128,128]{2,1,0:T(8,128)(2,1)S(1)}, u32[]{:S(2)}, u32[]{:S(2)}) collective-permute-start(bf16[8,128,128]{2,1,0:T(8,128)(2,1)S(1)} %slice.141.refs_4_.w_ref), channel_id=1, source_target_pairs={{0,2},{2,0},{1,3},{3,1},{4,6},{6,4},{5,7},{7,5},{8,10},{10,8},{9,1... | collective-permute-start | bytes 786440 | tf_op jit(solution)/shard_map/ppermute | solution.py:666
  103.2 21.2 %collective-permute-start.13 = (bf16[8,128,128]{2,1,0:T(8,128)(2,1)S(1)}, bf16[8,128,128]{2,1,0:T(8,128)(2,1)S(1)}, u32[]{:S(2)}, u32[]{:S(2)}) collective-permute-start(bf16[8,128,128]{2,1,0:T(8,128)(2,1)S(1)} %slice.141.refs_4_.w_ref), channel_id=1, source_target_pairs={{0,1},{1,0},{2,3},{3,2},{4,5},{5,4},{6,7},{7,6},{8,9},{9,8},{10,11... | collective-permute-start | bytes 786440 | tf_op jit(solution)/shard_map/ppermute | solution.py:666
  128.9 3.0 collective-permute-start.16
  130.7 237.1 %reduce-scatter.3.cloned.1.call-start = ((), (), s32[]{:S(2)}) async-start(), calls=%async_computation.4 | async-start | bytes 2580480 | tf_op jit(solution)/shard_map/reduce_scatter | solution.py:933
  136.2 30.0 %collective-permute-start.17 = (bf16[512,1024]{1,0:T(8,128)(2,1)}, bf16[512,1024]{1,0:T(8,128)(2,1)}, u32[]{:S(2)}, u32[]{:S(2)}) collective-permute-start(bf16[512,1024]{1,0:T(8,128)(2,1)} %multiply_convert_fusion), channel_id=1, source_target_pairs={{0,4},{4,0},{1,5},{5,1},{2,6},{6,2},{3,7},{7,3},{8,12},{12,8},{9,1... | collective-permute-start | bytes 3145736 | tf_op jit(solution)/shard_map/ppermute | solution.py:666
  136.4 24.6 %collective-permute-start.21 = (bf16[8,480,128]{2,1,0:T(8,128)(2,1)}, bf16[8,480,128]{2,1,0:T(8,128)(2,1)}, u32[]{:S(2)}, u32[]{:S(2)}) collective-permute-start(bf16[8,480,128]{2,1,0:T(8,128)(2,1)} %slice.138.wa_ref), channel_id=1, source_target_pairs={{0,2},{2,0},{1,3},{3,1},{4,6},{6,4},{5,7},{7,5},{8,10},{10,8},{9,1... | collective-permute-start | bytes 2949128 | tf_op jit(solution)/shard_map/ppermute | solution.py:666
  137.0 24.1 %collective-permute-start.20 = (bf16[8,480,128]{2,1,0:T(8,128)(2,1)}, bf16[8,480,128]{2,1,0:T(8,128)(2,1)}, u32[]{:S(2)}, u32[]{:S(2)}) collective-permute-start(bf16[8,480,128]{2,1,0:T(8,128)(2,1)} %slice.138.wa_ref), channel_id=1, source_target_pairs={{0,1},{1,0},{2,3},{3,2},{4,5},{5,4},{6,7},{7,6},{8,9},{9,8},{10,11... | collective-permute-start | bytes 2949128 | tf_op jit(solution)/shard_map/ppermute | solution.py:666
  158.1 27.0 %collective-permute-start.19 = (bf16[8,528,128]{2,1,0:T(8,128)(2,1)}, bf16[8,528,128]{2,1,0:T(8,128)(2,1)S(1)}, u32[]{:S(2)}, u32[]{:S(2)}) collective-permute-start(bf16[8,528,128]{2,1,0:T(8,128)(2,1)} %all-gather.5.cloned.1.call-done.wb_ref), channel_id=1, source_target_pairs={{0,2},{2,0},{1,3},{3,1},{4,6},{6,4},{5,7},{7,5},{8,10},{10,8},{9,1... | collective-permute-start | bytes 3244040 | tf_op jit(solution)/shard_map/ppermute | solution.py:666
  159.5 27.0 %collective-permute-start.18 = (bf16[8,528,128]{2,1,0:T(8,128)(2,1)}, bf16[8,528,128]{2,1,0:T(8,128)(2,1)S(1)}, u32[]{:S(2)}, u32[]{:S(2)}) collective-permute-start(bf16[8,528,128]{2,1,0:T(8,128)(2,1)} %all-gather.5.cloned.1.call-done.wb_ref), channel_id=1, source_target_pairs={{0,1},{1,0},{2,3},{3,2},{4,5},{5,4},{6,7},{7,6},{8,9},{9,8},{10,11... | collective-permute-start | bytes 3244040 | tf_op jit(solution)/shard_map/ppermute | solution.py:666
  163.2 53.9 %collective-permute-start.23 = (bf16[4,480,128]{2,1,0:T(8,128)(2,1)S(1)}, bf16[4,480,128]{2,1,0:T(8,128)(2,1)S(1)}, u32[]{:S(2)}, u32[]{:S(2)}) collective-permute-start(bf16[4,480,128]{2,1,0:T(8,128)(2,1)S(1)} %slice.144), channel_id=1, source_target_pairs={{0,1},{1,0},{2,3},{3,2},{4,5},{5,4},{6,7},{7,6},{8,9},{9,8},{10,11... | collective-permute-start | bytes 1474568 | tf_op jit(solution)/shard_map/ppermute | solution.py:666
  164.8 53.8 %collective-permute-start.24 = (bf16[4,480,128]{2,1,0:T(8,128)(2,1)S(1)}, bf16[4,480,128]{2,1,0:T(8,128)(2,1)}, u32[]{:S(2)}, u32[]{:S(2)}) collective-permute-start(bf16[4,480,128]{2,1,0:T(8,128)(2,1)S(1)} %slice.145), channel_id=1, source_target_pairs={{0,2},{2,0},{1,3},{3,1},{4,6},{6,4},{5,7},{7,5},{8,10},{10,8},{9,1... | collective-permute-start | bytes 1474568 | tf_op jit(solution)/shard_map/ppermute | solution.py:666
  186.6 32.0 %collective-permute-start.25 = (bf16[4,528,128]{2,1,0:T(8,128)(2,1)S(1)}, bf16[4,528,128]{2,1,0:T(8,128)(2,1)S(1)}, u32[]{:S(2)}, u32[]{:S(2)}) collective-permute-start(bf16[4,528,128]{2,1,0:T(8,128)(2,1)S(1)} %slice.146), channel_id=1, source_target_pairs={{0,1},{1,0},{2,3},{3,2},{4,5},{5,4},{6,7},{7,6},{8,9},{9,8},{10,11... | collective-permute-start | bytes 1622024 | tf_op jit(solution)/shard_map/ppermute | solution.py:666
  202.1 27.2 %collective-permute-start.22 = (bf16[4,1008,128]{2,1,0:T(8,128)(2,1)S(1)}, bf16[4,1008,128]{2,1,0:T(8,128)(2,1)}, u32[]{:S(2)}, u32[]{:S(2)}) collective-permute-start(bf16[4,1008,128]{2,1,0:T(8,128)(2,1)S(1)} %get-tuple-element.132), channel_id=1, source_target_pairs={{0,1},{1,0},{2,3},{3,2},{4,5},{5,4},{6,7},{7,6},{8,9},{9,8},{10,11... | collective-permute-start | bytes 3096584 | tf_op jit(solution)/shard_map/ppermute | solution.py:666
  202.6 16.0 %collective-permute-start.26 = (bf16[4,528,128]{2,1,0:T(8,128)(2,1)S(1)}, bf16[4,528,128]{2,1,0:T(8,128)(2,1)S(1)}, u32[]{:S(2)}, u32[]{:S(2)}) collective-permute-start(bf16[4,528,128]{2,1,0:T(8,128)(2,1)S(1)} %slice.147), channel_id=1, source_target_pairs={{0,2},{2,0},{1,3},{3,1},{4,6},{6,4},{5,7},{7,5},{8,10},{10,8},{9,1... | collective-permute-start | bytes 1622024 | tf_op jit(solution)/shard_map/ppermute | solution.py:666
  217.1 27.8 %collective-permute-start.28 = (bf16[4,1008,128]{2,1,0:T(8,128)(2,1)S(1)}, bf16[4,1008,128]{2,1,0:T(8,128)(2,1)S(1)}, u32[]{:S(2)}, u32[]{:S(2)}) collective-permute-start(bf16[4,1008,128]{2,1,0:T(8,128)(2,1)S(1)} %get-tuple-element.148), channel_id=1, source_target_pairs={{0,2},{2,0},{1,3},{3,1},{4,6},{6,4},{5,7},{7,5},{8,10},{10,8},{9,1... | collective-permute-start | bytes 3096584 | tf_op jit(solution)/shard_map/ppermute | solution.py:666
  245.0 2.7 collective-permute-start.29
  246.1 3.9 collective-permute-start.27
  252.9 2.7 collective-permute-start.30
  253.1 25.1 %collective-permute-start.33 = (bf16[4,1008,128]{2,1,0:T(8,128)(2,1)S(1)}, bf16[4,1008,128]{2,1,0:T(8,128)(2,1)S(1)}, u32[]{:S(2)}, u32[]{:S(2)}) collective-permute-start(bf16[4,1008,128]{2,1,0:T(8,128)(2,1)S(1)} %get-tuple-element.161), channel_id=1, source_target_pairs={{0,2},{2,0},{1,3},{3,1},{4,6},{6,4},{5,7},{7,5},{8,10},{10,8},{9,1... | collective-permute-start | bytes 3096584 | tf_op jit(solution)/shard_map/ppermute | solution.py:666
  253.8 24.9 %collective-permute-start.31 = (bf16[4,1008,128]{2,1,0:T(8,128)(2,1)S(1)}, bf16[4,1008,128]{2,1,0:T(8,128)(2,1)S(1)}, u32[]{:S(2)}, u32[]{:S(2)}) collective-permute-start(bf16[4,1008,128]{2,1,0:T(8,128)(2,1)S(1)} %get-tuple-element.158), channel_id=1, source_target_pairs={{0,1},{1,0},{2,3},{3,2},{4,5},{5,4},{6,7},{7,6},{8,9},{9,8},{10,11... | collective-permute-start | bytes 3096584 | tf_op jit(solution)/shard_map/ppermute | solution.py:666
  255.8 42.7 %copy-start.5 = (bf16[1024,1024]{1,0:T(8,128)(2,1)}, bf16[1024,1024]{1,0:T(8,128)(2,1)S(1)}, u32[]{:S(2)}) copy-start(bf16[1024,1024]{1,0:T(8,128)(2,1)S(1)} %pad_maximum_fusion.3.da_ref) | copy-start | bytes 6291460
  278.9 32.0 %collective-permute-start.32 = (bf16[4,1008,128]{2,1,0:T(8,128)(2,1)S(1)}, bf16[4,1008,128]{2,1,0:T(8,128)(2,1)S(1)}, u32[]{:S(2)}, u32[]{:S(2)}) collective-permute-start(bf16[4,1008,128]{2,1,0:T(8,128)(2,1)S(1)} %add_convert_fusion.5), channel_id=1, source_target_pairs={{0,2},{2,0},{1,3},{3,1},{4,6},{6,4},{5,7},{7,5},{8,10},{10,8},{9,1... | collective-permute-start | bytes 3096584 | tf_op jit(solution)/shard_map/ppermute | solution.py:666
  280.7 31.0 %collective-permute-start.34 = (bf16[4,1008,128]{2,1,0:T(8,128)(2,1)S(1)}, bf16[4,1008,128]{2,1,0:T(8,128)(2,1)S(1)}, u32[]{:S(2)}, u32[]{:S(2)}) collective-permute-start(bf16[4,1008,128]{2,1,0:T(8,128)(2,1)S(1)} %add_convert_fusion.4), channel_id=1, source_target_pairs={{0,1},{1,0},{2,3},{3,2},{4,5},{5,4},{6,7},{7,6},{8,9},{9,8},{10,11... | collective-permute-start | bytes 3096584 | tf_op jit(solution)/shard_map/ppermute | solution.py:666
  297.9 19.6 %collective-permute-start.36 = (bf16[4,512,128]{2,1,0:T(8,128)(2,1)}, bf16[4,512,128]{2,1,0:T(8,128)(2,1)}, u32[]{:S(2)}, u32[]{:S(2)}) collective-permute-start(bf16[4,512,128]{2,1,0:T(8,128)(2,1)} %get-tuple-element.183), channel_id=1, source_target_pairs={{0,1},{1,0},{2,3},{3,2},{4,5},{5,4},{6,7},{7,6},{8,9},{9,8},{10,11... | collective-permute-start | bytes 1572872 | tf_op jit(solution)/shard_map/ppermute | solution.py:666
  313.8 79.3 %reduce-scatter.5.cloned.1.call-start = ((), (), s32[]{:S(2)}) async-start(), calls=%async_computation.5 | async-start | bytes 1310720 | tf_op jit(solution)/shard_map/reduce_scatter | solution.py:943
  313.9 17.9 %copy-start.6 = (bf16[1024,1024]{1,0:T(8,128)(2,1)S(1)}, bf16[1024,1024]{1,0:T(8,128)(2,1)}, u32[]{:S(2)}) copy-start(bf16[1024,1024]{1,0:T(8,128)(2,1)} %copy-done.5) | copy-start | bytes 6291460
  313.9 15.1 %collective-permute-start.37 = (bf16[4,512,128]{2,1,0:T(8,128)(2,1)}, bf16[4,512,128]{2,1,0:T(8,128)(2,1)S(1)}, u32[]{:S(2)}, u32[]{:S(2)}) collective-permute-start(bf16[4,512,128]{2,1,0:T(8,128)(2,1)} %copy-done.28), channel_id=1, source_target_pairs={{0,2},{2,0},{1,3},{3,1},{4,6},{6,4},{5,7},{7,5},{8,10},{10,8},{9,1... | collective-permute-start | bytes 1572872 | tf_op jit(solution)/shard_map/ppermute | solution.py:666
  314.6 35.0 %collective-permute-start.40 = (bf16[4,512,128]{2,1,0:T(8,128)(2,1)}, bf16[4,512,128]{2,1,0:T(8,128)(2,1)S(1)}, u32[]{:S(2)}, u32[]{:S(2)}) collective-permute-start(bf16[4,512,128]{2,1,0:T(8,128)(2,1)} %copy-done.29), channel_id=1, source_target_pairs={{0,2},{2,0},{1,3},{3,1},{4,6},{6,4},{5,7},{7,5},{8,10},{10,8},{9,1... | collective-permute-start | bytes 1572872 | tf_op jit(solution)/shard_map/ppermute | solution.py:666
  316.0 15.8 %collective-permute-start.35 = (bf16[4,512,128]{2,1,0:T(8,128)(2,1)}, bf16[4,512,128]{2,1,0:T(8,128)(2,1)S(1)}, u32[]{:S(2)}, u32[]{:S(2)}) collective-permute-start(bf16[4,512,128]{2,1,0:T(8,128)(2,1)} %copy-done.30), channel_id=1, source_target_pairs={{0,1},{1,0},{2,3},{3,2},{4,5},{5,4},{6,7},{7,6},{8,9},{9,8},{10,11... | collective-permute-start | bytes 1572872 | tf_op jit(solution)/shard_map/ppermute | solution.py:666
  318.8 30.7 %collective-permute-start.38 = (bf16[4,512,128]{2,1,0:T(8,128)(2,1)S(1)}, bf16[4,512,128]{2,1,0:T(8,128)(2,1)S(1)}, u32[]{:S(2)}, u32[]{:S(2)}) collective-permute-start(bf16[4,512,128]{2,1,0:T(8,128)(2,1)S(1)} %add_convert_fusion.12), channel_id=1, source_target_pairs={{0,2},{2,0},{1,3},{3,1},{4,6},{6,4},{5,7},{7,5},{8,10},{10,8},{9,1... | collective-permute-start | bytes 1572872 | tf_op jit(solution)/shard_map/ppermute | solution.py:666
  330.2 19.3 %collective-permute-start.39 = (bf16[4,512,128]{2,1,0:T(8,128)(2,1)S(1)}, bf16[4,512,128]{2,1,0:T(8,128)(2,1)S(1)}, u32[]{:S(2)}, u32[]{:S(2)}) collective-permute-start(bf16[4,512,128]{2,1,0:T(8,128)(2,1)S(1)} %add_convert_fusion.11), channel_id=1, source_target_pairs={{0,1},{1,0},{2,3},{3,2},{4,5},{5,4},{6,7},{7,6},{8,9},{9,8},{10,11... | collective-permute-start | bytes 1572872 | tf_op jit(solution)/shard_map/ppermute | solution.py:666
  364.1 2.7 collective-permute-start.43
  365.0 9.5 %collective-permute-start.41 = (bf16[256,1024]{1,0:T(8,128)(2,1)}, bf16[256,1024]{1,0:T(8,128)(2,1)}, u32[]{:S(2)}, u32[]{:S(2)}) collective-permute-start(bf16[256,1024]{1,0:T(8,128)(2,1)} %broadcast_select_fusion.4), channel_id=1, source_target_pairs={{0,1},{1,0},{2,4},{3,5},{4,2},{5,3},{6,7},{7,6},{8,9},{9,8},{10,12... | collective-permute-start | bytes 1572872 | tf_op jit(solution)/shard_map/ppermute | solution.py:697
  370.9 9.2 %collective-permute-start.44 = (bf16[256,1024]{1,0:T(8,128)(2,1)S(1)}, bf16[256,1024]{1,0:T(8,128)(2,1)S(1)}, u32[]{:S(2)}, u32[]{:S(2)}) collective-permute-start(bf16[256,1024]{1,0:T(8,128)(2,1)S(1)} %broadcast_select_fusion.3), channel_id=1, source_target_pairs={{0,1},{1,0},{2,4},{3,5},{4,2},{5,3},{6,7},{7,6},{8,9},{9,8},{10,12... | collective-permute-start | bytes 1572872 | tf_op jit(solution)/shard_map/ppermute | solution.py:697
  375.4 10.8 %collective-permute-start.42 = (bf16[256,1024]{1,0:T(8,128)(2,1)S(1)}, bf16[256,1024]{1,0:T(8,128)(2,1)S(1)}, u32[]{:S(2)}, u32[]{:S(2)}) collective-permute-start(bf16[256,1024]{1,0:T(8,128)(2,1)S(1)} %get-tuple-element.226), channel_id=1, source_target_pairs={{2,5},{3,4},{4,3},{5,2},{10,13},{11,12},{12,11},{13,10},{18,21},{1... | collective-permute-start | bytes 1572872 | tf_op jit(solution)/shard_map/ppermute | solution.py:698
  376.2 6.7 %collective-permute-start.50 = (bf16[1008,128]{1,0:T(8,128)(2,1)S(1)}, bf16[1008,128]{1,0:T(8,128)(2,1)S(1)}, u32[]{:S(2)}, u32[]{:S(2)}) collective-permute-start(bf16[1008,128]{1,0:T(8,128)(2,1)S(1)} %get-tuple-element.240), channel_id=1, source_target_pairs={{0,4},{4,0},{1,5},{5,1},{2,6},{6,2},{3,7},{7,3},{8,12},{12,8},{9,1... | collective-permute-start | bytes 774152 | tf_op jit(solution)/shard_map/ppermute | solution.py:666
  381.3 18.9 %collective-permute-start.45 = (bf16[256,1024]{1,0:T(8,128)(2,1)}, bf16[256,1024]{1,0:T(8,128)(2,1)}, u32[]{:S(2)}, u32[]{:S(2)}) collective-permute-start(bf16[256,1024]{1,0:T(8,128)(2,1)} %get-tuple-element.224), channel_id=1, source_target_pairs={{2,5},{3,4},{4,3},{5,2},{10,13},{11,12},{12,11},{13,10},{18,21},{1... | collective-permute-start | bytes 1572872 | tf_op jit(solution)/shard_map/ppermute | solution.py:698
  383.0 25.9 %collective-permute-start.53 = (bf16[2,1008,128]{2,1,0:T(8,128)(2,1)S(1)}, bf16[2,1008,128]{2,1,0:T(8,128)(2,1)S(1)}, u32[]{:S(2)}, u32[]{:S(2)}) collective-permute-start(bf16[2,1008,128]{2,1,0:T(8,128)(2,1)S(1)} %pad_maximum_fusion.12.refs_0_), channel_id=1, source_target_pairs={{0,3},{1,2},{2,1},{3,0},{4,7},{5,6},{6,5},{7,4},{8,11},{9,10},{10,... | collective-permute-start | bytes 1548296 | tf_op jit(solution)/shard_map/ppermute | solution.py:724
  394.1 5.4 %collective-permute-start.46 = (bf16[512,128]{1,0:T(8,128)(2,1)S(1)}, bf16[512,128]{1,0:T(8,128)(2,1)S(1)}, u32[]{:S(2)}, u32[]{:S(2)}) collective-permute-start(bf16[512,128]{1,0:T(8,128)(2,1)S(1)} %get-tuple-element.242), channel_id=1, source_target_pairs={{0,4},{4,0},{1,5},{5,1},{2,6},{6,2},{3,7},{7,3},{8,12},{12,8},{9,1... | collective-permute-start | bytes 393224 | tf_op jit(solution)/shard_map/ppermute | solution.py:666
  396.6 22.2 %collective-permute-start.52 = (bf16[2,1008,128]{2,1,0:T(8,128)(2,1)S(1)}, bf16[2,1008,128]{2,1,0:T(8,128)(2,1)S(1)}, u32[]{:S(2)}, u32[]{:S(2)}) collective-permute-start(bf16[2,1008,128]{2,1,0:T(8,128)(2,1)S(1)} %pad_maximum_fusion.12.refs_0_), channel_id=1, source_target_pairs={{0,2},{2,0},{1,3},{3,1},{4,6},{6,4},{5,7},{7,5},{8,10},{10,8},{9,1... | collective-permute-start | bytes 1548296 | tf_op jit(solution)/shard_map/ppermute | solution.py:666
  398.1 20.7 %collective-permute-start.51 = (bf16[2,1008,128]{2,1,0:T(8,128)(2,1)S(1)}, bf16[2,1008,128]{2,1,0:T(8,128)(2,1)S(1)}, u32[]{:S(2)}, u32[]{:S(2)}) collective-permute-start(bf16[2,1008,128]{2,1,0:T(8,128)(2,1)S(1)} %pad_maximum_fusion.12.refs_0_), channel_id=1, source_target_pairs={{0,1},{1,0},{2,3},{3,2},{4,5},{5,4},{6,7},{7,6},{8,9},{9,8},{10,11... | collective-permute-start | bytes 1548296 | tf_op jit(solution)/shard_map/ppermute | solution.py:666
  399.6 24.9 %collective-permute-start.49 = (bf16[2,512,128]{2,1,0:T(8,128)(2,1)S(1)}, bf16[2,512,128]{2,1,0:T(8,128)(2,1)S(1)}, u32[]{:S(2)}, u32[]{:S(2)}) collective-permute-start(bf16[2,512,128]{2,1,0:T(8,128)(2,1)S(1)} %pad_maximum_fusion.13.refs_0_), channel_id=1, source_target_pairs={{0,3},{1,2},{2,1},{3,0},{4,7},{5,6},{6,5},{7,4},{8,11},{9,10},{10,... | collective-permute-start | bytes 786440 | tf_op jit(solution)/shard_map/ppermute | solution.py:724
  400.2 27.0 %collective-permute-start.48 = (bf16[2,512,128]{2,1,0:T(8,128)(2,1)S(1)}, bf16[2,512,128]{2,1,0:T(8,128)(2,1)S(1)}, u32[]{:S(2)}, u32[]{:S(2)}) collective-permute-start(bf16[2,512,128]{2,1,0:T(8,128)(2,1)S(1)} %pad_maximum_fusion.13.refs_0_), channel_id=1, source_target_pairs={{0,2},{2,0},{1,3},{3,1},{4,6},{6,4},{5,7},{7,5},{8,10},{10,8},{9,1... | collective-permute-start | bytes 786440 | tf_op jit(solution)/shard_map/ppermute | solution.py:666
  408.8 18.3 %collective-permute-start.47 = (bf16[2,512,128]{2,1,0:T(8,128)(2,1)S(1)}, bf16[2,512,128]{2,1,0:T(8,128)(2,1)S(1)}, u32[]{:S(2)}, u32[]{:S(2)}) collective-permute-start(bf16[2,512,128]{2,1,0:T(8,128)(2,1)S(1)} %pad_maximum_fusion.13.refs_0_), channel_id=1, source_target_pairs={{0,1},{1,0},{2,3},{3,2},{4,5},{5,4},{6,7},{7,6},{8,9},{9,8},{10,11... | collective-permute-start | bytes 786440 | tf_op jit(solution)/shard_map/ppermute | solution.py:666
  408.9 20.7 %copy-start.1 = (bf16[2624,128]{1,0:T(8,128)(2,1)S(1)}, bf16[2624,128]{1,0:T(8,128)(2,1)}, u32[]{:S(2)}) copy-start(bf16[2624,128]{1,0:T(8,128)(2,1)} %param.14) | copy-start | bytes 2015236
  (114 other events, 573.2 us)
Sparse Core Ops, SparseCore 0:
  54.8 30.6 all-gather.2
  130.8 27.2 all-gather.4
  313.9 42.0 reduce-scatter.2
  367.9 25.1 reduce-scatter.4
